TPU v7x, 32 devices: a whole 2x2x4 slice. The times are simulated.
32 devices in a mesh: mod: 2 (over core), dp: 16 (over z, y, x).
Axes of the slice: x: 2, y: 2, z: 4, core: 2. Of those that a mesh axis runs over, the one named last changes fastest.
Arguments:
- rows: bfloat16 [2, 32, 196, 768], P('mod', 'dp'), may hold values from -6 to 6
- cotangent: bfloat16 [2, 32, 196, 768], P('mod', 'dp'), may hold values from -6 to 6
- master: float32 [7095552], P(('mod', 'dp')), as said below
- first_moment: float32 [7095552], P(('mod', 'dp')), may hold values from -0.0014648438 to 0.0014648438
- second_moment: float32 [7095552], P(('mod', 'dp')), may hold values from 5.919201e-09 to 2.3535872e-08
- average: float32 [7095552], P(('mod', 'dp')), as said below
- lengths: int32 [32], P('dp'), may hold values from 1 to 196, 3136 in all
- buckets: int32 [392, 392], replicated, may hold values from 0 to 62
Outputs:
- result_rows: bfloat16 [2, 32, 196, 768], P('mod', 'dp')
- grad_rows: float32 [2, 32, 196, 768], P('mod', 'dp')
- grad_norm: float32 [], replicated
- new_master: float32 [7095552], P(('mod', 'dp'))
- new_first: float32 [7095552], P(('mod', 'dp'))
- new_second: float32 [7095552], P(('mod', 'dp'))
- new_average: float32 [7095552], P(('mod', 'dp'))
- new_copy: bfloat16 [7095552], P(('mod', 'dp'))
Inputs may be any that keep to these rules, and one draw needn't show every extreme that they name: `master`: a flat vector of parameters in the order of the steps, gains about 1, biases and matrices about zero. `average`: laid out as master.
All inputs are finite; a program needn't handle non-finite values. No bound on the sum of `lengths` on one device may be relied on, other than what follows from the above.
Results may differ from a plain program's by a relative error of at most 0.011.
Values may be sent and summed in bfloat16 or wider, within the bound.
No kernel may reach another device: no remote copies, remote signals or barrier semaphores. Data moves between devices by JAX's collectives and lax.ppermute only.
A program may use at most 192 MiB of HBM per device.

v0:
```python
import jax
import jax.numpy as jnp
from jax import lax
from jax.sharding import PartitionSpec as P

D = 768
H = 12
HD = 64
FF = 3072
NB = 63
P_SIZE = 196
STEP = 5


def from_partner(block, axis, bit):
    count = lax.axis_size(axis)
    route = []
    for low in range(count):
        high = low | 1 << bit
        if high != low and high < count:
            route += [(low, high), (high, low)]
    return lax.ppermute(block, axis, route)


def layer_norm(values, gain, shift):
    center = values - jnp.mean(values, axis=-1, keepdims=True)
    spread = jnp.mean(center * center, axis=-1, keepdims=True)
    return center * lax.rsqrt(spread + 1e-05) * gain + shift


def norm_back(values, gain, shift, grad_after):
    _, pullback = jax.vjp(layer_norm, values, gain, shift)
    return pullback(grad_after)


def matmul(left, right):
    return jnp.dot(left, right, preferred_element_type=jnp.float32)


def matmul_tn(left, right):
    return lax.dot_general(
        left, right, (((0,), (0,)), ((), ())), preferred_element_type=jnp.float32
    )


def matmul_nt(left, right):
    return lax.dot_general(
        left, right, (((1,), (1,)), ((), ())), preferred_element_type=jnp.float32
    )


def exact_gelu(values):
    return jax.nn.gelu(values, approximate=False)


def unpack(flat):
    pairs = [(D, D), (D, D), (D, D), (D, D), (D, FF), (FF, D), (10, D), (3, FF), (NB + 1, H)]
    pieces = []
    offset = 0
    for dims_pair in pairs:
        extent = dims_pair[0] * dims_pair[1]
        pieces.append(flat[offset : offset + extent].reshape(dims_pair))
        offset += extent
    return pieces


def on_device(rows, cotangent, master, first_moment, second_moment, average, lengths, buckets):
    side = lax.axis_index("mod")
    own_copy = master.astype(jnp.bfloat16)
    flat = lax.all_gather(own_copy, ("mod", "dp"), axis=0, tiled=True)
    w_query, w_key, w_value, w_out, w_inner, w_outer, vec_model, vec_inner, head_table = unpack(
        flat
    )
    model_vec = vec_model.astype(jnp.float32)
    inner_vec = vec_inner.astype(jnp.float32)
    head_vals = head_table.astype(jnp.float32)
    head_scale = head_vals[NB]
    num_seq = rows.shape[1]
    num_rows = num_seq * P_SIZE
    slots = jnp.arange(P_SIZE, dtype=jnp.int32)
    text_valid = (slots[None, :] < lengths[:, None]).astype(jnp.float32)
    image_valid = jnp.ones_like(text_valid)
    own_valid = jnp.where(side == 0, image_valid, text_valid)
    other_valid = jnp.where(side == 0, text_valid, image_valid)
    key_valid = jnp.concatenate([own_valid, other_valid], axis=1)
    doubled = jnp.concatenate([buckets, buckets], axis=1)
    start = side * P_SIZE
    block_ids = lax.dynamic_slice(doubled, (start, start), (P_SIZE, 2 * P_SIZE))
    rel_bias = jnp.take(head_vals[:NB], block_ids, axis=0).transpose(2, 0, 1)
    inputs = rows[0].astype(jnp.float32).reshape(num_rows, D)
    normed = layer_norm(inputs, model_vec[0], model_vec[1])
    normed_low = normed.astype(jnp.bfloat16)
    query = (
        (matmul(normed_low, w_query) + model_vec[2])
        .astype(jnp.bfloat16)
        .reshape(num_seq, P_SIZE, H, HD)
    )
    keys_own = matmul(normed_low, w_key).astype(jnp.bfloat16).reshape(num_seq, P_SIZE, H, HD)
    values_own = (
        (matmul(normed_low, w_value) + model_vec[3])
        .astype(jnp.bfloat16)
        .reshape(num_seq, P_SIZE, H, HD)
    )
    keys_other, values_other = from_partner((keys_own, values_own), "mod", 0)
    keys_all = jnp.concatenate([keys_own, keys_other], axis=1)
    values_all = jnp.concatenate([values_own, values_other], axis=1)

    def masked_scores():
        logits = (
            jnp.einsum("gqhe,gkhe->ghqk", query, keys_all, preferred_element_type=jnp.float32)
            * 0.125
            + rel_bias[None]
        )
        return jnp.where(key_valid[:, None, None, :] > 0, logits, -1e30)

    scores = masked_scores()
    log_total = jax.nn.logsumexp(scores, axis=-1, keepdims=True)
    probs = jnp.exp(scores - log_total)
    attended = jnp.einsum(
        "ghqk,gkhe->gqhe",
        probs.astype(jnp.bfloat16),
        values_all,
        preferred_element_type=jnp.float32,
    )
    scaled = (attended * head_scale[None, None, :, None]).reshape(num_rows, D)
    mixed = layer_norm(scaled, model_vec[4], model_vec[5])
    mixed_low = mixed.astype(jnp.bfloat16)
    middle = inputs + (matmul(mixed_low, w_out) + model_vec[6])
    normed_two = layer_norm(middle, model_vec[7], model_vec[8])
    normed_two_low = normed_two.astype(jnp.bfloat16)
    inner = matmul(normed_two_low, w_inner) + inner_vec[0]
    activated = exact_gelu(inner)
    inner_normed = layer_norm(activated, inner_vec[1], inner_vec[2])
    inner_low = inner_normed.astype(jnp.bfloat16)
    result = middle + (matmul(inner_low, w_outer) + model_vec[9])
    result_rows = result.astype(jnp.bfloat16).reshape(1, num_seq, P_SIZE, D)
    grad_out = cotangent[0].astype(jnp.float32).reshape(num_rows, D) * own_valid.reshape(
        num_rows, 1
    )
    grad_branch = grad_out.astype(jnp.bfloat16)
    grad_w_outer = matmul_tn(inner_low, grad_branch)
    grad_b_outer = jnp.sum(grad_branch.astype(jnp.float32), axis=0)
    grad_inner_normed = matmul_nt(grad_branch, w_outer)
    grad_activated, grad_gain_ff, grad_shift_ff = norm_back(
        activated, inner_vec[1], inner_vec[2], grad_inner_normed
    )
    _, gelu_pull = jax.vjp(exact_gelu, inner)
    grad_inner_low = gelu_pull(grad_activated)[0].astype(jnp.bfloat16)
    grad_w_inner = matmul_tn(normed_two_low, grad_inner_low)
    grad_b_inner = jnp.sum(grad_inner_low.astype(jnp.float32), axis=0)
    grad_normed_two = matmul_nt(grad_inner_low, w_inner)
    grad_mid_part, grad_gain_two, grad_shift_two = norm_back(
        middle, model_vec[7], model_vec[8], grad_normed_two
    )
    grad_middle = grad_out + grad_mid_part
    grad_attn_low = grad_middle.astype(jnp.bfloat16)
    grad_w_out = matmul_tn(mixed_low, grad_attn_low)
    grad_b_out = jnp.sum(grad_attn_low.astype(jnp.float32), axis=0)
    grad_mixed = matmul_nt(grad_attn_low, w_out)
    grad_scaled, grad_gain_attn, grad_shift_attn = norm_back(
        scaled, model_vec[4], model_vec[5], grad_mixed
    )
    grad_scaled_heads = grad_scaled.reshape(num_seq, P_SIZE, H, HD)
    grad_head_scale = jnp.sum(grad_scaled_heads * attended, axis=(0, 1, 3))
    grad_attended = (grad_scaled_heads * head_scale[None, None, :, None]).astype(jnp.bfloat16)
    scores_again = masked_scores()
    probs_again = jnp.exp(scores_again - log_total)
    grad_probs = jnp.einsum(
        "gqhe,gkhe->ghqk", grad_attended, values_all, preferred_element_type=jnp.float32
    )
    grad_values_all = jnp.einsum(
        "ghqk,gqhe->gkhe",
        probs_again.astype(jnp.bfloat16),
        grad_attended,
        preferred_element_type=jnp.float32,
    )
    grad_scores = probs_again * (
        grad_probs - jnp.sum(probs_again * grad_probs, axis=-1, keepdims=True)
    )
    grad_scores_low = grad_scores.astype(jnp.bfloat16)
    grad_query = (
        (
            jnp.einsum(
                "ghqk,gkhe->gqhe", grad_scores_low, keys_all, preferred_element_type=jnp.float32
            )
            * 0.125
        )
        .astype(jnp.bfloat16)
        .reshape(num_rows, D)
    )
    grad_keys_all = (
        jnp.einsum("ghqk,gqhe->gkhe", grad_scores_low, query, preferred_element_type=jnp.float32)
        * 0.125
    )
    back_keys, back_values = (
        from_partner(grad_keys_all[:, P_SIZE:].astype(jnp.bfloat16), "mod", 0).astype(jnp.float32),
        from_partner(grad_values_all[:, P_SIZE:].astype(jnp.bfloat16), "mod", 0).astype(
            jnp.float32
        ),
    )
    grad_key = (grad_keys_all[:, :P_SIZE] + back_keys).astype(jnp.bfloat16).reshape(num_rows, D)
    grad_value = (
        (grad_values_all[:, :P_SIZE] + back_values).astype(jnp.bfloat16).reshape(num_rows, D)
    )
    bias_terms = jnp.sum(grad_scores_low.astype(jnp.float32), axis=0).reshape(
        H, 2 * P_SIZE * P_SIZE
    )
    bucket_hot = (
        block_ids.reshape(-1)[:, None] == jnp.arange(NB, dtype=jnp.int32)[None, :]
    ).astype(jnp.float32)
    grad_table = jnp.einsum("pb,hp->bh", bucket_hot, bias_terms, precision=lax.Precision.HIGHEST)
    grad_w_query = matmul_tn(normed_low, grad_query)
    grad_w_key = matmul_tn(normed_low, grad_key)
    grad_w_value = matmul_tn(normed_low, grad_value)
    grad_b_query = jnp.sum(grad_query.astype(jnp.float32), axis=0)
    grad_b_value = jnp.sum(grad_value.astype(jnp.float32), axis=0)
    grad_normed = (
        matmul_nt(grad_query, w_query) + matmul_nt(grad_key, w_key) + matmul_nt(grad_value, w_value)
    )
    grad_in_part, grad_gain_one, grad_shift_one = norm_back(
        inputs, model_vec[0], model_vec[1], grad_normed
    )
    grad_rows = (grad_middle + grad_in_part).reshape(1, num_seq, P_SIZE, D)
    grad_model_vec = jnp.stack(
        [
            grad_gain_one,
            grad_shift_one,
            grad_b_query,
            grad_b_value,
            grad_gain_attn,
            grad_shift_attn,
            grad_b_out,
            grad_gain_two,
            grad_shift_two,
            grad_b_outer,
        ]
    )
    grad_inner_vec = jnp.stack([grad_b_inner, grad_gain_ff, grad_shift_ff])
    grad_heads = jnp.concatenate([grad_table, grad_head_scale[None, :]], axis=0)
    tokens_all = 2 * num_seq * P_SIZE * lax.axis_size("dp")
    local_grad = (
        jnp.concatenate(
            [
                grad_w_query.reshape(-1),
                grad_w_key.reshape(-1),
                grad_w_value.reshape(-1),
                grad_w_out.reshape(-1),
                grad_w_inner.reshape(-1),
                grad_w_outer.reshape(-1),
                grad_model_vec.reshape(-1),
                grad_inner_vec.reshape(-1),
                grad_heads.reshape(-1),
            ]
        )
        / tokens_all
    )
    half_size = local_grad.shape[0] // 2
    own_half = lax.dynamic_slice_in_dim(local_grad, side * half_size, half_size)
    other_half = lax.dynamic_slice_in_dim(local_grad, (1 - side) * half_size, half_size)
    partner_half = from_partner(other_half.astype(jnp.bfloat16), "mod", 0).astype(other_half.dtype)
    grad_shard = lax.psum_scatter(own_half + partner_half, "dp", scatter_dimension=0, tiled=True)
    square_sum = lax.psum(jnp.sum(grad_shard * grad_shard), ("mod", "dp"))
    grad_norm = jnp.sqrt(square_sum)
    clip_scale = jnp.minimum(1.0, 0.25 / (grad_norm + 1e-06))
    clipped = grad_shard * clip_scale
    new_first = 0.5 * first_moment + 0.5 * clipped
    new_second = 0.6 * second_moment + 0.4 * clipped * clipped
    direction = new_first / (1.0 - 0.5**STEP) / (jnp.sqrt(new_second / (1.0 - 0.6**STEP)) + 1e-08)
    new_master = master - 0.04 * (direction + 0.01 * master)
    new_average = 0.5 * average + 0.5 * new_master
    return (
        result_rows,
        grad_rows,
        grad_norm,
        new_master,
        new_first,
        new_second,
        new_average,
        new_master.astype(jnp.bfloat16),
    )


def solution(mesh):
    placed = (
        P("mod", "dp", None, None),
        P("mod", "dp", None, None),
        P(("mod", "dp")),
        P(("mod", "dp")),
        P(("mod", "dp")),
        P(("mod", "dp")),
        P("dp"),
        P(),
    )
    return jax.shard_map(
        on_device,
        mesh=mesh,
        in_specs=placed,
        out_specs=(
            P("mod", "dp", None, None),
            P("mod", "dp", None, None),
            P(),
            P(("mod", "dp")),
            P(("mod", "dp")),
            P(("mod", "dp")),
            P(("mod", "dp")),
            P(("mod", "dp")),
        ),
        check_vma=False,
    )
```

profile of v0, /device:TPU:0, one launch (start us, length us, event | category | flops | bytes accessed | tf_op | source)
XLA Modules:
  0.0 1247.1 jit_solution(1993844263286797758)
XLA Ops:
  8.4 5.2 broadcast.424
  13.7 7.6 dynamic-update-slice
  37.8 236.4 %all-reduce.5.cloned.1.call-done = bf16[7095552]{0:T(1024)(128)(2,1)} async-done(((bf16[7095552]{0:T(1024)(128)(2,1)}), bf16[7095552]{0:T(1024)(128)(2,1)}) %all-reduce.5.cloned.1.call-update) | async-done | bytes 14191120
  284.8 141.8 %gather_fusion = f32[76832,12]{1,0:T(8,128)} fusion(f32[63,12]{1,0:T(8,128)S(1)} %slice.186, s32[77824]{0:T(1024)S(1)} %pad_clamp_fusion), kind=kCustom, calls=%fused_computation | custom fusion | bytes 7683200 | tf_op jit(solution)/shard_map/jit(_take)/gather | solution.py:89
  426.6 25.7 %copy.208 = f32[196,392,12]{0,1,2:T(8,128)} copy(f32[196,392,12]{2,1,0:T(8,128)} %bitcast.63) | data formatting | bytes 7375872 | tf_op jit(solution)/shard_map/jit(_take)/gather | solution.py:89
  487.1 8.2 fusion.51
  495.3 9.2 slice.201
  504.5 8.2 reshape.520
  538.7 14.4 %fusion.47 = (f32[392]{0:T(512)S(1)}, f32[392,3072]{1,0:T(8,128)S(1)}, f32[392,3072]{1,0:T(8,128)S(1)}, f32[392,3072]{1,0:T(8,128)S(1)}) fusion(f32[3072]{0:T(1024)S(1)} %get-tuple-element.111, bf16[768,3072]{1,0:T(8,128)(2,1)} %reshape.520, f32[392,768]{1,0:T(8,128)S(1)} %get-tuple-element.132, f32[768]{0:T(1024)S(1)} %copy-done.48, ...), kind=kOutput, calls=%fused_computation.163 | convolution fusion | flops 1930671744 | bytes 20396640 | tf_op jit(solution)/shard_map/dot_general | solution.py:37
  553.2 6.7 multiply_reduce_fusion.2
  562.3 4.8 convert_reduce_fusion.1
  567.1 4.7 multiply_reduce_fusion.5
  576.5 5.4 convolution_bitcast_fusion
  587.7 7.1 convolution_bitcast_fusion.1
  594.8 7.1 multiply_reduce_fusion
  602.0 6.9 convert_reduce_fusion
  608.9 5.8 multiply_bitcast_fusion
  640.4 9.6 copy.237
  650.0 8.9 fusion.38
  659.0 10.7 reshape.532
  669.9 5.9 copy.221
  675.8 6.6 reshape.543
  682.4 11.8 fusion
  728.2 9.6 constant_dynamic-update-slice_fusion.4
  745.7 10.7 broadcast_multiply_fusion
  756.4 9.4 copy-done.1
  765.8 5.0 dynamic_slice.22
  770.8 11.6 collective-permute-done.4
  782.4 13.2 %convert_add_fusion = f32[3547776]{0:T(1024)} fusion(bf16[3547776]{0:T(1024)(128)(2,1)} %collective-permute-done.4, f32[7095552]{0:T(1024)} %copy-done.1, s32[]{:T(128)S(6)} %select_n.76), kind=kLoop, calls=%fused_computation.3 | loop fusion | flops 7095552 | bytes 35477764 | tf_op jit(solution)/shard_map/add | solution.py:261
  797.5 7.7 fusion.15
  810.0 380.3 %all-reduce.7.cloned.1.call-done = f32[3547776]{0:T(1024)} async-done(((f32[3547776]{0:T(1024)}), f32[3547776]{0:T(1024)}) %all-reduce.7.cloned.1.call-update) | async-done | bytes 14191120
  1194.1 39.2 %psum.7 = f32[]{:T(128)} all-reduce(f32[]{:T(128)} %multiply_reduce_fusion.13), channel_id=1, replica_groups=mesh['mod'=2,'dp'=16] {'mod','dp'}, use_global_device_ids=true, to_apply=%region_36.37 | all-reduce | flops 1 | bytes 8 | tf_op jit(solution)/shard_map/psum | solution.py:262
  (275 shorter events, 183.7 us)
Async XLA Ops:
  7.2 267.0 %all-reduce.5.cloned.1.call-start = ((), (), s32[]{:S(2)}) async-start(), calls=%async_computation | async-start | bytes 28385280
  21.3 1169.0 %all-reduce.7.cloned.1.call-start = ((), (), s32[]{:S(2)}) async-start(), calls=%async_computation.1 | async-start | bytes 28385280
  30.4 7.3 copy-start.29
  31.9 242.3 %copy-start.41 = (f32[392]{0:T(512)}, f32[392]{0:T(512)S(1)}, u32[]{:S(2)}) copy-start(f32[392]{0:T(512)S(1)} %add.225) | copy-start | bytes 4708
  31.9 423.8 %copy-start.37 = (f32[392]{0:T(512)}, f32[392]{0:T(512)S(1)}, u32[]{:S(2)}) copy-start(f32[392]{0:T(512)S(1)} %rsqrt.47) | copy-start | bytes 4708
  32.0 423.7 %copy-start.39 = (f32[392]{0:T(512)}, f32[392]{0:T(512)S(1)}, u32[]{:S(2)}) copy-start(f32[392]{0:T(512)S(1)} %div.109) | copy-start | bytes 4708
  275.5 237.3 %copy-start.34 = (f32[768]{0:T(1024)}, f32[768]{0:T(1024)S(1)}, u32[]{:S(2)}) copy-start(f32[768]{0:T(1024)S(1)} %get-tuple-element.121) | copy-start | bytes 9220
  462.2 55.8 %copy-start.11 = (bf16[2,196,12,64]{1,3,2,0:T(8,128)(2,1)}, bf16[2,196,12,64]{1,3,2,0:T(8,128)(2,1)S(1)}, u32[]{:S(2)}) copy-start(bf16[2,196,12,64]{1,3,2,0:T(8,128)(2,1)S(1)} %copy.206) | copy-start | bytes 1806340
  474.5 43.4 %collective-permute-start.1 = (bf16[2,196,12,64]{1,3,2,0:T(8,128)(2,1)}, bf16[2,196,12,64]{1,3,2,0:T(8,128)(2,1)}, u32[]{:S(2)}, u32[]{:S(2)}) collective-permute-start(bf16[2,196,12,64]{1,3,2,0:T(8,128)(2,1)} %copy.205), channel_id=1, source_target_pairs={{0,16},{16,0},{1,17},{17,1},{2,18},{18,2},{3,19},{19,3},{4,20},{20... | collective-permute-start | bytes 1806344 | tf_op jit(solution)/shard_map/ppermute | solution.py:22
  486.6 36.9 %collective-permute-start = (bf16[2,196,12,64]{1,3,2,0:T(8,128)(2,1)}, bf16[2,196,12,64]{1,3,2,0:T(8,128)(2,1)}, u32[]{:S(2)}, u32[]{:S(2)}) collective-permute-start(bf16[2,196,12,64]{1,3,2,0:T(8,128)(2,1)} %copy.201), channel_id=1, source_target_pairs={{0,16},{16,0},{1,17},{17,1},{2,18},{18,2},{3,19},{19,3},{4,20},{20... | collective-permute-start | bytes 1806344 | tf_op jit(solution)/shard_map/ppermute | solution.py:22
  504.5 8.2 copy-start.32
  538.4 38.2 %copy-start.20 = (f32[392,768]{1,0:T(8,128)}, f32[392,768]{1,0:T(8,128)S(1)}, u32[]{:S(2)}) copy-start(f32[392,768]{1,0:T(8,128)S(1)} %get-tuple-element.132) | copy-start | bytes 3612676
  538.7 14.5 %copy-start.18 = (f32[392,768]{1,0:T(8,128)S(1)}, f32[392,768]{1,0:T(8,128)}, u32[]{:S(2)}) copy-start(f32[392,768]{1,0:T(8,128)} %reshape.546) | copy-start | bytes 3612676
  538.7 14.5 %copy-start.46 = (f32[392]{0:T(512)S(1)}, f32[392]{0:T(512)}, u32[]{:S(2)}) copy-start(f32[392]{0:T(512)} %select_n.75) | copy-start | bytes 4708
  553.2 9.1 copy-start.3
  587.7 7.2 copy-start.14
  587.7 14.3 %slice-start = ((s8[9633792]{0:T(1024)(128)(4,1)}), s8[4194304]{0:T(1024)(128)(4,1)S(1)}, s32[]{:S(2)}) async-start(s8[9633792]{0:T(1024)(128)(4,1)} %bitcast.61), calls=%async_computation.2 | async-start | bytes 8388608
  587.7 14.3 %slice-start.1 = ((s8[9633792]{0:T(1024)(128)(4,1)}), s8[4194304]{0:T(1024)(128)(4,1)S(1)}, s32[]{:S(2)}) async-start(s8[9633792]{0:T(1024)(128)(4,1)} %bitcast.61), calls=%async_computation.3 | async-start | bytes 8388608
  594.8 7.1 slice-start.2
  602.0 6.9 copy-start.12
  624.9 73.5 %collective-permute-start.2 = (bf16[2,196,12,64]{1,3,2,0:T(8,128)(2,1)}, bf16[2,196,12,64]{1,3,2,0:T(8,128)(2,1)}, u32[]{:S(2)}, u32[]{:S(2)}) collective-permute-start(bf16[2,196,12,64]{1,3,2,0:T(8,128)(2,1)} %slice.247), channel_id=1, source_target_pairs={{0,16},{16,0},{1,17},{17,1},{2,18},{18,2},{3,19},{19,3},{4,20},{20... | collective-permute-start | bytes 1806344 | tf_op jit(solution)/shard_map/ppermute | solution.py:22
  627.7 79.2 %collective-permute-start.3 = (bf16[2,196,12,64]{1,3,2,0:T(8,128)(2,1)}, bf16[2,196,12,64]{1,3,2,0:T(8,128)(2,1)}, u32[]{:S(2)}, u32[]{:S(2)}) collective-permute-start(bf16[2,196,12,64]{1,3,2,0:T(8,128)(2,1)} %slice.246), channel_id=1, source_target_pairs={{0,16},{16,0},{1,17},{17,1},{2,18},{18,2},{3,19},{19,3},{4,20},{20... | collective-permute-start | bytes 1806344 | tf_op jit(solution)/shard_map/ppermute | solution.py:22
  640.4 9.7 copy-start.19
  682.4 11.8 copy-start.16
  726.6 11.2 slice-start.3
  728.2 9.6 slice-start.4
  728.2 9.6 slice-start.5
  756.4 9.4 copy-start.1
  770.8 11.7 collective-permute-start.4
  797.5 10.3 copy-start.42
  809.8 424.2 %copy-start.24 = (f32[221736]{0:T(1024)S(1)}, f32[221736]{0:T(1024)}, u32[]{:S(2)}) copy-start(f32[221736]{0:T(1024)} %param.10) | copy-start | bytes 2660836
  810.0 424.0 %copy-start.30 = (f32[221736]{0:T(1024)S(1)}, f32[221736]{0:T(1024)}, u32[]{:S(2)}) copy-start(f32[221736]{0:T(1024)} %param.11) | copy-start | bytes 2660836
  (33 other events, 103.5 us)
Sparse Core Ops, SparseCore 0:
  21.4 252.6 all-reduce.4
  795.8 394.5 all-reduce.6
where the time goes:
time: 1260 us; the launch traced here: 1250 us
  waiting for transfers between devices  628 us (50%)
  local copies, waits for them, and re-layouts  376 us (30%)
  matrix products  119 us (9%)
  other arithmetic  65.5 us (5%)
  blocking collectives  39.2 us (3%)
  between operations  17.7 us (1%)
    unnamed x4, waiting for transfers between devices  617 us
    gather x2, local copies, waits for them, and re-layouts, on_device(): rel_bias = jnp.take(head_vals[:NB], block_ids, axis=0).transpose(2, 0, 1)  168 us
    unnamed x131, local copies, waits for them, and re-layouts  66.3 us
    psum x1, blocking collectives, on_device(): square_sum = lax.psum(jnp.sum(grad_shard * grad_shard), ('mod', 'dp'))  39.2 us
    slice x7, local copies, waits for them, and re-layouts, unpack(): pieces.append(flat[offset:offset + extent].reshape(dims_pair))  36.2 us
    dot_general x6, matrix products, matmul(): return jnp.dot(left, right, preferred_element_type=jnp.float32)  31.7 us
  transfers between devices with their start and end apart: 7, of which 3 were waited for; matrix products, arithmetic and copies ran while one was open for 13% of the time, Pallas kernels for 0%

commit v1 on v0

--- a/solution.py
+++ b/solution.py
@@ -1,6 +1,9 @@
+import functools
 import jax
 import jax.numpy as jnp
 from jax import lax
+from jax.experimental import pallas as pl
+from jax.experimental.pallas import tpu as pltpu
 from jax.sharding import PartitionSpec as P
 
 D = 768
@@ -10,6 +13,177 @@
 NB = 63
 P_SIZE = 196
 STEP = 5
+
+
+HALF = D // 2
+BLOCK = 144
+PHASE_ROWS = 32 * BLOCK
+BF = jnp.bfloat16
+F32 = jnp.float32
+DP = 16
+EDGE = 17664
+
+
+def x_swap():
+    return [(i, i ^ 1) for i in range(DP)]
+
+
+def y_swap():
+    return [(i, i ^ 2) for i in range(DP)]
+
+
+def z_turn(step):
+    return [(i, (i // 4 + step) % 4 * 4 + i % 4) for i in range(DP)]
+
+
+def send_dp(block, route):
+    return lax.ppermute(block, "dp", route)
+
+
+def send_mod(block):
+    return lax.ppermute(block, "mod", [(0, 1), (1, 0)])
+
+
+def pack_shard(own, side, place):
+    lead = 8832 * side + 552 * place
+    count = BLOCK * D
+    lent = lax.dynamic_slice(own, (count - lead,), (count,))
+    given = send_mod(lent)
+    nxt = [(i, i + 1) for i in range(2 * DP - 1)]
+    edge = lax.ppermute(own[own.shape[0] - EDGE :], ("mod", "dp"), nxt)
+    kept = lax.dynamic_slice(jnp.concatenate([edge, own[:count]]), (EDGE - lead,), (count,))
+    kept = kept.reshape(BLOCK, D)
+    given = given.reshape(BLOCK, D)
+    return jnp.where(side == 0, kept, given), jnp.where(side == 0, given, kept)
+
+
+def unpack_shard(first, second, vec, side, place):
+    lead = 8832 * side + 552 * place
+    even = jnp.where(side == 0, first, second).reshape(-1)
+    lent = jnp.where(side == 0, second, first)
+    odd = send_mod(lent).reshape(-1)
+    back = [(i + 1, i) for i in range(2 * DP - 1)]
+    edge = lax.ppermute(even[:EDGE], ("mod", "dp"), back)
+    is_last = jnp.logical_and(side == 1, place == DP - 1)
+    edge = jnp.where(is_last, vec.reshape(-1)[:EDGE], edge)
+    return lax.dynamic_slice(jnp.concatenate([even, odd, edge]), (lead,), (221736,))
+
+
+def sum_all_small(part):
+    for route in (x_swap(), y_swap(), z_turn(2)):
+        part = part + send_dp(part, route)
+    part = part + send_dp(part, [(i, i ^ 4) for i in range(DP)])
+    return part + send_mod(part)
+
+
+def gather_phase(block):
+    stack = jnp.stack([block] + [send_dp(block, z_turn(step)) for step in (1, 2, 3)])
+    left, right = stack[:, :, :HALF], stack[:, :, HALF:]
+    left_x = send_dp(left, x_swap())
+    right_y = send_dp(right, y_swap())
+    left_y = send_dp(left, y_swap())
+    right_x = send_dp(right, x_swap())
+    left_xy = send_dp(left_x, y_swap())
+    right_xy = send_dp(right_y, x_swap())
+    mine = [left, left_x, left_y, left_xy, right, right_x, right_y, right_xy]
+    return mine + [send_mod(piece) for piece in mine]
+
+
+def coords():
+    side = lax.axis_index("mod")
+    place = lax.axis_index("dp")
+    return jnp.stack([side, place // 4, place // 2 % 2, place % 2]).astype(jnp.int32)
+
+
+def assemble_body(phase, spot, *refs):
+    pieces, out, sem = refs[:16], refs[16], refs[17]
+    side, z, y, x = spot[0], spot[1], spot[2], spot[3]
+    copies = []
+    for index in range(16):
+        other, half, yr, xr = index // 8, index // 4 % 2, index // 2 % 2, index % 2
+        owner = side ^ other
+        parity = owner if phase == 0 else 1 - owner
+        for turn in range(4):
+            home = ((z - turn) & 3) * 4 + (y ^ yr) * 2 + (x ^ xr)
+            copies.append(
+                pltpu.make_async_copy(
+                    pieces[index].at[turn],
+                    out.at[home * 2 + parity, :, pl.ds(half * HALF, HALF)],
+                    sem.at[index * 4 + turn],
+                )
+            )
+    for copy in copies:
+        copy.start()
+    for copy in copies:
+        copy.wait()
+
+
+def assemble(phase, spot, pieces):
+    return pl.pallas_call(
+        functools.partial(assemble_body, phase),
+        out_shape=jax.ShapeDtypeStruct((32, BLOCK, D), BF),
+        in_specs=[pl.BlockSpec(memory_space=pltpu.SMEM)] + [pl.BlockSpec(memory_space=pl.ANY)] * 16,
+        out_specs=pl.BlockSpec(memory_space=pltpu.VMEM),
+        scratch_shapes=[pltpu.SemaphoreType.DMA((64,))],
+        name="assemble",
+    )(spot, *pieces).reshape(PHASE_ROWS, D)
+
+
+def scatter_body(phase, spot, src, out, sem):
+    side, z, y, x = spot[0], spot[1], spot[2], spot[3]
+    copies = []
+    for block in range(32):
+        home, parity = block // 2, block % 2
+        owner = parity if phase == 0 else 1 - parity
+        other = side ^ owner
+        turn = (home // 4 - z) & 3
+        yr = (home // 2 % 2) ^ y
+        xr = (home % 2) ^ x
+        for half in range(2):
+            copies.append(
+                pltpu.make_async_copy(
+                    src.at[block, :, pl.ds(half * HALF, HALF)],
+                    out.at[other, half, yr, xr, turn],
+                    sem.at[block * 2 + half],
+                )
+            )
+    for copy in copies:
+        copy.start()
+    for copy in copies:
+        copy.wait()
+
+
+def scatter(phase, spot, grads):
+    return pl.pallas_call(
+        functools.partial(scatter_body, phase),
+        out_shape=jax.ShapeDtypeStruct((2, 2, 2, 2, 4, BLOCK, HALF), BF),
+        in_specs=[pl.BlockSpec(memory_space=pltpu.SMEM), pl.BlockSpec(memory_space=pltpu.VMEM)],
+        out_specs=pl.BlockSpec(memory_space=pl.ANY),
+        scratch_shapes=[pltpu.SemaphoreType.DMA((64,))],
+        name="scatter",
+    )(spot, grads.reshape(32, BLOCK, D))
+
+
+def plus(left, right):
+    return (left.astype(F32) + right.astype(F32)).astype(BF)
+
+
+def reduce_phase(parts):
+    theirs = send_mod(parts[1])
+    left_out = send_dp(plus(parts[0, 0, :, 1], theirs[0, :, 1]), x_swap())
+    right_out = send_dp(plus(parts[0, 1, 1], theirs[1, 1]), y_swap())
+    left_in = plus(parts[0, 0, :, 0], theirs[0, :, 0])
+    right_in = plus(parts[0, 1, 0], theirs[1, 0])
+    left_next = send_dp(plus(left_in[1], left_out[1]), y_swap())
+    right_next = send_dp(plus(right_in[1], right_out[1]), x_swap())
+    left = left_in[0].astype(F32) + left_out[0].astype(F32) + left_next.astype(F32)
+    right = right_in[0].astype(F32) + right_out[0].astype(F32) + right_next.astype(F32)
+    both = jnp.concatenate([left, right], axis=-1)
+    low = both.astype(BF)
+    total = both[0]
+    for step in (1, 2, 3):
+        total = total + send_dp(low[step], z_turn(step)).astype(F32)
+    return total
 
 
 def from_partner(block, axis, bit):
@@ -66,8 +240,24 @@
 
 def on_device(rows, cotangent, master, first_moment, second_moment, average, lengths, buckets):
     side = lax.axis_index("mod")
+    place = lax.axis_index("dp")
+    fast = lax.axis_size("dp") == DP
     own_copy = master.astype(jnp.bfloat16)
-    flat = lax.all_gather(own_copy, ("mod", "dp"), axis=0, tiled=True)
+    if fast:
+        spot = coords()
+        first, second = pack_shard(own_copy, side, place)
+        is_last = jnp.logical_and(side == 1, place == DP - 1)
+        vec = jnp.where(is_last, own_copy[-EDGE:], jnp.zeros((), BF))
+        vec = jnp.pad(vec, (0, D)).reshape(24, D)
+        flat = jnp.concatenate(
+            [
+                assemble(0, spot, gather_phase(first)),
+                assemble(1, spot, gather_phase(second)),
+                sum_all_small(vec)[:23],
+            ]
+        ).reshape(-1)
+    else:
+        flat = lax.all_gather(own_copy, ("mod", "dp"), axis=0, tiled=True)
     w_query, w_key, w_value, w_out, w_inner, w_outer, vec_model, vec_inner, head_table = unpack(
         flat
     )
@@ -254,11 +444,19 @@
         )
         / tokens_all
     )
-    half_size = local_grad.shape[0] // 2
-    own_half = lax.dynamic_slice_in_dim(local_grad, side * half_size, half_size)
-    other_half = lax.dynamic_slice_in_dim(local_grad, (1 - side) * half_size, half_size)
-    partner_half = from_partner(other_half.astype(jnp.bfloat16), "mod", 0).astype(other_half.dtype)
-    grad_shard = lax.psum_scatter(own_half + partner_half, "dp", scatter_dimension=0, tiled=True)
+    if fast:
+        table = local_grad.reshape(-1, D)
+        low = table[: 2 * PHASE_ROWS].astype(BF)
+        second = reduce_phase(scatter(1, spot, low[PHASE_ROWS:]))
+        first = reduce_phase(scatter(0, spot, low[:PHASE_ROWS]))
+        vec_grad = sum_all_small(jnp.pad(table[2 * PHASE_ROWS :], ((0, 1), (0, 0))))
+        grad_shard = unpack_shard(first, second, vec_grad, side, place)
+    else:
+        half_size = local_grad.shape[0] // 2
+        own_half = lax.dynamic_slice_in_dim(local_grad, side * half_size, half_size)
+        other_half = lax.dynamic_slice_in_dim(local_grad, (1 - side) * half_size, half_size)
+        partner_half = from_partner(other_half.astype(jnp.bfloat16), "mod", 0).astype(other_half.dtype)
+        grad_shard = lax.psum_scatter(own_half + partner_half, "dp", scatter_dimension=0, tiled=True)
     square_sum = lax.psum(jnp.sum(grad_shard * grad_shard), ("mod", "dp"))
     grad_norm = jnp.sqrt(square_sum)
     clip_scale = jnp.minimum(1.0, 0.25 / (grad_norm + 1e-06))

time: 1260 us -> 840 us (0.67)
  waiting for transfers between devices: 628 us -> 81.9 us
  starting transfers between devices: 1.12 us -> 96.6 us
  Pallas kernels: 0 us -> 27.5 us
  other arithmetic: 65.5 us -> 88.3 us
  between operations: 17.7 us -> 4.69 us
    unnamed x4 -> x0, waiting for transfers between devices: 617 us -> none
    ppermute x0 -> x64, starting transfers between devices: none -> 95.5 us  [the longest x40 87.5 us: send_dp(): return lax.ppermute(block, 'dp', route)]
    ppermute x0 -> x64, waiting for transfers between devices: none -> 81.9 us  [the longest x40 78.2 us: send_dp(): return lax.ppermute(block, 'dp', route)]
    slice x8 -> x9, local copies, waits for them, and re-layouts: 36.3 us -> 7.34 us  [the longest x1 5.38 us: on_device(): first = reduce_phase(scatter(0, spot, low[:PHASE_ROWS]))]
    pallas_call x0 -> x4, Pallas kernels: none -> 27.5 us  [the longest x2 14.5 us: assemble(): pl.pallas_call(functools.partial(assemble_body, phase), out_shape=jax.Sha...]
    reshape x0 -> x5, local copies, waits for them, and re-layouts: none -> 26.2 us  [the longest x2 26.1 us: scatter(): grads.reshape(32, BLOCK, D)]
    another operation x0 -> x4, other arithmetic: none -> 24.4 us
    unnamed x131 -> x202, local copies, waits for them, and re-layouts: 66.3 us -> 45.5 us
  transfers between devices with their start and end apart: 7 -> 68, of which waited for: 3 -> 16; matrix products, arithmetic and copies ran while one was open for 13% -> 49% of each run, Pallas kernels for 0% -> 3%
where the time goes in v1:
time: 840 us; the launch traced here: 825 us
  local copies, waits for them, and re-layouts  374 us (45%)
  matrix products  112 us (13%)
  starting transfers between devices  96.6 us (12%)
  other arithmetic  88.3 us (11%)
  waiting for transfers between devices  81.9 us (10%)
  blocking collectives  39.5 us (5%)
  Pallas kernels  27.5 us (3%)
    gather x2, local copies, waits for them, and re-layouts, on_device(): rel_bias = jnp.take(head_vals[:NB], block_ids, axis=0).transpose(2, 0, 1)  182 us
    ppermute x40, starting transfers between devices, send_dp(): return lax.ppermute(block, 'dp', route)  87.5 us
    ppermute x40, waiting for transfers between devices, send_dp(): return lax.ppermute(block, 'dp', route)  78.2 us
    unnamed x202, local copies, waits for them, and re-layouts  45.5 us
    psum x1, blocking collectives, on_device(): square_sum = lax.psum(jnp.sum(grad_shard * grad_shard), ('mod', 'dp'))  39.5 us
    dot_general x6, matrix products, matmul(): return jnp.dot(left, right, preferred_element_type=jnp.float32)  33.2 us
    reshape x2, local copies, waits for them, and re-layouts, scatter(): grads.reshape(32, BLOCK, D)  26.1 us
    dot_general x6, matrix products, matmul_tn(): lax.dot_general(left, right, (((0,), (0,)), ((), ())), preferred_element_...  23.4 us
  transfers between devices with their start and end apart: 68, of which 16 were waited for; matrix products, arithmetic and copies ran while one was open for 49% of the time, Pallas kernels for 3%

profile of v1, /device:TPU:0, one launch (start us, length us, event | category | flops | bytes accessed | tf_op | source)
XLA Modules:
  0.0 825.1 jit_solution(5309816598549283956)
XLA Ops:
  49.0 13.6 %collective-permute-done.8 = bf16[144,768]{1,0:T(8,128)(2,1)S(1)} collective-permute-done((bf16[144,768]{1,0:T(8,128)(2,1)S(1)}, bf16[144,768]{1,0:T(8,128)(2,1)S(1)}, u32[]{:S(2)}, u32[]{:S(2)}) %collective-permute-start.8) | collective-permute-done | bytes 221216 | tf_op jit(solution)/shard_map/ppermute | solution.py:40
  68.0 155.9 %gather_fusion = f32[76832,12]{1,0:T(8,128)} fusion(f32[63,12]{1,0:T(8,128)S(1)} %slice.313, s32[77824]{0:T(1024)} %pad_clamp_fusion), kind=kCustom, calls=%fused_computation | custom fusion | bytes 7683200 | tf_op jit(solution)/shard_map/jit(_take)/gather | solution.py:279
  223.9 25.7 %copy.244 = f32[196,392,12]{0,1,2:T(8,128)} copy(f32[196,392,12]{2,1,0:T(8,128)} %bitcast.205) | data formatting | bytes 7375872 | tf_op jit(solution)/shard_map/jit(_take)/gather | solution.py:279
  282.0 7.2 collective-permute-done.12.refs_3_
  295.2 7.2 assemble.2
  329.3 7.3 assemble.3
  341.5 8.9 %reshape.609 = bf16[768,3072]{1,0:T(8,128)(2,1)} reshape(bf16[3072,768]{1,0:T(8,128)(2,1)} %pad_maximum_fusion) | data formatting | bytes 9437184 | tf_op jit(solution)/shard_map/reshape | solution.py:236
  350.4 5.7 fusion.108
  373.1 15.6 %fusion.99 = (f32[392]{0:T(512)S(1)}, f32[392,3072]{1,0:T(8,128)S(1)}, f32[392,3072]{1,0:T(8,128)S(1)}, f32[392,3072]{1,0:T(8,128)}) fusion(f32[3072]{0:T(1024)S(1)} %add.424, bf16[768,3072]{1,0:T(8,128)(2,1)} %reshape.609, f32[392,768]{1,0:T(8,128)S(1)} %get-tuple-element.159, f32[768]{0:T(1024)S(1)} %copy-done.79, f32[768]{0:T(1024)S(1)} %copy-done.71, ...), kind=kOutput, calls=%fused_computation.277 | convolution fusion | flops 1930671744 | bytes 20396640 | tf_op jit(solution)/shard_map/dot_general | solution.py:211
  421.1 5.4 convolution_bitcast_fusion.1
  433.0 5.8 convert_reduce_fusion
  457.6 9.0 %fusion.87 = f32[3072,768]{1,0:T(8,128)} fusion(f32[392,768]{1,0:T(8,128)S(1)} %copy-done.27, f32[392]{0:T(512)S(1)} %copy-done.77, f32[392,3072]{1,0:T(8,128)} %copy-done.1, f32[3072]{0:T(1024)S(1)} %copy-done.75, f32[3072]{0:T(1024)S(1)} %copy-done.57, f32[392]{0:T(512)S(1)} %get-tuple-element.152, f32[392]{0:T(512)S(1)} %broadcast_multiply_fusion.3), kind=kOutput, calls=%fused_computation.270 | convolution fusion | flops 1856311296 | bytes 15487584 | tf_op jit(solution)/shard_map/dot_general | solution.py:215
  470.4 9.4 %copy.285 = f32[96,24,8,128]{3,1,2,0:T(8,128)} copy(f32[96,24,8,128]{3,2,1,0:T(8,128)} %convolution_bitcast_fusion) | data formatting | bytes 18874368
  479.8 10.7 %reshape.621 = f32[2359296]{0:T(1024)} reshape(f32[3072,768]{1,0:T(8,128)} %fusion.87) | data formatting | bytes 18874368 | tf_op jit(solution)/shard_map/reshape | solution.py:439
  490.8 5.9 copy.257
  496.6 6.7 reshape.632
  503.3 11.6 %fusion = f32[63,12]{0,1:T(8,128)S(1)} fusion(f32[12,76832]{1,0:T(8,128)} %reshape.632, s32[76832]{0:T(1024)S(1)} %copy-done.51), kind=kOutput, calls=%fused_computation.2 | convolution fusion | flops 701860352 | bytes 3998288 | tf_op jit(solution)/shard_map/pb,hp->bh/dot_general | solution.py:401
  553.1 9.6 %constant_dynamic-update-slice_fusion.4 = f32[7095552]{0:T(1024)} fusion(f32[7095552]{0:T(1024)} %constant_dynamic-update-slice_fusion.5, f32[2359296]{0:T(1024)} %bitcast.217), kind=kLoop, calls=%fused_computation.222 | loop fusion | bytes 18874368
  570.6 21.4 %fusion.89 = (bf16[7095552]{0:T(1024)(128)(2,1)S(1)}, f32[7095552]{0:T(1024)}) fusion(f32[7095552]{0:T(1024)} %constant_dynamic-update-slice_fusion), kind=kLoop, calls=%fused_computation.272 | loop fusion | flops 14191104 | bytes 70955520 | tf_op jit(solution)/shard_map/convert.18
  592.0 5.4 fusion.103
  597.4 13.2 %reshape.635.src = bf16[32,144,768]{2,1,0:T(8,128)(2,1)} reshape(bf16[3538944]{0:T(1024)(128)(2,1)} %get-tuple-element.120) | data formatting | bytes 14155776 | tf_op jit(solution)/shard_map/reshape | solution.py:164
  610.6 6.5 scatter.3
  621.7 12.9 %reshape.634.src = bf16[32,144,768]{2,1,0:T(8,128)(2,1)} reshape(bf16[3538944]{0:T(1024)(128)(2,1)} %get-tuple-element.119) | data formatting | bytes 14155776 | tf_op jit(solution)/shard_map/reshape | solution.py:164
  634.6 6.5 scatter.2
  645.4 6.9 fusion.35
  672.3 12.3 %collective-permute-start.64 = (f32[24,768]{1,0:T(8,128)S(1)}, f32[24,768]{1,0:T(8,128)S(1)}, u32[]{:S(2)}, u32[]{:S(2)}) collective-permute-start(f32[24,768]{1,0:T(8,128)S(1)} %add.474), channel_id=1, source_target_pairs={{0,8},{1,9},{2,10},{3,11},{4,12},{5,13},{6,14},{7,15},{8,0},{9,1},... | collective-permute-start | bytes 221192 | tf_op jit(solution)/shard_map/ppermute | solution.py:40
  692.0 15.7 %collective-permute-done.48 = bf16[2,4,144,384]{3,2,1,0:T(8,128)(2,1)S(1)} collective-permute-done((bf16[2,4,144,384]{3,2,1,0:T(8,128)(2,1)S(1)}, bf16[2,4,144,384]{3,2,1,0:T(8,128)(2,1)S(1)}, u32[]{:S(2)}, u32[]{:S(2)}) %collective-permute-start.48) | collective-permute-done | bytes 884768 | tf_op jit(solution)/shard_map/ppermute | solution.py:40
  709.9 7.8 collective-permute-done.57
  720.3 11.9 %collective-permute-start.59 = (bf16[144,768]{1,0:T(8,128)(2,1)}, bf16[144,768]{1,0:T(8,128)(2,1)}, u32[]{:S(2)}, u32[]{:S(2)}) collective-permute-start(bf16[144,768]{1,0:T(8,128)(2,1)} %get-tuple-element.135), channel_id=1, source_target_pairs={{0,8},{1,9},{2,10},{3,11},{4,12},{5,13},{6,14},{7,15},{8,0},{9,1},... | collective-permute-start | bytes 663560 | tf_op jit(solution)/shard_map/ppermute | solution.py:40
  741.3 7.9 collective-permute-start.50
  760.8 6.2 collective-permute-done.51
  778.6 39.5 %psum.7 = f32[]{:T(128)} all-reduce(f32[]{:T(128)} %get-tuple-element.91), channel_id=1, replica_groups=mesh['mod'=2,'dp'=16] {'mod','dp'}, use_global_device_ids=true, to_apply=%region_35.36 | all-reduce | flops 1 | bytes 8 | tf_op jit(solution)/shard_map/psum | solution.py:460
  (523 shorter events, 325.3 us)
Async XLA Ops:
  6.6 31.0 %collective-permute-start.6 = (bf16[110592]{0:T(1024)(128)(2,1)}, bf16[110592]{0:T(1024)(128)(2,1)}, u32[]{:S(2)}, u32[]{:S(2)}) collective-permute-start(bf16[110592]{0:T(1024)(128)(2,1)} %get-tuple-element.145), channel_id=1, source_target_pairs={{0,16},{16,0},{1,17},{17,1},{2,18},{18,2},{3,19},{19,3},{4,20},{20... | collective-permute-start | bytes 663560 | tf_op jit(solution)/shard_map/ppermute | solution.py:44
  6.6 31.0 %collective-permute-start.5 = (bf16[17664]{0:T(1024)(128)(2,1)}, bf16[17664]{0:T(1024)(128)(2,1)}, u32[]{:S(2)}, u32[]{:S(2)}) collective-permute-start(bf16[17664]{0:T(1024)(128)(2,1)} %get-tuple-element.143), channel_id=1, source_target_pairs={{0,1},{1,2},{2,3},{3,4},{4,5},{5,6},{6,7},{7,8},{8,9},{9,10},{10,1... | collective-permute-start | bytes 105992 | tf_op jit(solution)/shard_map/ppermute | solution.py:53
  42.9 19.7 %collective-permute-start.8 = (bf16[144,768]{1,0:T(8,128)(2,1)S(1)}, bf16[144,768]{1,0:T(8,128)(2,1)S(1)}, u32[]{:S(2)}, u32[]{:S(2)}) collective-permute-start(bf16[144,768]{1,0:T(8,128)(2,1)S(1)} %select_n.161), channel_id=1, source_target_pairs={{0,8},{1,9},{2,10},{3,11},{4,12},{5,13},{6,14},{7,15},{8,0},{9,1},... | collective-permute-start | bytes 663560 | tf_op jit(solution)/shard_map/ppermute | solution.py:40
  44.8 23.0 %collective-permute-start.28 = (bf16[144,768]{1,0:T(8,128)(2,1)}, bf16[144,768]{1,0:T(8,128)(2,1)S(1)}, u32[]{:S(2)}, u32[]{:S(2)}) collective-permute-start(bf16[144,768]{1,0:T(8,128)(2,1)} %select_n.174), channel_id=1, source_target_pairs={{0,12},{1,13},{2,14},{3,15},{4,0},{5,1},{6,2},{7,3},{8,4},{9,5},{1... | collective-permute-start | bytes 663560 | tf_op jit(solution)/shard_map/ppermute | solution.py:40
  47.9 202.0 %collective-permute-start.27 = (bf16[144,768]{1,0:T(8,128)(2,1)}, bf16[144,768]{1,0:T(8,128)(2,1)}, u32[]{:S(2)}, u32[]{:S(2)}) collective-permute-start(bf16[144,768]{1,0:T(8,128)(2,1)} %select_n.174), channel_id=1, source_target_pairs={{0,8},{1,9},{2,10},{3,11},{4,12},{5,13},{6,14},{7,15},{8,0},{9,1},... | collective-permute-start | bytes 663560 | tf_op jit(solution)/shard_map/ppermute | solution.py:40
  49.0 201.4 %collective-permute-start.26 = (bf16[144,768]{1,0:T(8,128)(2,1)}, bf16[144,768]{1,0:T(8,128)(2,1)}, u32[]{:S(2)}, u32[]{:S(2)}) collective-permute-start(bf16[144,768]{1,0:T(8,128)(2,1)} %select_n.174), channel_id=1, source_target_pairs={{0,4},{1,5},{2,6},{3,7},{4,8},{5,9},{6,10},{7,11},{8,12},{9,13},{1... | collective-permute-start | bytes 663560 | tf_op jit(solution)/shard_map/ppermute | solution.py:40
  63.8 188.1 %collective-permute-start.10 = (bf16[4,144,384]{2,1,0:T(8,128)(2,1)S(1)}, bf16[4,144,384]{2,1,0:T(8,128)(2,1)}, u32[]{:S(2)}, u32[]{:S(2)}) collective-permute-start(bf16[4,144,384]{2,1,0:T(8,128)(2,1)S(1)} %get-tuple-element.139.refs_0_), channel_id=1, source_target_pairs={{0,1},{1,0},{2,3},{3,2},{4,5},{5,4},{6,7},{7,6},{8,9},{9,8},{10,11... | collective-permute-start | bytes 1327112 | tf_op jit(solution)/shard_map/ppermute | solution.py:40
  66.3 186.1 %collective-permute-start.11 = (bf16[4,144,384]{2,1,0:T(8,128)(2,1)S(1)}, bf16[4,144,384]{2,1,0:T(8,128)(2,1)}, u32[]{:S(2)}, u32[]{:S(2)}) collective-permute-start(bf16[4,144,384]{2,1,0:T(8,128)(2,1)S(1)} %get-tuple-element.139.refs_0_), channel_id=1, source_target_pairs={{0,2},{1,3},{2,0},{3,1},{4,6},{5,7},{6,4},{7,5},{8,10},{9,11},{10,... | collective-permute-start | bytes 1327112 | tf_op jit(solution)/shard_map/ppermute | solution.py:40
  67.8 186.6 %collective-permute-start.13 = (bf16[4,144,384]{2,1,0:T(8,128)(2,1)S(1)}, bf16[4,144,384]{2,1,0:T(8,128)(2,1)}, u32[]{:S(2)}, u32[]{:S(2)}) collective-permute-start(bf16[4,144,384]{2,1,0:T(8,128)(2,1)S(1)} %get-tuple-element.138.refs_4_), channel_id=1, source_target_pairs={{0,1},{1,0},{2,3},{3,2},{4,5},{5,4},{6,7},{7,6},{8,9},{9,8},{10,11... | collective-permute-start | bytes 1327112 | tf_op jit(solution)/shard_map/ppermute | solution.py:40
  265.6 23.5 %collective-permute-start.12 = (bf16[4,144,384]{2,1,0:T(8,128)(2,1)}, bf16[4,144,384]{2,1,0:T(8,128)(2,1)}, u32[]{:S(2)}, u32[]{:S(2)}) collective-permute-start(bf16[4,144,384]{2,1,0:T(8,128)(2,1)} %collective-permute-done.10.refs_1_), channel_id=1, source_target_pairs={{0,2},{1,3},{2,0},{3,1},{4,6},{5,7},{6,4},{7,5},{8,10},{9,11},{10,... | collective-permute-start | bytes 1327112 | tf_op jit(solution)/shard_map/ppermute | solution.py:40
  267.2 22.5 %collective-permute-start.17 = (bf16[4,144,384]{2,1,0:T(8,128)(2,1)}, bf16[4,144,384]{2,1,0:T(8,128)(2,1)S(1)}, u32[]{:S(2)}, u32[]{:S(2)}) collective-permute-start(bf16[4,144,384]{2,1,0:T(8,128)(2,1)} %collective-permute-done.10.refs_1_), channel_id=1, source_target_pairs={{0,16},{16,0},{1,17},{17,1},{2,18},{18,2},{3,19},{19,3},{4,20},{20... | collective-permute-start | bytes 1327112 | tf_op jit(solution)/shard_map/ppermute | solution.py:44
  320.7 29.7 %collective-permute-start.25 = (bf16[2,196,12,64]{1,3,2,0:T(8,128)(2,1)}, bf16[2,196,12,64]{1,3,2,0:T(8,128)(2,1)}, u32[]{:S(2)}, u32[]{:S(2)}) collective-permute-start(bf16[2,196,12,64]{1,3,2,0:T(8,128)(2,1)} %copy.241), channel_id=1, source_target_pairs={{0,16},{16,0},{1,17},{17,1},{2,18},{18,2},{3,19},{19,3},{4,20},{20... | collective-permute-start | bytes 1806344 | tf_op jit(solution)/shard_map/ppermute | solution.py:196
  329.1 28.6 %collective-permute-start.24 = (bf16[2,196,12,64]{1,3,2,0:T(8,128)(2,1)S(1)}, bf16[2,196,12,64]{1,3,2,0:T(8,128)(2,1)}, u32[]{:S(2)}, u32[]{:S(2)}) collective-permute-start(bf16[2,196,12,64]{1,3,2,0:T(8,128)(2,1)S(1)} %copy.237), channel_id=1, source_target_pairs={{0,16},{16,0},{1,17},{17,1},{2,18},{18,2},{3,19},{19,3},{4,20},{20... | collective-permute-start | bytes 1806344 | tf_op jit(solution)/shard_map/ppermute | solution.py:196
  428.5 95.7 %collective-permute-start.44 = (bf16[2,196,12,64]{1,3,2,0:T(8,128)(2,1)}, bf16[2,196,12,64]{1,3,2,0:T(8,128)(2,1)}, u32[]{:S(2)}, u32[]{:S(2)}) collective-permute-start(bf16[2,196,12,64]{1,3,2,0:T(8,128)(2,1)} %slice.620), channel_id=1, source_target_pairs={{0,16},{16,0},{1,17},{17,1},{2,18},{18,2},{3,19},{19,3},{4,20},{20... | collective-permute-start | bytes 1806344 | tf_op jit(solution)/shard_map/ppermute | solution.py:196
  441.7 73.5 %collective-permute-start.43 = (bf16[2,196,12,64]{1,3,2,0:T(8,128)(2,1)}, bf16[2,196,12,64]{1,3,2,0:T(8,128)(2,1)}, u32[]{:S(2)}, u32[]{:S(2)}) collective-permute-start(bf16[2,196,12,64]{1,3,2,0:T(8,128)(2,1)} %slice.621), channel_id=1, source_target_pairs={{0,16},{16,0},{1,17},{17,1},{2,18},{18,2},{3,19},{19,3},{4,20},{20... | collective-permute-start | bytes 1806344 | tf_op jit(solution)/shard_map/ppermute | solution.py:196
  621.3 40.9 %collective-permute-start.53 = (bf16[2,2,2,4,144,384]{5,4,3,1,2,0:T(8,128)(2,1)}, bf16[2,2,2,4,144,384]{5,4,3,1,2,0:T(8,128)(2,1)}, u32[]{:S(2)}, u32[]{:S(2)}) collective-permute-start(bf16[2,2,2,4,144,384]{5,4,3,1,2,0:T(8,128)(2,1)} %copy_bitcast_fusion), channel_id=1, source_target_pairs={{0,16},{16,0},{1,17},{17,1},{2,18},{18,2},{3,19},{19,3},{4,20},{20... | collective-permute-start | bytes 10616840 | tf_op jit(solution)/shard_map/ppermute | solution.py:44
  645.3 22.0 %collective-permute-start.45 = (bf16[2,2,2,4,144,384]{5,4,3,2,1,0:T(8,128)(2,1)}, bf16[2,2,2,4,144,384]{5,4,3,2,1,0:T(8,128)(2,1)}, u32[]{:S(2)}, u32[]{:S(2)}) collective-permute-start(bf16[2,2,2,4,144,384]{5,4,3,2,1,0:T(8,128)(2,1)} %slice_bitcast_fusion), channel_id=1, source_target_pairs={{0,16},{16,0},{1,17},{17,1},{2,18},{18,2},{3,19},{19,3},{4,20},{20... | collective-permute-start | bytes 10616840 | tf_op jit(solution)/shard_map/ppermute | solution.py:44
  666.1 23.9 %collective-permute-start.56 = (bf16[2,4,144,384]{3,2,1,0:T(8,128)(2,1)S(1)}, bf16[2,4,144,384]{3,2,1,0:T(8,128)(2,1)S(1)}, u32[]{:S(2)}, u32[]{:S(2)}) collective-permute-start(bf16[2,4,144,384]{3,2,1,0:T(8,128)(2,1)S(1)} %get-tuple-element.126), channel_id=1, source_target_pairs={{0,2},{1,3},{2,0},{3,1},{4,6},{5,7},{6,4},{7,5},{8,10},{9,11},{10,... | collective-permute-start | bytes 2654216 | tf_op jit(solution)/shard_map/ppermute | solution.py:40
  666.9 23.7 %collective-permute-start.54 = (bf16[2,4,144,384]{3,2,1,0:T(8,128)(2,1)S(1)}, bf16[2,4,144,384]{3,2,1,0:T(8,128)(2,1)S(1)}, u32[]{:S(2)}, u32[]{:S(2)}) collective-permute-start(bf16[2,4,144,384]{3,2,1,0:T(8,128)(2,1)S(1)} %get-tuple-element.128), channel_id=1, source_target_pairs={{0,1},{1,0},{2,3},{3,2},{4,5},{5,4},{6,7},{7,6},{8,9},{9,8},{10,11... | collective-permute-start | bytes 2654216 | tf_op jit(solution)/shard_map/ppermute | solution.py:40
  670.5 37.2 %collective-permute-start.48 = (bf16[2,4,144,384]{3,2,1,0:T(8,128)(2,1)S(1)}, bf16[2,4,144,384]{3,2,1,0:T(8,128)(2,1)S(1)}, u32[]{:S(2)}, u32[]{:S(2)}) collective-permute-start(bf16[2,4,144,384]{3,2,1,0:T(8,128)(2,1)S(1)} %get-tuple-element.122), channel_id=1, source_target_pairs={{0,2},{1,3},{2,0},{3,1},{4,6},{5,7},{6,4},{7,5},{8,10},{9,11},{10,... | collective-permute-start | bytes 2654216 | tf_op jit(solution)/shard_map/ppermute | solution.py:40
  684.7 23.6 %collective-permute-start.46 = (bf16[2,4,144,384]{3,2,1,0:T(8,128)(2,1)S(1)}, bf16[2,4,144,384]{3,2,1,0:T(8,128)(2,1)S(1)}, u32[]{:S(2)}, u32[]{:S(2)}) collective-permute-start(bf16[2,4,144,384]{3,2,1,0:T(8,128)(2,1)S(1)} %get-tuple-element.124), channel_id=1, source_target_pairs={{0,1},{1,0},{2,3},{3,2},{4,5},{5,4},{6,7},{7,6},{8,9},{9,8},{10,11... | collective-permute-start | bytes 2654216 | tf_op jit(solution)/shard_map/ppermute | solution.py:40
  687.5 50.8 %collective-permute-start.65 = (f32[24,768]{1,0:T(8,128)S(1)}, f32[24,768]{1,0:T(8,128)S(1)}, u32[]{:S(2)}, u32[]{:S(2)}) collective-permute-start(f32[24,768]{1,0:T(8,128)S(1)} %add.475), channel_id=1, source_target_pairs={{0,4},{1,5},{2,6},{3,7},{4,0},{5,1},{6,2},{7,3},{8,12},{9,13},{10,... | collective-permute-start | bytes 221192 | tf_op jit(solution)/shard_map/ppermute | solution.py:40
  690.1 27.5 %collective-permute-start.57 = (bf16[4,144,384]{2,1,0:T(8,128)(2,1)S(1)}, bf16[4,144,384]{2,1,0:T(8,128)(2,1)S(1)}, u32[]{:S(2)}, u32[]{:S(2)}) collective-permute-start(bf16[4,144,384]{2,1,0:T(8,128)(2,1)S(1)} %fusion.62), channel_id=1, source_target_pairs={{0,1},{1,0},{2,3},{3,2},{4,5},{5,4},{6,7},{7,6},{8,9},{9,8},{10,11... | collective-permute-start | bytes 1327112 | tf_op jit(solution)/shard_map/ppermute | solution.py:40
  690.7 27.0 %collective-permute-start.55 = (bf16[4,144,384]{2,1,0:T(8,128)(2,1)S(1)}, bf16[4,144,384]{2,1,0:T(8,128)(2,1)S(1)}, u32[]{:S(2)}, u32[]{:S(2)}) collective-permute-start(bf16[4,144,384]{2,1,0:T(8,128)(2,1)S(1)} %fusion.61), channel_id=1, source_target_pairs={{0,2},{1,3},{2,0},{3,1},{4,6},{5,7},{6,4},{7,5},{8,10},{9,11},{10,... | collective-permute-start | bytes 1327112 | tf_op jit(solution)/shard_map/ppermute | solution.py:40
  707.8 24.4 %collective-permute-start.49 = (bf16[4,144,384]{2,1,0:T(8,128)(2,1)S(1)}, bf16[4,144,384]{2,1,0:T(8,128)(2,1)S(1)}, u32[]{:S(2)}, u32[]{:S(2)}) collective-permute-start(bf16[4,144,384]{2,1,0:T(8,128)(2,1)S(1)} %fusion.60), channel_id=1, source_target_pairs={{0,1},{1,0},{2,3},{3,2},{4,5},{5,4},{6,7},{7,6},{8,9},{9,8},{10,11... | collective-permute-start | bytes 1327112 | tf_op jit(solution)/shard_map/ppermute | solution.py:40
  708.4 28.8 %collective-permute-start.47 = (bf16[4,144,384]{2,1,0:T(8,128)(2,1)S(1)}, bf16[4,144,384]{2,1,0:T(8,128)(2,1)S(1)}, u32[]{:S(2)}, u32[]{:S(2)}) collective-permute-start(bf16[4,144,384]{2,1,0:T(8,128)(2,1)S(1)} %fusion.59), channel_id=1, source_target_pairs={{0,2},{1,3},{2,0},{3,1},{4,6},{5,7},{6,4},{7,5},{8,10},{9,11},{10,... | collective-permute-start | bytes 1327112 | tf_op jit(solution)/shard_map/ppermute | solution.py:40
  718.9 22.4 %collective-permute-start.60 = (bf16[144,768]{1,0:T(8,128)(2,1)S(1)}, bf16[144,768]{1,0:T(8,128)(2,1)}, u32[]{:S(2)}, u32[]{:S(2)}) collective-permute-start(bf16[144,768]{1,0:T(8,128)(2,1)S(1)} %get-tuple-element.134), channel_id=1, source_target_pairs={{0,12},{1,13},{2,14},{3,15},{4,0},{5,1},{6,2},{7,3},{8,4},{9,5},{1... | collective-permute-start | bytes 663560 | tf_op jit(solution)/shard_map/ppermute | solution.py:40
  720.3 40.5 %collective-permute-start.59 = (bf16[144,768]{1,0:T(8,128)(2,1)}, bf16[144,768]{1,0:T(8,128)(2,1)}, u32[]{:S(2)}, u32[]{:S(2)}) collective-permute-start(bf16[144,768]{1,0:T(8,128)(2,1)} %get-tuple-element.135), channel_id=1, source_target_pairs={{0,8},{1,9},{2,10},{3,11},{4,12},{5,13},{6,14},{7,15},{8,0},{9,1},... | collective-permute-start | bytes 663560 | tf_op jit(solution)/shard_map/ppermute | solution.py:40
  732.2 28.6 %collective-permute-start.58 = (bf16[144,768]{1,0:T(8,128)(2,1)}, bf16[144,768]{1,0:T(8,128)(2,1)}, u32[]{:S(2)}, u32[]{:S(2)}) collective-permute-start(bf16[144,768]{1,0:T(8,128)(2,1)} %get-tuple-element.133), channel_id=1, source_target_pairs={{0,4},{1,5},{2,6},{3,7},{4,8},{5,9},{6,10},{7,11},{8,12},{9,13},{1... | collective-permute-start | bytes 663560 | tf_op jit(solution)/shard_map/ppermute | solution.py:40
  738.3 22.5 %collective-permute-start.52 = (bf16[144,768]{1,0:T(8,128)(2,1)}, bf16[144,768]{1,0:T(8,128)(2,1)}, u32[]{:S(2)}, u32[]{:S(2)}) collective-permute-start(bf16[144,768]{1,0:T(8,128)(2,1)} %get-tuple-element.131), channel_id=1, source_target_pairs={{0,12},{1,13},{2,14},{3,15},{4,0},{5,1},{6,2},{7,3},{8,4},{9,5},{1... | collective-permute-start | bytes 663560 | tf_op jit(solution)/shard_map/ppermute | solution.py:40
  738.3 28.7 %collective-permute-start.51 = (bf16[144,768]{1,0:T(8,128)(2,1)}, bf16[144,768]{1,0:T(8,128)(2,1)}, u32[]{:S(2)}, u32[]{:S(2)}) collective-permute-start(bf16[144,768]{1,0:T(8,128)(2,1)} %get-tuple-element.132), channel_id=1, source_target_pairs={{0,8},{1,9},{2,10},{3,11},{4,12},{5,13},{6,14},{7,15},{8,0},{9,1},... | collective-permute-start | bytes 663560 | tf_op jit(solution)/shard_map/ppermute | solution.py:40
  741.3 25.7 %collective-permute-start.50 = (bf16[144,768]{1,0:T(8,128)(2,1)}, bf16[144,768]{1,0:T(8,128)(2,1)}, u32[]{:S(2)}, u32[]{:S(2)}) collective-permute-start(bf16[144,768]{1,0:T(8,128)(2,1)} %get-tuple-element.130), channel_id=1, source_target_pairs={{0,4},{1,5},{2,6},{3,7},{4,8},{5,9},{6,10},{7,11},{8,12},{9,13},{1... | collective-permute-start | bytes 663560 | tf_op jit(solution)/shard_map/ppermute | solution.py:40
  (131 other events, 2592.9 us)

commit v2 on v1

v2 whole, which is shorter than its diff:
```python
import functools
import jax
import jax.numpy as jnp
from jax import lax
from jax.experimental import pallas as pl
from jax.experimental.pallas import tpu as pltpu
from jax.sharding import PartitionSpec as P

D = 768
H = 12
HD = 64
FF = 3072
NB = 63
P_SIZE = 196
STEP = 5


HALF = D // 2
BLOCK = 144
PHASE_ROWS = 32 * BLOCK
BF = jnp.bfloat16
F32 = jnp.float32
DP = 16
EDGE = 17664
PAD = 208
KEYS = 512
HALF_KEYS = KEYS // 2
PAIR = 2 * HD


def x_swap():
    return [(i, i ^ 1) for i in range(DP)]


def y_swap():
    return [(i, i ^ 2) for i in range(DP)]


def z_turn(step):
    return [(i, (i // 4 + step) % 4 * 4 + i % 4) for i in range(DP)]


def send_dp(block, route):
    return lax.ppermute(block, "dp", route)


def send_mod(block):
    return lax.ppermute(block, "mod", [(0, 1), (1, 0)])


def pack_shard(own, side, place):
    lead = 8832 * side + 552 * place
    count = BLOCK * D
    lent = lax.dynamic_slice(own, (count - lead,), (count,))
    given = send_mod(lent)
    nxt = [(i, i + 1) for i in range(2 * DP - 1)]
    edge = lax.ppermute(own[own.shape[0] - EDGE :], ("mod", "dp"), nxt)
    kept = lax.dynamic_slice(jnp.concatenate([edge, own[:count]]), (EDGE - lead,), (count,))
    kept = kept.reshape(BLOCK, D)
    given = given.reshape(BLOCK, D)
    return jnp.where(side == 0, kept, given), jnp.where(side == 0, given, kept)


def unpack_shard(first, second, vec, side, place):
    lead = 8832 * side + 552 * place
    even = jnp.where(side == 0, first, second).reshape(-1)
    lent = jnp.where(side == 0, second, first)
    odd = send_mod(lent).reshape(-1)
    back = [(i + 1, i) for i in range(2 * DP - 1)]
    edge = lax.ppermute(even[:EDGE], ("mod", "dp"), back)
    is_last = jnp.logical_and(side == 1, place == DP - 1)
    edge = jnp.where(is_last, vec.reshape(-1)[:EDGE], edge)
    return lax.dynamic_slice(jnp.concatenate([even, odd, edge]), (lead,), (221736,))


def sum_all_small(part):
    for route in (x_swap(), y_swap(), z_turn(2)):
        part = part + send_dp(part, route)
    part = part + send_dp(part, [(i, i ^ 4) for i in range(DP)])
    return part + send_mod(part)


def gather_phase(block):
    stack = jnp.stack([block] + [send_dp(block, z_turn(step)) for step in (1, 2, 3)])
    left, right = stack[:, :, :HALF], stack[:, :, HALF:]
    left_x = send_dp(left, x_swap())
    right_y = send_dp(right, y_swap())
    left_y = send_dp(left, y_swap())
    right_x = send_dp(right, x_swap())
    left_xy = send_dp(left_x, y_swap())
    right_xy = send_dp(right_y, x_swap())
    mine = [left, left_x, left_y, left_xy, right, right_x, right_y, right_xy]
    return mine + [send_mod(piece) for piece in mine]


def coords():
    side = lax.axis_index("mod")
    place = lax.axis_index("dp")
    return jnp.stack([side, place // 4, place // 2 % 2, place % 2]).astype(jnp.int32)


def assemble_body(phase, spot, *refs):
    pieces, out, sem = refs[:16], refs[16], refs[17]
    side, z, y, x = spot[0], spot[1], spot[2], spot[3]
    copies = []
    for index in range(16):
        other, half, yr, xr = index // 8, index // 4 % 2, index // 2 % 2, index % 2
        owner = side ^ other
        parity = owner if phase == 0 else 1 - owner
        for turn in range(4):
            home = ((z - turn) & 3) * 4 + (y ^ yr) * 2 + (x ^ xr)
            copies.append(
                pltpu.make_async_copy(
                    pieces[index].at[turn],
                    out.at[home * 2 + parity, :, pl.ds(half * HALF, HALF)],
                    sem.at[index * 4 + turn],
                )
            )
    for copy in copies:
        copy.start()
    for copy in copies:
        copy.wait()


def assemble(phase, spot, pieces):
    return pl.pallas_call(
        functools.partial(assemble_body, phase),
        out_shape=jax.ShapeDtypeStruct((32, BLOCK, D), BF),
        in_specs=[pl.BlockSpec(memory_space=pltpu.SMEM)] + [pl.BlockSpec(memory_space=pl.ANY)] * 16,
        out_specs=pl.BlockSpec(memory_space=pltpu.VMEM),
        scratch_shapes=[pltpu.SemaphoreType.DMA((64,))],
        name="assemble",
    )(spot, *pieces).reshape(PHASE_ROWS, D)


def scatter_body(phase, pieces, spot, *refs):
    sources, out, sem = refs[:-2], refs[-2], refs[-1]
    side, z, y, x = spot[0], spot[1], spot[2], spot[3]
    copies = []
    for block in range(32):
        home, parity = block // 2, block % 2
        owner = parity if phase == 0 else 1 - parity
        other = side ^ owner
        turn = (home // 4 - z) & 3
        yr = (home // 2 % 2) ^ y
        xr = (home % 2) ^ x
        for index, source_row, block_row, count in pieces[block]:
            for half in range(2):
                copies.append(
                    pltpu.make_async_copy(
                        sources[index].at[pl.ds(source_row, count), pl.ds(half * HALF, HALF)],
                        out.at[other, half, yr, xr, turn, pl.ds(block_row, count), :],
                        sem.at[len(copies)],
                    )
                )
    for copy in copies:
        copy.start()
    for copy in copies:
        copy.wait()


def scatter(phase, spot, tables):
    starts = [0]
    for table in tables:
        starts.append(starts[-1] + table.shape[0])
    pieces = []
    for block in range(32):
        low = phase * PHASE_ROWS + block * BLOCK
        parts = []
        for index in range(len(tables)):
            first, last = max(low, starts[index]), min(low + BLOCK, starts[index + 1])
            if first < last:
                parts.append((index, first - starts[index], first - low, last - first))
        pieces.append(parts)
    used = sorted({part[0] for parts in pieces for part in parts})
    pieces = [[(used.index(part[0]),) + part[1:] for part in parts] for parts in pieces]
    count = 2 * sum(len(parts) for parts in pieces)
    return pl.pallas_call(
        functools.partial(scatter_body, phase, pieces),
        out_shape=jax.ShapeDtypeStruct((2, 2, 2, 2, 4, BLOCK, HALF), BF),
        in_specs=[pl.BlockSpec(memory_space=pltpu.SMEM)]
        + [pl.BlockSpec(memory_space=pl.ANY)] * len(used),
        out_specs=pl.BlockSpec(memory_space=pl.ANY),
        scratch_shapes=[pltpu.SemaphoreType.DMA((count,))],
        name="scatter",
    )(spot, *[tables[index] for index in used])


def plus(left, right):
    return (left.astype(F32) + right.astype(F32)).astype(BF)


def reduce_phase(parts):
    theirs = send_mod(parts[1])
    left_out = send_dp(plus(parts[0, 0, :, 1], theirs[0, :, 1]), x_swap())
    right_out = send_dp(plus(parts[0, 1, 1], theirs[1, 1]), y_swap())
    left_in = plus(parts[0, 0, :, 0], theirs[0, :, 0])
    right_in = plus(parts[0, 1, 0], theirs[1, 0])
    left_next = send_dp(plus(left_in[1], left_out[1]), y_swap())
    right_next = send_dp(plus(right_in[1], right_out[1]), x_swap())
    left = left_in[0].astype(F32) + left_out[0].astype(F32) + left_next.astype(F32)
    right = right_in[0].astype(F32) + right_out[0].astype(F32) + right_next.astype(F32)
    both = jnp.concatenate([left, right], axis=-1)
    low = both.astype(BF)
    total = both[0]
    for step in (1, 2, 3):
        total = total + send_dp(low[step], z_turn(step)).astype(F32)
    return total


def dot_f32(left, right, dims):
    return lax.dot_general(left, right, (dims, ((), ())), preferred_element_type=F32)


NN = ((1,), (0,))
NT = ((1,), (1,))
TN = ((0,), (0,))


def bias_of(table_ref, ids_ref, head):
    entry = jnp.broadcast_to(table_ref[pl.ds(head, 1), :], (PAD, 128))
    return [
        jnp.take_along_axis(
            entry, ids_ref[:, c * 128 : (c + 1) * 128], axis=1, mode="promise_in_bounds"
        )
        for c in range(KEYS // 128)
    ]


def joint_keys(own_ref, other_ref, seq):
    rows = pl.ds(seq * PAD, PAD)
    gap = jnp.zeros((HALF_KEYS - PAD, PAIR), BF)
    return jnp.concatenate([own_ref[rows, :], gap, other_ref[rows, :], gap], axis=0)


def key_mask(counts_ref, seq):
    lane = lax.broadcasted_iota(jnp.int32, (1, KEYS), 1)
    own, other = counts_ref[seq], counts_ref[2 + seq]
    return jnp.logical_or(
        lane < own, jnp.logical_and(lane >= HALF_KEYS, lane < HALF_KEYS + other)
    )


def half_only(values, part):
    lane = lax.broadcasted_iota(jnp.int32, values.shape, 1)
    keep = lane < HD if part == 0 else lane >= HD
    return jnp.where(keep, values, jnp.zeros((), values.dtype))


def attend_body(counts, ids, table, query, key_own, key_other, value_own, value_other, out, logs):
    pair = pl.program_id(0)
    keys = [joint_keys(key_own, key_other, seq) for seq in range(2)]
    values = [joint_keys(value_own, value_other, seq) for seq in range(2)]
    masks = [key_mask(counts, seq) for seq in range(2)]
    lane = lax.broadcasted_iota(jnp.int32, (PAD, 128), 1)
    done = [None, None]
    for part in range(2):
        head = 2 * pair + part
        bias = jnp.concatenate(bias_of(table, ids, head), axis=1)
        for seq in range(2):
            rows = pl.ds(seq * PAD, PAD)
            scores = dot_f32(half_only(query[rows, :], part), keys[seq], NT) * 0.125 + bias
            scores = jnp.where(masks[seq], scores, -1e30)
            top = jnp.max(scores, axis=1, keepdims=True)
            powers = jnp.exp(scores - top)
            total = jnp.sum(powers, axis=1, keepdims=True)
            probs = (powers * (1.0 / total)).astype(BF)
            got = dot_f32(probs, values[seq], NN)
            done[seq] = got if part == 0 else jnp.where(lane < HD, done[seq], got)
            logs[rows, :] = jnp.where(lane == head, top + jnp.log(total), logs[rows, :])
    for seq in range(2):
        out[pl.ds(seq * PAD, PAD), :] = done[seq]


def fixed(shape):
    return pl.BlockSpec(shape, lambda i: (0,) * len(shape))


def by_pair():
    return pl.BlockSpec((2 * PAD, PAIR), lambda i: (0, i))


def attend(counts, ids, table, query, key_own, key_other, value_own, value_other):
    return pl.pallas_call(
        attend_body,
        grid=(H // 2,),
        out_shape=(
            jax.ShapeDtypeStruct((2 * PAD, D), F32),
            jax.ShapeDtypeStruct((2 * PAD, 128), F32),
        ),
        in_specs=[pl.BlockSpec(memory_space=pltpu.SMEM), fixed((PAD, KEYS)), fixed((16, 128))]
        + [by_pair()] * 5,
        out_specs=(by_pair(), fixed((2 * PAD, 128))),
        name="attend",
    )(counts, ids, table, query, key_own, key_other, value_own, value_other)


def attend_back_body(
    counts, ids, table, logs, query, key_own, key_other, value_own, value_other, grad,
    grad_query, grad_key_own, grad_value_own, grad_key_other, grad_value_other, terms,
):
    pair = pl.program_id(0)
    keys = [joint_keys(key_own, key_other, seq) for seq in range(2)]
    values = [joint_keys(value_own, value_other, seq) for seq in range(2)]
    masks = [key_mask(counts, seq) for seq in range(2)]
    lane = lax.broadcasted_iota(jnp.int32, (PAD, 128), 1)
    to_query, to_key, to_value = [0.0, 0.0], [0.0, 0.0], [0.0, 0.0]
    for part in range(2):
        head = 2 * pair + part
        bias = jnp.concatenate(bias_of(table, ids, head), axis=1)
        both = 0.0
        for seq in range(2):
            rows = pl.ds(seq * PAD, PAD)
            asked = half_only(query[rows, :], part)
            into = half_only(grad[rows, :], part)
            scores = dot_f32(asked, keys[seq], NT) * 0.125 + bias
            scores = jnp.where(masks[seq], scores, -1e30)
            log = jnp.sum(jnp.where(lane == head, logs[rows, :], 0.0), axis=1, keepdims=True)
            probs = jnp.exp(scores - log)
            grad_probs = dot_f32(into, values[seq], NT)
            mean = jnp.sum(probs * grad_probs, axis=1, keepdims=True)
            grad_scores = (probs * (grad_probs - mean)).astype(BF)
            both = both + grad_scores.astype(F32)
            to_value[seq] = to_value[seq] + dot_f32(probs.astype(BF), into, TN)
            to_query[seq] = to_query[seq] + dot_f32(grad_scores, half_only(keys[seq], part), NN)
            to_key[seq] = to_key[seq] + dot_f32(grad_scores, asked, TN)
        for c in range(KEYS // 128):
            terms[c, pl.ds(head, PAD, stride=16), :] = both[:, c * 128 : (c + 1) * 128]
    for seq in range(2):
        rows = pl.ds(seq * PAD, PAD)
        grad_query[rows, :] = (to_query[seq] * 0.125).astype(BF)
        grad_key_own[rows, :] = to_key[seq][:PAD] * 0.125
        grad_key_other[rows, :] = (to_key[seq][HALF_KEYS : HALF_KEYS + PAD] * 0.125).astype(BF)
        grad_value_own[rows, :] = to_value[seq][:PAD]
        grad_value_other[rows, :] = to_value[seq][HALF_KEYS : HALF_KEYS + PAD].astype(BF)


def attend_back(counts, ids, table, logs, query, keys, values, grad):
    def rows_of(kind):
        return jax.ShapeDtypeStruct((2 * PAD, D), kind)

    return pl.pallas_call(
        attend_back_body,
        grid=(H // 2,),
        out_shape=(
            rows_of(BF),
            rows_of(F32),
            rows_of(F32),
            rows_of(BF),
            rows_of(BF),
            jax.ShapeDtypeStruct((KEYS // 128, PAD * 16, 128), F32),
        ),
        in_specs=[
            pl.BlockSpec(memory_space=pltpu.SMEM),
            fixed((PAD, KEYS)),
            fixed((16, 128)),
            fixed((2 * PAD, 128)),
        ]
        + [by_pair()] * 6,
        out_specs=(by_pair(),) * 5 + (fixed((KEYS // 128, PAD * 16, 128)),),
        name="attend_back",
    )(counts, ids, table, logs, query, *keys, *values, grad)


GROUP = 4


def table_body(ids, terms, out):
    bucket = lax.broadcasted_iota(jnp.int32, (NB + 1, KEYS), 0)

    def step(index, totals):
        fresh = []
        for lane_group in range(GROUP):
            row = index * GROUP + lane_group
            hot = jnp.where(ids[pl.ds(row, 1), :] == bucket, 1.0, 0.0).astype(BF)
            start = pl.multiple_of(row * 16, 16)
            term = jnp.concatenate(
                [terms[c, pl.ds(start, 16), :] for c in range(KEYS // 128)], axis=1
            )
            high = term.astype(BF)
            low = (term - high.astype(F32)).astype(BF)
            both = jnp.concatenate([high, low], axis=0)
            fresh.append(totals[lane_group] + dot_f32(hot, both, NT))
        return tuple(fresh)

    zero = jnp.zeros((NB + 1, 32), F32)
    totals = lax.fori_loop(0, P_SIZE // GROUP, step, (zero,) * GROUP)
    total = totals[0] + totals[1] + totals[2] + totals[3]
    out[...] = total


def table_grad(ids, terms):
    whole = pl.BlockSpec(memory_space=pltpu.VMEM)
    both = pl.pallas_call(
        table_body,
        out_shape=jax.ShapeDtypeStruct((NB + 1, 32), F32),
        in_specs=[whole, whole],
        out_specs=whole,
        name="table_grad",
    )(ids, terms)
    return both[:NB, :H] + both[:NB, 16 : 16 + H]


def from_partner(block, axis, bit):
    count = lax.axis_size(axis)
    route = []
    for low in range(count):
        high = low | 1 << bit
        if high != low and high < count:
            route += [(low, high), (high, low)]
    return lax.ppermute(block, axis, route)


def layer_norm(values, gain, shift):
    center = values - jnp.mean(values, axis=-1, keepdims=True)
    spread = jnp.mean(center * center, axis=-1, keepdims=True)
    return center * lax.rsqrt(spread + 1e-05) * gain + shift


def norm_back(values, gain, shift, grad_after):
    _, pullback = jax.vjp(layer_norm, values, gain, shift)
    return pullback(grad_after)


def matmul(left, right):
    return jnp.dot(left, right, preferred_element_type=jnp.float32)


def matmul_tn(left, right):
    return lax.dot_general(
        left, right, (((0,), (0,)), ((), ())), preferred_element_type=jnp.float32
    )


def matmul_nt(left, right):
    return lax.dot_general(
        left, right, (((1,), (1,)), ((), ())), preferred_element_type=jnp.float32
    )


def exact_gelu(values):
    return jax.nn.gelu(values, approximate=False)


def unpack(flat):
    pairs = [(D, D), (D, D), (D, D), (D, D), (D, FF), (FF, D), (10, D), (3, FF), (NB + 1, H)]
    pieces = []
    offset = 0
    for dims_pair in pairs:
        extent = dims_pair[0] * dims_pair[1]
        pieces.append(flat[offset : offset + extent].reshape(dims_pair))
        offset += extent
    return pieces


def unpack_tables(first, second, vec):
    square = [first[i * D : (i + 1) * D] for i in range(4)]
    cut = PHASE_ROWS - 4 * D
    w_inner = jnp.concatenate(
        [first[4 * D :].reshape(cut // 4, FF), second[: FF - cut].reshape(D - cut // 4, FF)]
    )
    return square + [
        w_inner,
        second[FF - cut :],
        vec[:10],
        vec[10:22].reshape(3, FF),
        vec[22].reshape(NB + 1, H),
    ]


def widen(values):
    return jnp.pad(values, ((0, 0), (0, PAD - P_SIZE), (0, 0))).reshape(2 * PAD, D)


def narrow(values):
    return values.reshape(1, 2, PAD, D)[:, :, :P_SIZE]


def on_device(rows, cotangent, master, first_moment, second_moment, average, lengths, buckets):
    side = lax.axis_index("mod")
    place = lax.axis_index("dp")
    fast = lax.axis_size("dp") == DP
    own_copy = master.astype(jnp.bfloat16)
    if fast:
        spot = coords()
        first, second = pack_shard(own_copy, side, place)
        is_last = jnp.logical_and(side == 1, place == DP - 1)
        vec = jnp.where(is_last, own_copy[-EDGE:], jnp.zeros((), BF))
        vec = jnp.pad(vec, (0, D)).reshape(24, D)
        weights = unpack_tables(
            assemble(0, spot, gather_phase(first)),
            assemble(1, spot, gather_phase(second)),
            sum_all_small(vec),
        )
    else:
        weights = unpack(lax.all_gather(own_copy, ("mod", "dp"), axis=0, tiled=True))
    w_query, w_key, w_value, w_out, w_inner, w_outer, vec_model, vec_inner, head_table = weights
    model_vec = vec_model.astype(jnp.float32)
    inner_vec = vec_inner.astype(jnp.float32)
    head_vals = head_table.astype(jnp.float32)
    scale_row = jnp.repeat(head_vals[NB], HD)
    table = jnp.pad(head_vals.T, ((0, 16 - H), (0, 128 - NB - 1)))
    full = jnp.full_like(lengths, P_SIZE)
    own_count = jnp.where(side == 0, full, lengths)
    other_count = jnp.where(side == 0, lengths, full)
    counts = jnp.concatenate([own_count, other_count]).astype(jnp.int32)
    slots = jnp.arange(PAD, dtype=jnp.int32)
    own_valid = (slots[None, :] < own_count[:, None]).astype(F32).reshape(2 * PAD, 1)
    near = lax.dynamic_slice(buckets, (side * P_SIZE, side * P_SIZE), (P_SIZE, P_SIZE))
    far = lax.dynamic_slice(buckets, (side * P_SIZE, (1 - side) * P_SIZE), (P_SIZE, P_SIZE))
    room = ((0, PAD - P_SIZE), (0, HALF_KEYS - P_SIZE))
    ids = jnp.concatenate([jnp.pad(near, room), jnp.pad(far, room)], axis=1)

    inputs = widen(rows[0]).astype(F32)
    normed = layer_norm(inputs, model_vec[0], model_vec[1])
    normed_low = normed.astype(BF)
    keys_own = matmul(normed_low, w_key).astype(BF)
    values_own = (matmul(normed_low, w_value) + model_vec[3]).astype(BF)
    keys_other, values_other = from_partner((keys_own, values_own), "mod", 0)
    query = (matmul(normed_low, w_query) + model_vec[2]).astype(BF)
    keys_both, values_both = (keys_own, keys_other), (values_own, values_other)
    attended, logs = attend(counts, ids, table, query, *keys_both, *values_both)

    scaled = attended * scale_row
    mixed = layer_norm(scaled, model_vec[4], model_vec[5])
    mixed_low = mixed.astype(BF)
    middle = inputs + (matmul(mixed_low, w_out) + model_vec[6])
    normed_two = layer_norm(middle, model_vec[7], model_vec[8])
    normed_two_low = normed_two.astype(BF)
    inner = matmul(normed_two_low, w_inner) + inner_vec[0]
    activated = exact_gelu(inner)
    inner_normed = layer_norm(activated, inner_vec[1], inner_vec[2])
    inner_low = inner_normed.astype(BF)
    result = middle + (matmul(inner_low, w_outer) + model_vec[9])
    result_rows = narrow(result.astype(BF))

    tokens_all = 2 * rows.shape[1] * P_SIZE * lax.axis_size("dp")
    share = 1.0 / tokens_all

    def weight_grad(left, right):
        value = matmul_tn(left, right) * share
        return value.astype(BF) if fast else value

    grad_out = widen(cotangent[0]).astype(F32) * own_valid
    grad_branch = grad_out.astype(BF)
    grad_w_outer = weight_grad(inner_low, grad_branch)
    grad_b_outer = jnp.sum(grad_branch.astype(F32), axis=0)
    grad_inner_normed = matmul_nt(grad_branch, w_outer)
    grad_activated, grad_gain_ff, grad_shift_ff = norm_back(
        activated, inner_vec[1], inner_vec[2], grad_inner_normed
    )
    _, gelu_pull = jax.vjp(exact_gelu, inner)
    grad_inner_low = gelu_pull(grad_activated)[0].astype(BF)
    grad_w_inner = weight_grad(normed_two_low, grad_inner_low)
    grad_b_inner = jnp.sum(grad_inner_low.astype(F32), axis=0)
    grad_normed_two = matmul_nt(grad_inner_low, w_inner)
    grad_mid_part, grad_gain_two, grad_shift_two = norm_back(
        middle, model_vec[7], model_vec[8], grad_normed_two
    )
    grad_middle = grad_out + grad_mid_part
    grad_attn_low = grad_middle.astype(BF)
    grad_w_out = weight_grad(mixed_low, grad_attn_low)
    grad_b_out = jnp.sum(grad_attn_low.astype(F32), axis=0)
    grad_mixed = matmul_nt(grad_attn_low, w_out)
    grad_scaled, grad_gain_attn, grad_shift_attn = norm_back(
        scaled, model_vec[4], model_vec[5], grad_mixed
    )
    grad_head_scale = jnp.sum(jnp.sum(grad_scaled * attended, axis=0).reshape(H, HD), axis=1)
    grad_attended = (grad_scaled * scale_row).astype(BF)
    grad_query, key_kept, value_kept, key_sent, value_sent, terms = attend_back(
        counts, ids, table, logs, query, keys_both, values_both, grad_attended
    )
    back_keys, back_values = from_partner((key_sent, value_sent), "mod", 0)
    grad_key = (key_kept + back_keys.astype(F32)).astype(BF)
    grad_value = (value_kept + back_values.astype(F32)).astype(BF)
    grad_table = table_grad(ids, terms)
    grad_w_query = weight_grad(normed_low, grad_query)
    grad_w_key = weight_grad(normed_low, grad_key)
    grad_w_value = weight_grad(normed_low, grad_value)
    grad_b_query = jnp.sum(grad_query.astype(F32), axis=0)
    grad_b_value = jnp.sum(grad_value.astype(F32), axis=0)
    grad_normed = (
        matmul_nt(grad_query, w_query) + matmul_nt(grad_key, w_key) + matmul_nt(grad_value, w_value)
    )
    grad_in_part, grad_gain_one, grad_shift_one = norm_back(
        inputs, model_vec[0], model_vec[1], grad_normed
    )
    grad_rows = narrow(grad_middle + grad_in_part)
    grad_model_vec = jnp.stack(
        [
            grad_gain_one,
            grad_shift_one,
            grad_b_query,
            grad_b_value,
            grad_gain_attn,
            grad_shift_attn,
            grad_b_out,
            grad_gain_two,
            grad_shift_two,
            grad_b_outer,
        ]
    )
    grad_inner_vec = jnp.stack([grad_b_inner, grad_gain_ff, grad_shift_ff])
    grad_heads = jnp.concatenate([grad_table, grad_head_scale[None, :]], axis=0)
    vec_grad = (
        jnp.concatenate(
            [grad_model_vec, grad_inner_vec.reshape(12, D), grad_heads.reshape(1, D)], axis=0
        )
        * share
    )
    matrices = [grad_w_query, grad_w_key, grad_w_value, grad_w_out]
    matrices += [grad_w_inner.reshape(FF, D), grad_w_outer]
    if fast:
        second = reduce_phase(scatter(1, spot, matrices))
        first = reduce_phase(scatter(0, spot, matrices))
        vec_grad = sum_all_small(jnp.pad(vec_grad, ((0, 1), (0, 0))))
        square = jnp.sum(first * first) + jnp.sum(second * second)
        square = square + jnp.where(is_last, jnp.sum(vec_grad * vec_grad), 0.0)
        square_sum = sum_all_small(jnp.full((8, 128), square))[0, 0]
        grad_shard = unpack_shard(first, second, vec_grad, side, place)
    else:
        local_grad = jnp.concatenate([part.reshape(-1) for part in matrices + [vec_grad]])
        half_size = local_grad.shape[0] // 2
        own_half = lax.dynamic_slice_in_dim(local_grad, side * half_size, half_size)
        other_half = lax.dynamic_slice_in_dim(local_grad, (1 - side) * half_size, half_size)
        partner_half = from_partner(other_half.astype(BF), "mod", 0).astype(F32)
        grad_shard = lax.psum_scatter(own_half + partner_half, "dp", scatter_dimension=0, tiled=True)
        square_sum = lax.psum(jnp.sum(grad_shard * grad_shard), ("mod", "dp"))
    grad_norm = jnp.sqrt(square_sum)
    clip_scale = jnp.minimum(1.0, 0.25 / (grad_norm + 1e-06))
    clipped = grad_shard * clip_scale
    new_first = 0.5 * first_moment + 0.5 * clipped
    new_second = 0.6 * second_moment + 0.4 * clipped * clipped
    direction = new_first / (1.0 - 0.5**STEP) / (jnp.sqrt(new_second / (1.0 - 0.6**STEP)) + 1e-08)
    new_master = master - 0.04 * (direction + 0.01 * master)
    new_average = 0.5 * average + 0.5 * new_master
    return (
        result_rows,
        grad_rows,
        grad_norm,
        new_master,
        new_first,
        new_second,
        new_average,
        new_master.astype(jnp.bfloat16),
    )


def solution(mesh):
    placed = (
        P("mod", "dp", None, None),
        P("mod", "dp", None, None),
        P(("mod", "dp")),
        P(("mod", "dp")),
        P(("mod", "dp")),
        P(("mod", "dp")),
        P("dp"),
        P(),
    )
    return jax.shard_map(
        on_device,
        mesh=mesh,
        in_specs=placed,
        out_specs=(
            P("mod", "dp", None, None),
            P("mod", "dp", None, None),
            P(),
            P(("mod", "dp")),
            P(("mod", "dp")),
            P(("mod", "dp")),
            P(("mod", "dp")),
            P(("mod", "dp")),
        ),
        check_vma=False,
    )
```

time: 840 us -> 890 us (1.060)
  Pallas kernels: 27.5 us -> 498 us
  local copies, waits for them, and re-layouts: 374 us -> 58.1 us
  matrix products: 112 us -> 70.2 us
  blocking collectives: 39.5 us -> 0 us
  waiting for transfers between devices: 81.9 us -> 118 us
  other arithmetic: 88.3 us -> 60.6 us
  starting transfers between devices: 96.6 us -> 72.3 us
    pallas_call x2 -> x5, Pallas kernels: 13 us -> 484 us  [the longest x2 434 us: scatter(): pl.pallas_call(functools.partial(scatter_body, phase, pieces), out_shape=...]
    gather x2 -> x0, local copies, waits for them, and re-layouts: 182 us -> none  [on_device(): rel_bias = jnp.take(head_vals[:NB], block_ids, axis=0).transpose(2, 0, 1)]
    reshape x27 -> x6, local copies, waits for them, and re-layouts: 102 us -> 18.6 us  [the longest x1 8.65 us: on_device(): matrices += [grad_w_inner.reshape(FF, D), grad_w_outer]]
    ppermute x40 -> x44, waiting for transfers between devices: 78.2 us -> 118 us  [send_dp(): return lax.ppermute(block, 'dp', route)]
    psum x1 -> x0, blocking collectives: 39.5 us -> none  [on_device(): square_sum = lax.psum(jnp.sum(grad_shard * grad_shard), ('mod', 'dp'))]
    unnamed x202 -> x108, local copies, waits for them, and re-layouts: 45.5 us -> 8.87 us
    dot_general x7 -> x0, matrix products: 35.2 us -> none  [the longest x1 11.6 us: on_device(): jnp.einsum('pb,hp->bh', bucket_hot, bias_terms, precision=lax.Precision.H...]
    ppermute x40 -> x44, starting transfers between devices: 87.5 us -> 59.6 us  [send_dp(): return lax.ppermute(block, 'dp', route)]
  transfers between devices with their start and end apart: 68 -> 73, of which waited for: 16 -> 23; matrix products, arithmetic and copies ran while one was open for 49% -> 15% of each run, Pallas kernels for 3% -> 52%
where the time goes in v2:
time: 890 us; the launch traced here: 884 us
  Pallas kernels  498 us (56%)
  waiting for transfers between devices  118 us (13%)
  starting transfers between devices  72.3 us (8%)
  matrix products  70.2 us (8%)
  other arithmetic  60.6 us (7%)
  local copies, waits for them, and re-layouts  58.1 us (7%)
    pallas_call x2, Pallas kernels, scatter(): pl.pallas_call(functools.partial(scatter_body, phase, pieces), out_shape=...  434 us
    ppermute x44, waiting for transfers between devices, send_dp(): return lax.ppermute(block, 'dp', route)  118 us
    ppermute x44, starting transfers between devices, send_dp(): return lax.ppermute(block, 'dp', route)  59.6 us
    dot_general x6, matrix products, matmul(): return jnp.dot(left, right, preferred_element_type=jnp.float32)  31 us
    pallas_call x1, Pallas kernels, attend_back(): pl.pallas_call(attend_back_body, grid=(H // 2,), out_shape=(rows_of(BF),...  22.7 us
    dot_general x6, matrix products, matmul_tn(): lax.dot_general(left, right, (((0,), (0,)), ((), ())), preferred_element_...  21.2 us
    dot_general x6, matrix products, matmul_nt(): lax.dot_general(left, right, (((1,), (1,)), ((), ())), preferred_element_...  17.9 us
  transfers between devices with their start and end apart: 73, of which 23 were waited for; matrix products, arithmetic and copies ran while one was open for 15% of the time, Pallas kernels for 52%

profile of v2, /device:TPU:0, one launch (start us, length us, event | category | flops | bytes accessed | tf_op | source)
XLA Modules:
  0.0 883.8 jit_solution(14906058978719819291)
XLA Ops:
  30.2 8.5 collective-permute-done.3
  54.1 10.1 %collective-permute-done.27 = bf16[144,768]{1,0:T(8,128)(2,1)} collective-permute-done((bf16[144,768]{1,0:T(8,128)(2,1)}, bf16[144,768]{1,0:T(8,128)(2,1)}, u32[]{:S(2)}, u32[]{:S(2)}) %collective-permute-start.27) | collective-permute-done | bytes 221216 | tf_op jit(solution)/shard_map/ppermute | solution.py:44
  71.5 6.1 collective-permute-done.14.refs_6_
  82.3 4.8 collective-permute-done.30.refs_2_
  91.7 4.8 collective-permute-done.33.refs_6_
  96.5 8.1 collective-permute-done.12.refs_3_
  112.2 7.3 assemble.2
  128.3 4.9 reshape.362
  137.0 7.2 assemble.3
  147.4 4.9 reshape.364
  157.0 13.2 %attend.1 = (f32[416,768]{1,0:T(8,128)}, f32[416,128]{1,0:T(8,128)}) custom-call(s32[4]{0:T(128)} %pad_add_fusion.1.counts, s32[208,512]{1,0:T(8,128)} %pad_add_fusion.ids, f32[16,128]{1,0:T(8,128)} %pad.30.table, bf16[416,768]{1,0:T(8,128)(2,1)} %fusion.31.query, bf16[416,768]{1,0:T(8,128)(2,1)} %copy-done.23, ...), custom_call_target="tpu_custom_call" | custom-call | tf_op jit(solution)/shard_map/attend/pallas_call | solution.py:284
  174.9 14.9 %fusion.77 = (f32[416]{0:T(512)S(1)}, f32[416,3072]{1,0:T(8,128)S(1)}, f32[416,3072]{1,0:T(8,128)S(1)}, f32[416,3072]{1,0:T(8,128)}) fusion(f32[3072]{0:T(1024)S(1)} %add.413, bf16[768,3072]{1,0:T(8,128)(2,1)S(1)} %copy-done.29, f32[416,768]{1,0:T(8,128)S(1)} %get-tuple-element.109, f32[768]{0:T(1024)S(1)} %get-tuple-element.40, ...), kind=kOutput, calls=%fused_computation.237 | convolution fusion | flops 2048876160 | bytes 21355392 | tf_op jit(solution)/shard_map/dot_general | solution.py:426
  195.1 4.7 convert_reduce_fusion
  199.8 4.8 multiply_reduce_fusion.4
  204.6 4.9 multiply_convert_fusion.1
  214.9 22.7 %attend_back.1 = (bf16[416,768]{1,0:T(8,128)(2,1)}, f32[416,768]{1,0:T(8,128)}, f32[416,768]{1,0:T(8,128)}, bf16[416,768]{1,0:T(8,128)(2,1)}, bf16[416,768]{1,0:T(8,128)(2,1)}, /*index=5*/f32[4,3328,128]{2,1,0:T(8,128)}) custom-call(s32[4]{0:T(128)} %pad_add_fusion.1.counts, s32[208,512]{1,0:T(8,128)} %pad_add_fusion.ids, f32[16,128]{1,0:T(8,128)} %pad.30.table, ...), custom_call_target="tpu_custom_call" | custom-call | tf_op jit(solution)/shard_map/attend_back/pallas_call | solution.py:342
  238.2 8.6 reshape.367.refs_4_.refs_0_
  246.9 7.7 multiply_convert_fusion.refs_1_
  254.5 216.8 %scatter.3 = bf16[2,2,2,2,4,144,384]{6,5,4,3,2,1,0:T(8,128)(2,1)} custom-call(s32[4]{0:T(128)} %pad_add_fusion.2.spot, bf16[3072,768]{1,0:T(8,128)(2,1)} %reshape.367.refs_4_.refs_0_, bf16[3072,768]{1,0:T(8,128)(2,1)} %multiply_convert_fusion.refs_1_), custom_call_target="tpu_custom_call" | custom-call | tf_op jit(solution)/shard_map/scatter/pallas_call | solution.py:178
  486.0 216.8 %scatter.2 = bf16[2,2,2,2,4,144,384]{6,5,4,3,2,1,0:T(8,128)(2,1)} custom-call(s32[4]{0:T(128)} %pad_add_fusion.2.spot, bf16[768,768]{1,0:T(8,128)(2,1)} %multiply_convert_fusion.5.refs_0_, bf16[768,768]{1,0:T(8,128)(2,1)} %multiply_convert_fusion.4.refs_1_, bf16[768,768]{1,0:T(8,128)(2,1)} %multiply_convert_fusion.3.refs_2_, ...), custom_call_target="tpu_custom_call" | custom-call | tf_op jit(solution)/shard_map/scatter/pallas_call | solution.py:178
  707.8 14.2 %table_grad.1 = f32[64,32]{1,0:T(8,128)} custom-call(s32[208,512]{1,0:T(8,128)} %pad_add_fusion.ids, f32[4,3328,128]{2,1,0:T(8,128)} %get-tuple-element.23.terms), custom_call_target="tpu_custom_call" | custom-call | tf_op jit(solution)/shard_map/table_grad/pallas_call | solution.py:394
  727.4 5.1 fusion.16
  743.5 11.8 %collective-permute-done.56 = bf16[2,4,144,384]{3,2,1,0:T(8,128)(2,1)} collective-permute-done((bf16[2,4,144,384]{3,2,1,0:T(8,128)(2,1)}, bf16[2,4,144,384]{3,2,1,0:T(8,128)(2,1)}, u32[]{:S(2)}, u32[]{:S(2)}) %collective-permute-start.56) | collective-permute-done | bytes 884768 | tf_op jit(solution)/shard_map/ppermute | solution.py:44
  758.7 5.4 fusion.20
  767.3 5.3 collective-permute-done.63
  772.8 4.3 collective-permute-done.64
  779.3 14.3 %collective-permute-done.55 = bf16[4,144,384]{2,1,0:T(8,128)(2,1)} collective-permute-done((bf16[4,144,384]{2,1,0:T(8,128)(2,1)}, bf16[4,144,384]{2,1,0:T(8,128)(2,1)}, u32[]{:S(2)}, u32[]{:S(2)}) %collective-permute-start.55) | collective-permute-done | bytes 442400 | tf_op jit(solution)/shard_map/ppermute | solution.py:44
  803.2 5.7 collective-permute-done.49
  821.4 11.8 %collective-permute-done.59 = bf16[144,768]{1,0:T(8,128)(2,1)S(1)} collective-permute-done((bf16[144,768]{1,0:T(8,128)(2,1)}, bf16[144,768]{1,0:T(8,128)(2,1)S(1)}, u32[]{:S(2)}, u32[]{:S(2)}) %collective-permute-start.59) | collective-permute-done | bytes 221216 | tf_op jit(solution)/shard_map/ppermute | solution.py:44
  833.2 7.4 collective-permute-done.51
  846.6 6.5 fusion.28
  866.2 4.6 collective-permute-start.70
  (395 shorter events, 199.4 us)
Async XLA Ops:
  23.2 20.5 %collective-permute-start.9 = (bf16[144,768]{1,0:T(8,128)(2,1)}, bf16[144,768]{1,0:T(8,128)(2,1)S(1)}, u32[]{:S(2)}, u32[]{:S(2)}) collective-permute-start(bf16[144,768]{1,0:T(8,128)(2,1)} %select_n.131), channel_id=1, source_target_pairs={{0,12},{1,13},{2,14},{3,15},{4,0},{5,1},{6,2},{7,3},{8,4},{9,5},{1... | collective-permute-start | bytes 663560 | tf_op jit(solution)/shard_map/ppermute | solution.py:44
  24.5 20.4 %collective-permute-start.8 = (bf16[144,768]{1,0:T(8,128)(2,1)}, bf16[144,768]{1,0:T(8,128)(2,1)}, u32[]{:S(2)}, u32[]{:S(2)}) collective-permute-start(bf16[144,768]{1,0:T(8,128)(2,1)} %select_n.131), channel_id=1, source_target_pairs={{0,8},{1,9},{2,10},{3,11},{4,12},{5,13},{6,14},{7,15},{8,0},{9,1},... | collective-permute-start | bytes 663560 | tf_op jit(solution)/shard_map/ppermute | solution.py:44
  26.2 18.9 %collective-permute-start.7 = (bf16[144,768]{1,0:T(8,128)(2,1)}, bf16[144,768]{1,0:T(8,128)(2,1)}, u32[]{:S(2)}, u32[]{:S(2)}) collective-permute-start(bf16[144,768]{1,0:T(8,128)(2,1)} %select_n.131), channel_id=1, source_target_pairs={{0,4},{1,5},{2,6},{3,7},{4,8},{5,9},{6,10},{7,11},{8,12},{9,13},{1... | collective-permute-start | bytes 663560 | tf_op jit(solution)/shard_map/ppermute | solution.py:44
  43.6 20.6 %collective-permute-start.27 = (bf16[144,768]{1,0:T(8,128)(2,1)}, bf16[144,768]{1,0:T(8,128)(2,1)}, u32[]{:S(2)}, u32[]{:S(2)}) collective-permute-start(bf16[144,768]{1,0:T(8,128)(2,1)} %select_n.134), channel_id=1, source_target_pairs={{0,8},{1,9},{2,10},{3,11},{4,12},{5,13},{6,14},{7,15},{8,0},{9,1},... | collective-permute-start | bytes 663560 | tf_op jit(solution)/shard_map/ppermute | solution.py:44
  44.9 20.8 %collective-permute-start.26 = (bf16[144,768]{1,0:T(8,128)(2,1)}, bf16[144,768]{1,0:T(8,128)(2,1)}, u32[]{:S(2)}, u32[]{:S(2)}) collective-permute-start(bf16[144,768]{1,0:T(8,128)(2,1)} %select_n.134), channel_id=1, source_target_pairs={{0,4},{1,5},{2,6},{3,7},{4,8},{5,9},{6,10},{7,11},{8,12},{9,13},{1... | collective-permute-start | bytes 663560 | tf_op jit(solution)/shard_map/ppermute | solution.py:44
  47.4 20.5 %collective-permute-start.10 = (bf16[4,144,384]{2,1,0:T(8,128)(2,1)}, bf16[4,144,384]{2,1,0:T(8,128)(2,1)}, u32[]{:S(2)}, u32[]{:S(2)}) collective-permute-start(bf16[4,144,384]{2,1,0:T(8,128)(2,1)} %get-tuple-element.89.refs_0_), channel_id=1, source_target_pairs={{0,1},{1,0},{2,3},{3,2},{4,5},{5,4},{6,7},{7,6},{8,9},{9,8},{10,11... | collective-permute-start | bytes 1327112 | tf_op jit(solution)/shard_map/ppermute | solution.py:44
  49.9 18.6 %collective-permute-start.11 = (bf16[4,144,384]{2,1,0:T(8,128)(2,1)}, bf16[4,144,384]{2,1,0:T(8,128)(2,1)}, u32[]{:S(2)}, u32[]{:S(2)}) collective-permute-start(bf16[4,144,384]{2,1,0:T(8,128)(2,1)} %get-tuple-element.89.refs_0_), channel_id=1, source_target_pairs={{0,2},{1,3},{2,0},{3,1},{4,6},{5,7},{6,4},{7,5},{8,10},{9,11},{10,... | collective-permute-start | bytes 1327112 | tf_op jit(solution)/shard_map/ppermute | solution.py:44
  50.4 20.6 %collective-permute-start.13 = (bf16[4,144,384]{2,1,0:T(8,128)(2,1)}, bf16[4,144,384]{2,1,0:T(8,128)(2,1)}, u32[]{:S(2)}, u32[]{:S(2)}) collective-permute-start(bf16[4,144,384]{2,1,0:T(8,128)(2,1)} %get-tuple-element.88.refs_4_), channel_id=1, source_target_pairs={{0,1},{1,0},{2,3},{3,2},{4,5},{5,4},{6,7},{7,6},{8,9},{9,8},{10,11... | collective-permute-start | bytes 1327112 | tf_op jit(solution)/shard_map/ppermute | solution.py:44
  70.9 16.1 %collective-permute-start.30 = (bf16[4,144,384]{2,1,0:T(8,128)(2,1)}, bf16[4,144,384]{2,1,0:T(8,128)(2,1)}, u32[]{:S(2)}, u32[]{:S(2)}) collective-permute-start(bf16[4,144,384]{2,1,0:T(8,128)(2,1)} %get-tuple-element.87.refs_0_), channel_id=1, source_target_pairs={{0,2},{1,3},{2,0},{3,1},{4,6},{5,7},{6,4},{7,5},{8,10},{9,11},{10,... | collective-permute-start | bytes 1327112 | tf_op jit(solution)/shard_map/ppermute | solution.py:44
  80.0 16.5 %collective-permute-start.33 = (bf16[4,144,384]{2,1,0:T(8,128)(2,1)S(1)}, bf16[4,144,384]{2,1,0:T(8,128)(2,1)}, u32[]{:S(2)}, u32[]{:S(2)}) collective-permute-start(bf16[4,144,384]{2,1,0:T(8,128)(2,1)S(1)} %get-tuple-element.86.refs_4_), channel_id=1, source_target_pairs={{0,2},{1,3},{2,0},{3,1},{4,6},{5,7},{6,4},{7,5},{8,10},{9,11},{10,... | collective-permute-start | bytes 1327112 | tf_op jit(solution)/shard_map/ppermute | solution.py:44
  81.5 23.1 %collective-permute-start.12 = (bf16[4,144,384]{2,1,0:T(8,128)(2,1)}, bf16[4,144,384]{2,1,0:T(8,128)(2,1)}, u32[]{:S(2)}, u32[]{:S(2)}) collective-permute-start(bf16[4,144,384]{2,1,0:T(8,128)(2,1)} %collective-permute-done.10.refs_1_), channel_id=1, source_target_pairs={{0,2},{1,3},{2,0},{3,1},{4,6},{5,7},{6,4},{7,5},{8,10},{9,11},{10,... | collective-permute-start | bytes 1327112 | tf_op jit(solution)/shard_map/ppermute | solution.py:44
  82.3 22.9 %collective-permute-start.17 = (bf16[4,144,384]{2,1,0:T(8,128)(2,1)}, bf16[4,144,384]{2,1,0:T(8,128)(2,1)}, u32[]{:S(2)}, u32[]{:S(2)}) collective-permute-start(bf16[4,144,384]{2,1,0:T(8,128)(2,1)} %collective-permute-done.10.refs_1_), channel_id=1, source_target_pairs={{0,16},{16,0},{1,17},{17,1},{2,18},{18,2},{3,19},{19,3},{4,20},{20... | collective-permute-start | bytes 1327112 | tf_op jit(solution)/shard_map/ppermute | solution.py:48
  87.0 17.6 %collective-permute-start.15 = (bf16[4,144,384]{2,1,0:T(8,128)(2,1)}, bf16[4,144,384]{2,1,0:T(8,128)(2,1)}, u32[]{:S(2)}, u32[]{:S(2)}) collective-permute-start(bf16[4,144,384]{2,1,0:T(8,128)(2,1)} %collective-permute-done.14.refs_6_), channel_id=1, source_target_pairs={{0,1},{1,0},{2,3},{3,2},{4,5},{5,4},{6,7},{7,6},{8,9},{9,8},{10,11... | collective-permute-start | bytes 1327112 | tf_op jit(solution)/shard_map/ppermute | solution.py:44
  136.5 20.6 %collective-permute-start.24 = (bf16[416,768]{1,0:T(8,128)(2,1)S(1)}, bf16[416,768]{1,0:T(8,128)(2,1)}, u32[]{:S(2)}, u32[]{:S(2)}) collective-permute-start(bf16[416,768]{1,0:T(8,128)(2,1)S(1)} %convolution_convert_fusion.key_own), channel_id=1, source_target_pairs={{0,16},{16,0},{1,17},{17,1},{2,18},{18,2},{3,19},{19,3},{4,20},{20... | collective-permute-start | bytes 1916936 | tf_op jit(solution)/shard_map/ppermute | solution.py:411
  136.9 20.1 %collective-permute-start.25 = (bf16[416,768]{1,0:T(8,128)(2,1)S(1)}, bf16[416,768]{1,0:T(8,128)(2,1)}, u32[]{:S(2)}, u32[]{:S(2)}) collective-permute-start(bf16[416,768]{1,0:T(8,128)(2,1)S(1)} %fusion.32.value_own), channel_id=1, source_target_pairs={{0,16},{16,0},{1,17},{17,1},{2,18},{18,2},{3,19},{19,3},{4,20},{20... | collective-permute-start | bytes 1916936 | tf_op jit(solution)/shard_map/ppermute | solution.py:411
  237.6 245.4 %collective-permute-start.43 = (bf16[416,768]{1,0:T(8,128)(2,1)}, bf16[416,768]{1,0:T(8,128)(2,1)}, u32[]{:S(2)}, u32[]{:S(2)}) collective-permute-start(bf16[416,768]{1,0:T(8,128)(2,1)} %get-tuple-element.20), channel_id=1, source_target_pairs={{0,16},{16,0},{1,17},{17,1},{2,18},{18,2},{3,19},{19,3},{4,20},{20... | collective-permute-start | bytes 1916936 | tf_op jit(solution)/shard_map/ppermute | solution.py:411
  238.1 241.7 %collective-permute-start.44 = (bf16[416,768]{1,0:T(8,128)(2,1)}, bf16[416,768]{1,0:T(8,128)(2,1)}, u32[]{:S(2)}, u32[]{:S(2)}) collective-permute-start(bf16[416,768]{1,0:T(8,128)(2,1)} %get-tuple-element.22), channel_id=1, source_target_pairs={{0,16},{16,0},{1,17},{17,1},{2,18},{18,2},{3,19},{19,3},{4,20},{20... | collective-permute-start | bytes 1916936 | tf_op jit(solution)/shard_map/ppermute | solution.py:411
  475.5 251.8 %collective-permute-start.53 = (bf16[2,2,2,4,144,384]{5,4,3,1,2,0:T(8,128)(2,1)}, bf16[2,2,2,4,144,384]{5,4,3,1,2,0:T(8,128)(2,1)}, u32[]{:S(2)}, u32[]{:S(2)}) collective-permute-start(bf16[2,2,2,4,144,384]{5,4,3,1,2,0:T(8,128)(2,1)} %copy_bitcast_fusion), channel_id=1, source_target_pairs={{0,16},{16,0},{1,17},{17,1},{2,18},{18,2},{3,19},{19,3},{4,20},{20... | collective-permute-start | bytes 10616840 | tf_op jit(solution)/shard_map/ppermute | solution.py:48
  707.0 51.7 %collective-permute-start.45 = (bf16[2,2,2,4,144,384]{5,4,3,2,1,0:T(8,128)(2,1)}, bf16[2,2,2,4,144,384]{5,4,3,2,1,0:T(8,128)(2,1)}, u32[]{:S(2)}, u32[]{:S(2)}) collective-permute-start(bf16[2,2,2,4,144,384]{5,4,3,2,1,0:T(8,128)(2,1)} %slice_bitcast_fusion), channel_id=1, source_target_pairs={{0,16},{16,0},{1,17},{17,1},{2,18},{18,2},{3,19},{19,3},{4,20},{20... | collective-permute-start | bytes 10616840 | tf_op jit(solution)/shard_map/ppermute | solution.py:48
  732.5 22.8 %collective-permute-start.56 = (bf16[2,4,144,384]{3,2,1,0:T(8,128)(2,1)}, bf16[2,4,144,384]{3,2,1,0:T(8,128)(2,1)}, u32[]{:S(2)}, u32[]{:S(2)}) collective-permute-start(bf16[2,4,144,384]{3,2,1,0:T(8,128)(2,1)} %get-tuple-element.75), channel_id=1, source_target_pairs={{0,2},{1,3},{2,0},{3,1},{4,6},{5,7},{6,4},{7,5},{8,10},{9,11},{10,... | collective-permute-start | bytes 2654216 | tf_op jit(solution)/shard_map/ppermute | solution.py:44
  738.7 26.2 %collective-permute-start.54 = (bf16[2,4,144,384]{3,2,1,0:T(8,128)(2,1)}, bf16[2,4,144,384]{3,2,1,0:T(8,128)(2,1)S(1)}, u32[]{:S(2)}, u32[]{:S(2)}) collective-permute-start(bf16[2,4,144,384]{3,2,1,0:T(8,128)(2,1)} %get-tuple-element.77), channel_id=1, source_target_pairs={{0,1},{1,0},{2,3},{3,2},{4,5},{5,4},{6,7},{7,6},{8,9},{9,8},{10,11... | collective-permute-start | bytes 2654216 | tf_op jit(solution)/shard_map/ppermute | solution.py:44
  742.6 24.6 %collective-permute-start.62 = (f32[24,768]{1,0:T(8,128)S(1)}, f32[24,768]{1,0:T(8,128)S(1)}, u32[]{:S(2)}, u32[]{:S(2)}) collective-permute-start(f32[24,768]{1,0:T(8,128)S(1)} %pad_add_fusion.3), channel_id=1, source_target_pairs={{0,2},{1,3},{2,0},{3,1},{4,6},{5,7},{6,4},{7,5},{8,10},{9,11},{10,... | collective-permute-start | bytes 221192 | tf_op jit(solution)/shard_map/ppermute | solution.py:44
  757.4 20.5 %collective-permute-start.57 = (bf16[4,144,384]{2,1,0:T(8,128)(2,1)}, bf16[4,144,384]{2,1,0:T(8,128)(2,1)}, u32[]{:S(2)}, u32[]{:S(2)}) collective-permute-start(bf16[4,144,384]{2,1,0:T(8,128)(2,1)} %fusion.52), channel_id=1, source_target_pairs={{0,1},{1,0},{2,3},{3,2},{4,5},{5,4},{6,7},{7,6},{8,9},{9,8},{10,11... | collective-permute-start | bytes 1327112 | tf_op jit(solution)/shard_map/ppermute | solution.py:44
  764.1 30.8 %collective-permute-start.48 = (bf16[2,4,144,384]{3,2,1,0:T(8,128)(2,1)}, bf16[2,4,144,384]{3,2,1,0:T(8,128)(2,1)}, u32[]{:S(2)}, u32[]{:S(2)}) collective-permute-start(bf16[2,4,144,384]{3,2,1,0:T(8,128)(2,1)} %get-tuple-element.71), channel_id=1, source_target_pairs={{0,2},{1,3},{2,0},{3,1},{4,6},{5,7},{6,4},{7,5},{8,10},{9,11},{10,... | collective-permute-start | bytes 2654216 | tf_op jit(solution)/shard_map/ppermute | solution.py:44
  765.9 27.7 %collective-permute-start.55 = (bf16[4,144,384]{2,1,0:T(8,128)(2,1)}, bf16[4,144,384]{2,1,0:T(8,128)(2,1)}, u32[]{:S(2)}, u32[]{:S(2)}) collective-permute-start(bf16[4,144,384]{2,1,0:T(8,128)(2,1)} %fusion.51), channel_id=1, source_target_pairs={{0,2},{1,3},{2,0},{3,1},{4,6},{5,7},{6,4},{7,5},{8,10},{9,11},{10,... | collective-permute-start | bytes 1327112 | tf_op jit(solution)/shard_map/ppermute | solution.py:44
  777.1 38.7 %collective-permute-start.65 = (f32[24,768]{1,0:T(8,128)S(1)}, f32[24,768]{1,0:T(8,128)S(1)}, u32[]{:S(2)}, u32[]{:S(2)}) collective-permute-start(f32[24,768]{1,0:T(8,128)S(1)} %add.465), channel_id=1, source_target_pairs={{0,16},{16,0},{1,17},{17,1},{2,18},{18,2},{3,19},{19,3},{4,20},{20... | collective-permute-start | bytes 221192 | tf_op jit(solution)/shard_map/ppermute | solution.py:48
  777.2 22.8 %collective-permute-start.46 = (bf16[2,4,144,384]{3,2,1,0:T(8,128)(2,1)}, bf16[2,4,144,384]{3,2,1,0:T(8,128)(2,1)S(1)}, u32[]{:S(2)}, u32[]{:S(2)}) collective-permute-start(bf16[2,4,144,384]{3,2,1,0:T(8,128)(2,1)} %get-tuple-element.73), channel_id=1, source_target_pairs={{0,1},{1,0},{2,3},{3,2},{4,5},{5,4},{6,7},{7,6},{8,9},{9,8},{10,11... | collective-permute-start | bytes 2654216 | tf_op jit(solution)/shard_map/ppermute | solution.py:44
  801.7 31.4 %collective-permute-start.59 = (bf16[144,768]{1,0:T(8,128)(2,1)}, bf16[144,768]{1,0:T(8,128)(2,1)S(1)}, u32[]{:S(2)}, u32[]{:S(2)}) collective-permute-start(bf16[144,768]{1,0:T(8,128)(2,1)} %get-tuple-element.85), channel_id=1, source_target_pairs={{0,8},{1,9},{2,10},{3,11},{4,12},{5,13},{6,14},{7,15},{8,0},{9,1},... | collective-permute-start | bytes 663560 | tf_op jit(solution)/shard_map/ppermute | solution.py:44
  808.9 24.2 %collective-permute-start.58 = (bf16[144,768]{1,0:T(8,128)(2,1)}, bf16[144,768]{1,0:T(8,128)(2,1)}, u32[]{:S(2)}, u32[]{:S(2)}) collective-permute-start(bf16[144,768]{1,0:T(8,128)(2,1)} %get-tuple-element.83), channel_id=1, source_target_pairs={{0,4},{1,5},{2,6},{3,7},{4,8},{5,9},{6,10},{7,11},{8,12},{9,13},{1... | collective-permute-start | bytes 663560 | tf_op jit(solution)/shard_map/ppermute | solution.py:44
  812.6 20.6 %collective-permute-start.52 = (bf16[144,768]{1,0:T(8,128)(2,1)}, bf16[144,768]{1,0:T(8,128)(2,1)}, u32[]{:S(2)}, u32[]{:S(2)}) collective-permute-start(bf16[144,768]{1,0:T(8,128)(2,1)} %get-tuple-element.81), channel_id=1, source_target_pairs={{0,12},{1,13},{2,14},{3,15},{4,0},{5,1},{6,2},{7,3},{8,4},{9,5},{1... | collective-permute-start | bytes 663560 | tf_op jit(solution)/shard_map/ppermute | solution.py:44
  815.8 24.8 %collective-permute-start.51 = (bf16[144,768]{1,0:T(8,128)(2,1)}, bf16[144,768]{1,0:T(8,128)(2,1)}, u32[]{:S(2)}, u32[]{:S(2)}) collective-permute-start(bf16[144,768]{1,0:T(8,128)(2,1)} %get-tuple-element.82), channel_id=1, source_target_pairs={{0,8},{1,9},{2,10},{3,11},{4,12},{5,13},{6,14},{7,15},{8,0},{9,1},... | collective-permute-start | bytes 663560 | tf_op jit(solution)/shard_map/ppermute | solution.py:44
  815.8 24.8 %collective-permute-start.50 = (bf16[144,768]{1,0:T(8,128)(2,1)}, bf16[144,768]{1,0:T(8,128)(2,1)}, u32[]{:S(2)}, u32[]{:S(2)}) collective-permute-start(bf16[144,768]{1,0:T(8,128)(2,1)} %get-tuple-element.80), channel_id=1, source_target_pairs={{0,4},{1,5},{2,6},{3,7},{4,8},{5,9},{6,10},{7,11},{8,12},{9,13},{1... | collective-permute-start | bytes 663560 | tf_op jit(solution)/shard_map/ppermute | solution.py:44
  (92 other events, 862.7 us)

commit v3 on v2

--- a/solution.py
+++ b/solution.py
@@ -134,35 +134,36 @@
 
 
 def scatter_body(phase, pieces, spot, *refs):
-    sources, out, sem = refs[:-2], refs[-2], refs[-1]
+    sources, kept, lent, sem = refs[:-3], refs[-3], refs[-2], refs[-1]
     side, z, y, x = spot[0], spot[1], spot[2], spot[3]
     copies = []
     for block in range(32):
         home, parity = block // 2, block % 2
         owner = parity if phase == 0 else 1 - parity
-        other = side ^ owner
         turn = (home // 4 - z) & 3
         yr = (home // 2 % 2) ^ y
         xr = (home % 2) ^ x
         for index, source_row, block_row, count in pieces[block]:
             for half in range(2):
-                copies.append(
+                stay, leave = [
                     pltpu.make_async_copy(
                         sources[index].at[pl.ds(source_row, count), pl.ds(half * HALF, HALF)],
-                        out.at[other, half, yr, xr, turn, pl.ds(block_row, count), :],
+                        target.at[half, yr, xr, turn, pl.ds(block_row, count), :],
                         sem.at[len(copies)],
                     )
-                )
-    for copy in copies:
-        copy.start()
+                    for target in (kept, lent)
+                ]
+                pl.when(side == owner)(stay.start)
+                pl.when(side != owner)(leave.start)
+                copies.append(stay)
     for copy in copies:
         copy.wait()
 
 
 def scatter(phase, spot, tables):
     starts = [0]
-    for table in tables:
-        starts.append(starts[-1] + table.shape[0])
+    for rows in (D, D, D, D, FF, FF):
+        starts.append(starts[-1] + rows)
     pieces = []
     for block in range(32):
         low = phase * PHASE_ROWS + block * BLOCK
@@ -177,10 +178,10 @@
     count = 2 * sum(len(parts) for parts in pieces)
     return pl.pallas_call(
         functools.partial(scatter_body, phase, pieces),
-        out_shape=jax.ShapeDtypeStruct((2, 2, 2, 2, 4, BLOCK, HALF), BF),
+        out_shape=(jax.ShapeDtypeStruct((2, 2, 2, 4, BLOCK, HALF), BF),) * 2,
         in_specs=[pl.BlockSpec(memory_space=pltpu.SMEM)]
-        + [pl.BlockSpec(memory_space=pl.ANY)] * len(used),
-        out_specs=pl.BlockSpec(memory_space=pl.ANY),
+        + [pl.BlockSpec(memory_space=pltpu.VMEM)] * len(used),
+        out_specs=(pl.BlockSpec(memory_space=pl.ANY),) * 2,
         scratch_shapes=[pltpu.SemaphoreType.DMA((count,))],
         name="scatter",
     )(spot, *[tables[index] for index in used])
@@ -190,12 +191,11 @@
     return (left.astype(F32) + right.astype(F32)).astype(BF)
 
 
-def reduce_phase(parts):
-    theirs = send_mod(parts[1])
-    left_out = send_dp(plus(parts[0, 0, :, 1], theirs[0, :, 1]), x_swap())
-    right_out = send_dp(plus(parts[0, 1, 1], theirs[1, 1]), y_swap())
-    left_in = plus(parts[0, 0, :, 0], theirs[0, :, 0])
-    right_in = plus(parts[0, 1, 0], theirs[1, 0])
+def reduce_phase(mine, theirs):
+    left_out = send_dp(plus(mine[0, :, 1], theirs[0, :, 1]), x_swap())
+    right_out = send_dp(plus(mine[1, 1], theirs[1, 1]), y_swap())
+    left_in = plus(mine[0, :, 0], theirs[0, :, 0])
+    right_in = plus(mine[1, 0], theirs[1, 0])
     left_next = send_dp(plus(left_in[1], left_out[1]), y_swap())
     right_next = send_dp(plus(right_in[1], right_out[1]), x_swap())
     left = left_in[0].astype(F32) + left_out[0].astype(F32) + left_next.astype(F32)
@@ -401,6 +401,63 @@
     return both[:NB, :H] + both[:NB, 16 : 16 + H]
 
 
+CUT = PHASE_ROWS - 4 * D
+
+
+def spread_body(first, second, out, held):
+    for half, table in enumerate((first, second)):
+        start = 4 * D if half == 0 else 0
+        for c in range(D // 128):
+            lanes = pl.ds(c * 128, 128)
+            held[...] = table[pl.ds(start, CUT), lanes].astype(F32)
+            for part in range(4):
+                out[pl.ds(half * CUT // 4, CUT // 4), pl.ds(part * D + c * 128, 128)] = held[
+                    pl.ds(part, CUT // 4, stride=4), :
+                ].astype(BF)
+
+
+def spread(first, second):
+    whole = pl.BlockSpec(memory_space=pltpu.VMEM)
+    return pl.pallas_call(
+        spread_body,
+        out_shape=jax.ShapeDtypeStruct((D, FF), BF),
+        in_specs=[whole, whole],
+        out_specs=whole,
+        scratch_shapes=[pltpu.VMEM((CUT, 128), F32)],
+        name="spread",
+    )(first, second)
+
+
+def inner_grad_body(share, left, right, out, turned, held):
+    chunk = pl.program_id(0)
+
+    @pl.when(chunk == 0)
+    def _():
+        gap = jnp.zeros((KEYS - 2 * PAD, D), BF)
+        turned[...] = jnp.concatenate([left[...], gap], axis=0).T
+
+    gap = jnp.zeros((KEYS - 2 * PAD, 256), BF)
+    for part in range(4):
+        start = pl.multiple_of(part * D + chunk * 256, 256)
+        block = jnp.concatenate([right[:, pl.ds(start, 256)], gap], axis=0)
+        value = dot_f32(turned[...], block, NN) * share
+        for c in range(2):
+            held[c, pl.ds(part, D, stride=4), :] = value[:, c * 128 : (c + 1) * 128]
+    out[...] = jnp.concatenate([held[0], held[1]], axis=1).astype(BF)
+
+
+def inner_grad(left, right, share):
+    return pl.pallas_call(
+        functools.partial(inner_grad_body, share),
+        grid=(D // 256,),
+        out_shape=jax.ShapeDtypeStruct((FF, D), BF),
+        in_specs=[fixed((2 * PAD, D)), fixed((2 * PAD, FF))],
+        out_specs=pl.BlockSpec((FF, 256), lambda i: (0, i)),
+        scratch_shapes=[pltpu.VMEM((D, KEYS), BF), pltpu.VMEM((2, FF, 128), F32)],
+        name="inner_grad",
+    )(left, right)
+
+
 def from_partner(block, axis, bit):
     count = lax.axis_size(axis)
     route = []
@@ -455,13 +512,9 @@
 
 def unpack_tables(first, second, vec):
     square = [first[i * D : (i + 1) * D] for i in range(4)]
-    cut = PHASE_ROWS - 4 * D
-    w_inner = jnp.concatenate(
-        [first[4 * D :].reshape(cut // 4, FF), second[: FF - cut].reshape(D - cut // 4, FF)]
-    )
     return square + [
-        w_inner,
-        second[FF - cut :],
+        spread(first, second),
+        second[CUT:],
         vec[:10],
         vec[10:22].reshape(3, FF),
         vec[22].reshape(NB + 1, H),
@@ -487,6 +540,7 @@
         is_last = jnp.logical_and(side == 1, place == DP - 1)
         vec = jnp.where(is_last, own_copy[-EDGE:], jnp.zeros((), BF))
         vec = jnp.pad(vec, (0, D)).reshape(24, D)
+        vec, first = lax.optimization_barrier((vec, first))
         weights = unpack_tables(
             assemble(0, spot, gather_phase(first)),
             assemble(1, spot, gather_phase(second)),
@@ -551,7 +605,10 @@
     )
     _, gelu_pull = jax.vjp(exact_gelu, inner)
     grad_inner_low = gelu_pull(grad_activated)[0].astype(BF)
-    grad_w_inner = weight_grad(normed_two_low, grad_inner_low)
+    if fast:
+        grad_w_inner = inner_grad(normed_two_low, grad_inner_low, share)
+    else:
+        grad_w_inner = weight_grad(normed_two_low, grad_inner_low).reshape(FF, D)
     grad_b_inner = jnp.sum(grad_inner_low.astype(F32), axis=0)
     grad_normed_two = matmul_nt(grad_inner_low, w_inner)
     grad_mid_part, grad_gain_two, grad_shift_two = norm_back(
@@ -567,6 +624,10 @@
     )
     grad_head_scale = jnp.sum(jnp.sum(grad_scaled * attended, axis=0).reshape(H, HD), axis=1)
     grad_attended = (grad_scaled * scale_row).astype(BF)
+    if fast:
+        late = scatter(1, spot, [None] * 4 + [grad_w_inner, grad_w_outer])
+        late, grad_attended = lax.optimization_barrier((late, grad_attended))
+        late = (late[0], send_mod(late[1]))
     grad_query, key_kept, value_kept, key_sent, value_sent, terms = attend_back(
         counts, ids, table, logs, query, keys_both, values_both, grad_attended
     )
@@ -608,11 +669,11 @@
         )
         * share
     )
-    matrices = [grad_w_query, grad_w_key, grad_w_value, grad_w_out]
-    matrices += [grad_w_inner.reshape(FF, D), grad_w_outer]
+    matrices = [grad_w_query, grad_w_key, grad_w_value, grad_w_out, grad_w_inner, grad_w_outer]
     if fast:
-        second = reduce_phase(scatter(1, spot, matrices))
-        first = reduce_phase(scatter(0, spot, matrices))
+        second = reduce_phase(*late)
+        kept, lent = scatter(0, spot, matrices)
+        first = reduce_phase(kept, send_mod(lent))
         vec_grad = sum_all_small(jnp.pad(vec_grad, ((0, 1), (0, 0))))
         square = jnp.sum(first * first) + jnp.sum(second * second)
         square = square + jnp.where(is_last, jnp.sum(vec_grad * vec_grad), 0.0)

time: 890 us -> 461 us (0.52)
  Pallas kernels: 498 us -> 96.3 us
  local copies, waits for them, and re-layouts: 58.1 us -> 25.5 us
  waiting for transfers between devices: 118 us -> 127 us
    pallas_call x2, Pallas kernels: 434 us -> 14.7 us  [scatter(): pl.pallas_call(functools.partial(scatter_body, phase, pieces), out_shape=...]
    reshape x3 -> x0, local copies, waits for them, and re-layouts: 18.4 us -> none  [the longest x1 8.65 us: on_device(): matrices += [grad_w_inner.reshape(FF, D), grad_w_outer]]
    pallas_call x0 -> x2, Pallas kernels: none -> 16.3 us  [the longest x1 9.01 us: spread(): pl.pallas_call(spread_body, out_shape=jax.ShapeDtypeStruct((D, FF), BF),...]
    ppermute x44, waiting for transfers between devices: 118 us -> 127 us  [send_dp(): return lax.ppermute(block, 'dp', route)]
    dot_general x6 -> x5, matrix products: 21.2 us -> 13.4 us  [matmul_tn(): lax.dot_general(left, right, (((0,), (0,)), ((), ())), preferred_element_...]
  transfers between devices with their start and end apart: 73 -> 73, of which waited for: 23 -> 24; matrix products, arithmetic and copies ran while one was open for 15% -> 17% of each run, Pallas kernels for 52% -> 10%
where the time goes in v3:
time: 461 us; the launch traced here: 455 us
  waiting for transfers between devices  127 us (28%)
  Pallas kernels  96.3 us (21%)
  starting transfers between devices  75.8 us (16%)
  matrix products  66.4 us (14%)
  other arithmetic  57.5 us (12%)
  local copies, waits for them, and re-layouts  25.5 us (6%)
  between operations  6.52 us (1%)
    ppermute x44, waiting for transfers between devices, send_dp(): return lax.ppermute(block, 'dp', route)  127 us
    ppermute x44, starting transfers between devices, send_dp(): return lax.ppermute(block, 'dp', route)  60.2 us
    dot_general x6, matrix products, matmul(): return jnp.dot(left, right, preferred_element_type=jnp.float32)  31.5 us
    pallas_call x1, Pallas kernels, attend_back(): pl.pallas_call(attend_back_body, grid=(H // 2,), out_shape=(rows_of(BF),...  22.9 us
    dot_general x6, matrix products, matmul_nt(): lax.dot_general(left, right, (((1,), (1,)), ((), ())), preferred_element_...  21.5 us
    pallas_call x2, Pallas kernels, scatter(): pl.pallas_call(functools.partial(scatter_body, phase, pieces), out_shape=...  14.7 us
    pallas_call x2, Pallas kernels, assemble(): pl.pallas_call(functools.partial(assemble_body, phase), out_shape=jax.Sha...  14.5 us
    convert_element_type x9, other arithmetic, plus(): return (left.astype(F32) + right.astype(F32)).astype(BF)  14.4 us
  transfers between devices with their start and end apart: 73, of which 24 were waited for; matrix products, arithmetic and copies ran while one was open for 17% of the time, Pallas kernels for 10%

profile of v3, /device:TPU:0, one launch (start us, length us, event | category | flops | bytes accessed | tf_op | source)
XLA Modules:
  0.0 455.3 jit_solution(12765744498624745993)
XLA Ops:
  2.8 4.4 collective-permute-start
  17.9 3.7 collective-permute-start.9
  25.4 15.3 %collective-permute-done.4 = bf16[24,768]{1,0:T(8,128)(2,1)S(1)} collective-permute-done((bf16[24,768]{1,0:T(8,128)(2,1)S(1)}, bf16[24,768]{1,0:T(8,128)(2,1)S(1)}, u32[]{:S(2)}, u32[]{:S(2)}) %collective-permute-start.4) | collective-permute-done | bytes 36896 | tf_op jit(solution)/shard_map/ppermute | solution.py:44
  53.2 11.7 %collective-permute-done.27 = bf16[144,768]{1,0:T(8,128)(2,1)S(1)} collective-permute-done((bf16[144,768]{1,0:T(8,128)(2,1)}, bf16[144,768]{1,0:T(8,128)(2,1)S(1)}, u32[]{:S(2)}, u32[]{:S(2)}) %collective-permute-start.27) | collective-permute-done | bytes 221216 | tf_op jit(solution)/shard_map/ppermute | solution.py:44
  76.1 4.2 collective-permute-start.15
  81.7 4.6 %collective-permute-done.29.refs_1_ = bf16[4,144,384]{2,1,0:T(8,128)(2,1)} collective-permute-done((bf16[4,144,384]{2,1,0:T(8,128)(2,1)S(1)}, bf16[4,144,384]{2,1,0:T(8,128)(2,1)}, u32[]{:S(2)}, u32[]{:S(2)}) %collective-permute-start.29) | collective-permute-done | bytes 442400 | tf_op jit(solution)/shard_map/ppermute | solution.py:44
  86.8 8.0 %collective-permute-done.15.refs_7_ = bf16[4,144,384]{2,1,0:T(8,128)(2,1)S(1)} collective-permute-done((bf16[4,144,384]{2,1,0:T(8,128)(2,1)}, bf16[4,144,384]{2,1,0:T(8,128)(2,1)S(1)}, u32[]{:S(2)}, u32[]{:S(2)}) %collective-permute-start.15) | collective-permute-done | bytes 442400 | tf_op jit(solution)/shard_map/ppermute | solution.py:44
  100.8 7.3 %assemble.2 = bf16[32,144,768]{2,1,0:T(8,128)(2,1)} custom-call(s32[4]{0:T(128)} %pad_add_fusion.2.spot, bf16[4,144,384]{2,1,0:T(8,128)(2,1)} %get-tuple-element.105.refs_0_, bf16[4,144,384]{2,1,0:T(8,128)(2,1)} %collective-permute-done.10.refs_1_, bf16[4,144,384]{2,1,0:T(8,128)(2,1)} %collective-permute-done.11.refs_2_, bf16[4,144,384]{2,1,0:T(8,128)(2,1)} %copy-done.43, ...), custom_call_target="tpu_custom_call" | custom-call | tf_op jit(solution)/shard_map/assemble/pallas_call | solution.py:126
  110.2 7.9 %collective-permute-done.33.refs_6_ = bf16[4,144,384]{2,1,0:T(8,128)(2,1)} collective-permute-done((bf16[4,144,384]{2,1,0:T(8,128)(2,1)S(1)}, bf16[4,144,384]{2,1,0:T(8,128)(2,1)}, u32[]{:S(2)}, u32[]{:S(2)}) %collective-permute-start.33) | collective-permute-done | bytes 442400 | tf_op jit(solution)/shard_map/ppermute | solution.py:44
  132.1 7.2 %assemble.3 = bf16[32,144,768]{2,1,0:T(8,128)(2,1)} custom-call(s32[4]{0:T(128)} %pad_add_fusion.2.spot, bf16[4,144,384]{2,1,0:T(8,128)(2,1)} %copy-done.29, bf16[4,144,384]{2,1,0:T(8,128)(2,1)} %collective-permute-done.29.refs_1_, bf16[4,144,384]{2,1,0:T(8,128)(2,1)} %collective-permute-done.30.refs_2_, ...), custom_call_target="tpu_custom_call" | custom-call | tf_op jit(solution)/shard_map/assemble/pallas_call | solution.py:126
  139.3 9.0 %spread.1 = bf16[768,3072]{1,0:T(8,128)(2,1)} custom-call(bf16[4608,768]{1,0:T(8,128)(2,1)} %bitcast.169, bf16[4608,768]{1,0:T(8,128)(2,1)} %bitcast.178), custom_call_target="tpu_custom_call" | custom-call | tf_op jit(solution)/shard_map/spread/pallas_call | solution.py:421
  152.1 13.7 %attend.1 = (f32[416,768]{1,0:T(8,128)}, f32[416,128]{1,0:T(8,128)}) custom-call(s32[4]{0:T(128)} %pad_add_fusion.1.counts, s32[208,512]{1,0:T(8,128)} %pad_add_fusion.ids, f32[16,128]{1,0:T(8,128)} %pad.30.table, bf16[416,768]{1,0:T(8,128)(2,1)} %fusion.23.query, bf16[416,768]{1,0:T(8,128)(2,1)} %copy-done.23, bf16[416,768]{1,0:T(8,128)(2,1)} %copy-done.25, ...), custom_call_target="tpu_custom_call" | custom-call | tf_op jit(solution)/shard_map/attend/pallas_call | solution.py:284
  171.7 15.8 %fusion.84 = (f32[416]{0:T(512)S(1)}, f32[416,3072]{1,0:T(8,128)S(1)}, f32[416,3072]{1,0:T(8,128)S(1)}, f32[416,3072]{1,0:T(8,128)S(1)}) fusion(f32[3072]{0:T(1024)S(1)} %add.421, bf16[416,768]{1,0:T(8,128)(2,1)S(1)} %add_convert_fusion.12.left, bf16[768,3072]{1,0:T(8,128)(2,1)S(1)} %bitcast.194), kind=kOutput, calls=%fused_computation.232 | convolution fusion | flops 2047278720 | bytes 20706944 | tf_op jit(solution)/shard_map/dot_general | solution.py:483
  187.6 4.3 multiply_reduce_fusion.1
  194.3 5.6 %convert_reduce_fusion = (f32[3072]{0:T(1024)S(1)}, bf16[416,3072]{1,0:T(8,128)(2,1)}) fusion(f32[416,3072]{1,0:T(8,128)S(1)} %get-tuple-element.87, f32[416]{0:T(512)S(1)} %negate_multiply_fusion.4, f32[416]{0:T(512)S(1)} %get-tuple-element.120, f32[416,3072]{1,0:T(8,128)S(1)} %get-tuple-element.86, f32[416]{0:T(512)S(1)} %broadcast_multiply_fusion.3, ...), kind=kLoop, calls=%fused_computation.5 | loop fusion | flops 30667776 | bytes 23046656 | tf_op jit(solution)/shard_map/reduce_sum | solution.py:612
  199.9 7.3 %inner_grad.1.refs_0_.refs_4_ = bf16[3072,768]{1,0:T(8,128)(2,1)} custom-call(bf16[416,768]{1,0:T(8,128)(2,1)} %copy-done.26, bf16[416,3072]{1,0:T(8,128)(2,1)} %get-tuple-element.76.right), custom_call_target="tpu_custom_call" | custom-call | tf_op jit(solution)/shard_map/inner_grad/pallas_call | solution.py:450
  207.3 6.7 %multiply_reduce_fusion.4 = (f32[768]{0:T(1024)}, f32[416]{0:T(512)S(1)}, f32[768]{0:T(1024)}, f32[416,768]{1,0:T(8,128)S(1)}) fusion(f32[416,768]{1,0:T(8,128)} %copy-done.6, f32[416]{0:T(512)S(1)} %copy-done.76, f32[416]{0:T(512)S(1)} %copy-done.65, f32[768]{0:T(1024)S(1)} %get-tuple-element.56, bf16[416,3072]{1,0:T(8,128)(2,1)} %get-tuple-element.76.right, ...), kind=kOutput, calls=%fused_computation.69 | convolution fusion | flops 1965488256 | bytes 9844608 | tf_op jit(solution)/shard_map/dot_general | solution.py:493
  214.0 4.7 %multiply_convert_fusion.refs_1_ = bf16[3072,768]{1,0:T(8,128)(2,1)} fusion(bf16[416,768]{1,0:T(8,128)(2,1)S(1)} %copy-done.36, f32[416,3072]{1,0:T(8,128)S(1)} %bitcast.184, f32[3072]{0:T(1024)S(1)} %copy-done.87, f32[3072]{0:T(1024)S(1)} %mul.426, f32[416]{0:T(512)S(1)} %copy-done.81, f32[416]{0:T(512)S(1)} %copy-done.78), kind=kOutput, calls=%fused_computation | convolution fusion | flops 1974042624 | bytes 10497280 | tf_op jit(solution)/shard_map/dot_general | solution.py:487
  225.5 7.4 %scatter.2 = (bf16[2,2,2,4,144,384]{5,4,3,2,1,0:T(8,128)(2,1)}, bf16[2,2,2,4,144,384]{5,4,3,2,1,0:T(8,128)(2,1)}) custom-call(s32[4]{0:T(128)} %pad_add_fusion.2.spot, bf16[3072,768]{1,0:T(8,128)(2,1)} %inner_grad.1.refs_0_.refs_4_, bf16[3072,768]{1,0:T(8,128)(2,1)} %multiply_convert_fusion.refs_1_), custom_call_target="tpu_custom_call" | custom-call | tf_op jit(solution)/shard_map/scatter/pallas_call | solution.py:179
  235.9 22.9 %attend_back.1 = (bf16[416,768]{1,0:T(8,128)(2,1)}, f32[416,768]{1,0:T(8,128)}, f32[416,768]{1,0:T(8,128)}, bf16[416,768]{1,0:T(8,128)(2,1)}, bf16[416,768]{1,0:T(8,128)(2,1)}, /*index=5*/f32[4,3328,128]{2,1,0:T(8,128)}) custom-call(s32[4]{0:T(128)} %pad_add_fusion.1.counts, s32[208,512]{1,0:T(8,128)} %pad_add_fusion.ids, f32[16,128]{1,0:T(8,128)} %pad.30.table, ...), custom_call_target="tpu_custom_call" | custom-call | tf_op jit(solution)/shard_map/attend_back/pallas_call | solution.py:342
  269.3 7.4 %scatter.3 = (bf16[2,2,2,4,144,384]{5,4,3,2,1,0:T(8,128)(2,1)}, bf16[2,2,2,4,144,384]{5,4,3,2,1,0:T(8,128)(2,1)}) custom-call(s32[4]{0:T(128)} %pad_add_fusion.2.spot, bf16[768,768]{1,0:T(8,128)(2,1)} %multiply_convert_fusion.4.refs_0_, bf16[768,768]{1,0:T(8,128)(2,1)} %multiply_convert_fusion.3.refs_1_, bf16[768,768]{1,0:T(8,128)(2,1)} %multiply_convert_fusion.2.refs_2_, ...), custom_call_target="tpu_custom_call" | custom-call | tf_op jit(solution)/shard_map/scatter/pallas_call | solution.py:179
  277.8 14.2 %table_grad.1 = f32[64,32]{1,0:T(8,128)} custom-call(s32[208,512]{1,0:T(8,128)} %pad_add_fusion.ids, f32[4,3328,128]{2,1,0:T(8,128)} %get-tuple-element.41.terms), custom_call_target="tpu_custom_call" | custom-call | tf_op jit(solution)/shard_map/table_grad/pallas_call | solution.py:394
  297.2 3.3 multiply_reduce_fusion.6
  310.7 4.3 collective-permute-done.63
  315.2 3.8 add_convert_fusion.3
  330.0 11.7 %collective-permute-done.56 = bf16[2,4,144,384]{3,2,1,0:T(8,128)(2,1)} collective-permute-done((bf16[2,4,144,384]{3,2,1,0:T(8,128)(2,1)}, bf16[2,4,144,384]{3,2,1,0:T(8,128)(2,1)}, u32[]{:S(2)}, u32[]{:S(2)}) %collective-permute-start.56) | collective-permute-done | bytes 884768 | tf_op jit(solution)/shard_map/ppermute | solution.py:44
  349.2 20.3 %collective-permute-done.57 = bf16[4,144,384]{2,1,0:T(8,128)(2,1)S(1)} collective-permute-done((bf16[4,144,384]{2,1,0:T(8,128)(2,1)S(1)}, bf16[4,144,384]{2,1,0:T(8,128)(2,1)S(1)}, u32[]{:S(2)}, u32[]{:S(2)}) %collective-permute-start.57) | collective-permute-done | bytes 442400 | tf_op jit(solution)/shard_map/ppermute | solution.py:44
  391.8 14.9 %collective-permute-done.59 = bf16[144,768]{1,0:T(8,128)(2,1)} collective-permute-done((bf16[144,768]{1,0:T(8,128)(2,1)}, bf16[144,768]{1,0:T(8,128)(2,1)}, u32[]{:S(2)}, u32[]{:S(2)}) %collective-permute-start.59) | collective-permute-done | bytes 221216 | tf_op jit(solution)/shard_map/ppermute | solution.py:44
  406.7 5.9 %collective-permute-done.51 = bf16[144,768]{1,0:T(8,128)(2,1)} collective-permute-done((bf16[144,768]{1,0:T(8,128)(2,1)}, bf16[144,768]{1,0:T(8,128)(2,1)}, u32[]{:S(2)}, u32[]{:S(2)}) %collective-permute-start.51) | collective-permute-done | bytes 221216 | tf_op jit(solution)/shard_map/ppermute | solution.py:44
  418.7 6.2 %fusion.20 = bf16[416,768]{1,0:T(8,128)(2,1)S(1)} fusion(f32[416,768]{1,0:T(8,128)S(1)} %copy-done.8, bf16[4608,768]{1,0:T(8,128)(2,1)} %bitcast.179, f32[768]{0:T(1024)S(1)} %copy-done.91, f32[416,3072]{1,0:T(8,128)} %copy-done, f32[3072]{0:T(1024)S(1)} %copy-done.88, f32[3072]{0:T(1024)S(1)} %mul.426, f32[416]{0:T(512)S(1)} %copy-done.82, ...), kind=kOutput, calls=%fused_computation.60 | convolution fusion | flops 1970282496 | bytes 11778304 | tf_op jit(solution)/shard_map/dot_general | solution.py:483
  438.1 4.5 collective-permute-start.70
  448.6 3.8 fusion.76
  (499 shorter events, 176.8 us)
Async XLA Ops:
  17.9 28.7 %collective-permute-start.9 = (bf16[144,768]{1,0:T(8,128)(2,1)S(1)}, bf16[144,768]{1,0:T(8,128)(2,1)S(1)}, u32[]{:S(2)}, u32[]{:S(2)}) collective-permute-start(bf16[144,768]{1,0:T(8,128)(2,1)S(1)} %select_n.116), channel_id=1, source_target_pairs={{0,12},{1,13},{2,14},{3,15},{4,0},{5,1},{6,2},{7,3},{8,4},{9,5},{1... | collective-permute-start | bytes 663560 | tf_op jit(solution)/shard_map/ppermute | solution.py:44
  21.6 27.4 %collective-permute-start.8 = (bf16[144,768]{1,0:T(8,128)(2,1)S(1)}, bf16[144,768]{1,0:T(8,128)(2,1)S(1)}, u32[]{:S(2)}, u32[]{:S(2)}) collective-permute-start(bf16[144,768]{1,0:T(8,128)(2,1)S(1)} %select_n.116), channel_id=1, source_target_pairs={{0,8},{1,9},{2,10},{3,11},{4,12},{5,13},{6,14},{7,15},{8,0},{9,1},... | collective-permute-start | bytes 663560 | tf_op jit(solution)/shard_map/ppermute | solution.py:44
  21.6 27.4 %collective-permute-start.7 = (bf16[144,768]{1,0:T(8,128)(2,1)S(1)}, bf16[144,768]{1,0:T(8,128)(2,1)S(1)}, u32[]{:S(2)}, u32[]{:S(2)}) collective-permute-start(bf16[144,768]{1,0:T(8,128)(2,1)S(1)} %select_n.116), channel_id=1, source_target_pairs={{0,4},{1,5},{2,6},{3,7},{4,8},{5,9},{6,10},{7,11},{8,12},{9,13},{1... | collective-permute-start | bytes 663560 | tf_op jit(solution)/shard_map/ppermute | solution.py:44
  22.6 18.1 %collective-permute-start.4 = (bf16[24,768]{1,0:T(8,128)(2,1)S(1)}, bf16[24,768]{1,0:T(8,128)(2,1)S(1)}, u32[]{:S(2)}, u32[]{:S(2)}) collective-permute-start(bf16[24,768]{1,0:T(8,128)(2,1)S(1)} %add.392), channel_id=1, source_target_pairs={{0,8},{1,9},{2,10},{3,11},{4,12},{5,13},{6,14},{7,15},{8,0},{9,1},... | collective-permute-start | bytes 110600 | tf_op jit(solution)/shard_map/ppermute | solution.py:44
  45.6 19.3 %collective-permute-start.27 = (bf16[144,768]{1,0:T(8,128)(2,1)}, bf16[144,768]{1,0:T(8,128)(2,1)S(1)}, u32[]{:S(2)}, u32[]{:S(2)}) collective-permute-start(bf16[144,768]{1,0:T(8,128)(2,1)} %select_n.123), channel_id=1, source_target_pairs={{0,8},{1,9},{2,10},{3,11},{4,12},{5,13},{6,14},{7,15},{8,0},{9,1},... | collective-permute-start | bytes 663560 | tf_op jit(solution)/shard_map/ppermute | solution.py:44
  46.6 20.2 %collective-permute-start.26 = (bf16[144,768]{1,0:T(8,128)(2,1)}, bf16[144,768]{1,0:T(8,128)(2,1)}, u32[]{:S(2)}, u32[]{:S(2)}) collective-permute-start(bf16[144,768]{1,0:T(8,128)(2,1)} %select_n.123), channel_id=1, source_target_pairs={{0,4},{1,5},{2,6},{3,7},{4,8},{5,9},{6,10},{7,11},{8,12},{9,13},{1... | collective-permute-start | bytes 663560 | tf_op jit(solution)/shard_map/ppermute | solution.py:44
  50.0 22.6 %collective-permute-start.10 = (bf16[4,144,384]{2,1,0:T(8,128)(2,1)}, bf16[4,144,384]{2,1,0:T(8,128)(2,1)}, u32[]{:S(2)}, u32[]{:S(2)}) collective-permute-start(bf16[4,144,384]{2,1,0:T(8,128)(2,1)} %get-tuple-element.105.refs_0_), channel_id=1, source_target_pairs={{0,1},{1,0},{2,3},{3,2},{4,5},{5,4},{6,7},{7,6},{8,9},{9,8},{10,11... | collective-permute-start | bytes 1327112 | tf_op jit(solution)/shard_map/ppermute | solution.py:44
  51.1 22.0 %collective-permute-start.11 = (bf16[4,144,384]{2,1,0:T(8,128)(2,1)}, bf16[4,144,384]{2,1,0:T(8,128)(2,1)}, u32[]{:S(2)}, u32[]{:S(2)}) collective-permute-start(bf16[4,144,384]{2,1,0:T(8,128)(2,1)} %get-tuple-element.105.refs_0_), channel_id=1, source_target_pairs={{0,2},{1,3},{2,0},{3,1},{4,6},{5,7},{6,4},{7,5},{8,10},{9,11},{10,... | collective-permute-start | bytes 1327112 | tf_op jit(solution)/shard_map/ppermute | solution.py:44
  52.0 22.2 %collective-permute-start.13 = (bf16[4,144,384]{2,1,0:T(8,128)(2,1)S(1)}, bf16[4,144,384]{2,1,0:T(8,128)(2,1)}, u32[]{:S(2)}, u32[]{:S(2)}) collective-permute-start(bf16[4,144,384]{2,1,0:T(8,128)(2,1)S(1)} %get-tuple-element.104.refs_4_), channel_id=1, source_target_pairs={{0,1},{1,0},{2,3},{3,2},{4,5},{5,4},{6,7},{7,6},{8,9},{9,8},{10,11... | collective-permute-start | bytes 1327112 | tf_op jit(solution)/shard_map/ppermute | solution.py:44
  76.1 18.7 %collective-permute-start.17 = (bf16[4,144,384]{2,1,0:T(8,128)(2,1)}, bf16[4,144,384]{2,1,0:T(8,128)(2,1)S(1)}, u32[]{:S(2)}, u32[]{:S(2)}) collective-permute-start(bf16[4,144,384]{2,1,0:T(8,128)(2,1)} %collective-permute-done.10.refs_1_), channel_id=1, source_target_pairs={{0,16},{16,0},{1,17},{17,1},{2,18},{18,2},{3,19},{19,3},{4,20},{20... | collective-permute-start | bytes 1327112 | tf_op jit(solution)/shard_map/ppermute | solution.py:48
  76.1 18.7 %collective-permute-start.15 = (bf16[4,144,384]{2,1,0:T(8,128)(2,1)}, bf16[4,144,384]{2,1,0:T(8,128)(2,1)S(1)}, u32[]{:S(2)}, u32[]{:S(2)}) collective-permute-start(bf16[4,144,384]{2,1,0:T(8,128)(2,1)} %collective-permute-done.14.refs_6_), channel_id=1, source_target_pairs={{0,1},{1,0},{2,3},{3,2},{4,5},{5,4},{6,7},{7,6},{8,9},{9,8},{10,11... | collective-permute-start | bytes 1327112 | tf_op jit(solution)/shard_map/ppermute | solution.py:44
  98.4 19.6 %collective-permute-start.33 = (bf16[4,144,384]{2,1,0:T(8,128)(2,1)S(1)}, bf16[4,144,384]{2,1,0:T(8,128)(2,1)}, u32[]{:S(2)}, u32[]{:S(2)}) collective-permute-start(bf16[4,144,384]{2,1,0:T(8,128)(2,1)S(1)} %get-tuple-element.102.refs_4_), channel_id=1, source_target_pairs={{0,2},{1,3},{2,0},{3,1},{4,6},{5,7},{6,4},{7,5},{8,10},{9,11},{10,... | collective-permute-start | bytes 1327112 | tf_op jit(solution)/shard_map/ppermute | solution.py:44
  98.5 20.6 %collective-permute-start.35 = (bf16[4,144,384]{2,1,0:T(8,128)(2,1)S(1)}, bf16[4,144,384]{2,1,0:T(8,128)(2,1)S(1)}, u32[]{:S(2)}, u32[]{:S(2)}) collective-permute-start(bf16[4,144,384]{2,1,0:T(8,128)(2,1)S(1)} %get-tuple-element.103.refs_0_), channel_id=1, source_target_pairs={{0,16},{16,0},{1,17},{17,1},{2,18},{18,2},{3,19},{19,3},{4,20},{20... | collective-permute-start | bytes 1327112 | tf_op jit(solution)/shard_map/ppermute | solution.py:48
  98.6 20.5 %collective-permute-start.39 = (bf16[4,144,384]{2,1,0:T(8,128)(2,1)S(1)}, bf16[4,144,384]{2,1,0:T(8,128)(2,1)}, u32[]{:S(2)}, u32[]{:S(2)}) collective-permute-start(bf16[4,144,384]{2,1,0:T(8,128)(2,1)S(1)} %get-tuple-element.102.refs_4_), channel_id=1, source_target_pairs={{0,16},{16,0},{1,17},{17,1},{2,18},{18,2},{3,19},{19,3},{4,20},{20... | collective-permute-start | bytes 1327112 | tf_op jit(solution)/shard_map/ppermute | solution.py:48
  108.6 18.1 %collective-permute-start.31 = (bf16[4,144,384]{2,1,0:T(8,128)(2,1)}, bf16[4,144,384]{2,1,0:T(8,128)(2,1)}, u32[]{:S(2)}, u32[]{:S(2)}) collective-permute-start(bf16[4,144,384]{2,1,0:T(8,128)(2,1)} %collective-permute-done.29.refs_1_), channel_id=1, source_target_pairs={{0,2},{1,3},{2,0},{3,1},{4,6},{5,7},{6,4},{7,5},{8,10},{9,11},{10,... | collective-permute-start | bytes 1327112 | tf_op jit(solution)/shard_map/ppermute | solution.py:44
  110.1 18.7 %collective-permute-start.36 = (bf16[4,144,384]{2,1,0:T(8,128)(2,1)}, bf16[4,144,384]{2,1,0:T(8,128)(2,1)S(1)}, u32[]{:S(2)}, u32[]{:S(2)}) collective-permute-start(bf16[4,144,384]{2,1,0:T(8,128)(2,1)} %collective-permute-done.29.refs_1_), channel_id=1, source_target_pairs={{0,16},{16,0},{1,17},{17,1},{2,18},{18,2},{3,19},{19,3},{4,20},{20... | collective-permute-start | bytes 1327112 | tf_op jit(solution)/shard_map/ppermute | solution.py:48
  129.3 22.0 %collective-permute-start.24 = (bf16[416,768]{1,0:T(8,128)(2,1)S(1)}, bf16[416,768]{1,0:T(8,128)(2,1)S(1)}, u32[]{:S(2)}, u32[]{:S(2)}) collective-permute-start(bf16[416,768]{1,0:T(8,128)(2,1)S(1)} %convolution_convert_fusion.key_own), channel_id=1, source_target_pairs={{0,16},{16,0},{1,17},{17,1},{2,18},{18,2},{3,19},{19,3},{4,20},{20... | collective-permute-start | bytes 1916936 | tf_op jit(solution)/shard_map/ppermute | solution.py:468
  130.1 21.2 %collective-permute-start.25 = (bf16[416,768]{1,0:T(8,128)(2,1)S(1)}, bf16[416,768]{1,0:T(8,128)(2,1)}, u32[]{:S(2)}, u32[]{:S(2)}) collective-permute-start(bf16[416,768]{1,0:T(8,128)(2,1)S(1)} %fusion.24.value_own), channel_id=1, source_target_pairs={{0,16},{16,0},{1,17},{17,1},{2,18},{18,2},{3,19},{19,3},{4,20},{20... | collective-permute-start | bytes 1916936 | tf_op jit(solution)/shard_map/ppermute | solution.py:468
  259.4 55.8 %collective-permute-start.53 = (bf16[2,2,2,4,144,384]{5,4,3,2,1,0:T(8,128)(2,1)}, bf16[2,2,2,4,144,384]{5,4,3,2,1,0:T(8,128)(2,1)}, u32[]{:S(2)}, u32[]{:S(2)}) collective-permute-start(bf16[2,2,2,4,144,384]{5,4,3,2,1,0:T(8,128)(2,1)} %get-tuple-element.40), channel_id=1, source_target_pairs={{0,16},{16,0},{1,17},{17,1},{2,18},{18,2},{3,19},{19,3},{4,20},{20... | collective-permute-start | bytes 10616840 | tf_op jit(solution)/shard_map/ppermute | solution.py:48
  276.7 48.2 %collective-permute-start.45 = (bf16[2,2,2,4,144,384]{5,4,3,2,1,0:T(8,128)(2,1)}, bf16[2,2,2,4,144,384]{5,4,3,2,1,0:T(8,128)(2,1)}, u32[]{:S(2)}, u32[]{:S(2)}) collective-permute-start(bf16[2,2,2,4,144,384]{5,4,3,2,1,0:T(8,128)(2,1)} %get-tuple-element.38), channel_id=1, source_target_pairs={{0,16},{16,0},{1,17},{17,1},{2,18},{18,2},{3,19},{19,3},{4,20},{20... | collective-permute-start | bytes 10616840 | tf_op jit(solution)/shard_map/ppermute | solution.py:48
  318.9 22.8 %collective-permute-start.56 = (bf16[2,4,144,384]{3,2,1,0:T(8,128)(2,1)}, bf16[2,4,144,384]{3,2,1,0:T(8,128)(2,1)}, u32[]{:S(2)}, u32[]{:S(2)}) collective-permute-start(bf16[2,4,144,384]{3,2,1,0:T(8,128)(2,1)} %get-tuple-element.93), channel_id=1, source_target_pairs={{0,2},{1,3},{2,0},{3,1},{4,6},{5,7},{6,4},{7,5},{8,10},{9,11},{10,... | collective-permute-start | bytes 2654216 | tf_op jit(solution)/shard_map/ppermute | solution.py:44
  323.0 22.8 %collective-permute-start.54 = (bf16[2,4,144,384]{3,2,1,0:T(8,128)(2,1)}, bf16[2,4,144,384]{3,2,1,0:T(8,128)(2,1)}, u32[]{:S(2)}, u32[]{:S(2)}) collective-permute-start(bf16[2,4,144,384]{3,2,1,0:T(8,128)(2,1)} %get-tuple-element.91), channel_id=1, source_target_pairs={{0,1},{1,0},{2,3},{3,2},{4,5},{5,4},{6,7},{7,6},{8,9},{9,8},{10,11... | collective-permute-start | bytes 2654216 | tf_op jit(solution)/shard_map/ppermute | solution.py:44
  324.7 62.8 %collective-permute-start.65 = (f32[24,768]{1,0:T(8,128)S(1)}, f32[24,768]{1,0:T(8,128)S(1)}, u32[]{:S(2)}, u32[]{:S(2)}) collective-permute-start(f32[24,768]{1,0:T(8,128)S(1)} %add.473), channel_id=1, source_target_pairs={{0,16},{16,0},{1,17},{17,1},{2,18},{18,2},{3,19},{19,3},{4,20},{20... | collective-permute-start | bytes 221192 | tf_op jit(solution)/shard_map/ppermute | solution.py:48
  327.4 45.0 %collective-permute-start.48 = (bf16[2,4,144,384]{3,2,1,0:T(8,128)(2,1)S(1)}, bf16[2,4,144,384]{3,2,1,0:T(8,128)(2,1)S(1)}, u32[]{:S(2)}, u32[]{:S(2)}) collective-permute-start(bf16[2,4,144,384]{3,2,1,0:T(8,128)(2,1)S(1)} %get-tuple-element.89), channel_id=1, source_target_pairs={{0,2},{1,3},{2,0},{3,1},{4,6},{5,7},{6,4},{7,5},{8,10},{9,11},{10,... | collective-permute-start | bytes 2654216 | tf_op jit(solution)/shard_map/ppermute | solution.py:44
  329.4 45.5 %collective-permute-start.46 = (bf16[2,4,144,384]{3,2,1,0:T(8,128)(2,1)S(1)}, bf16[2,4,144,384]{3,2,1,0:T(8,128)(2,1)S(1)}, u32[]{:S(2)}, u32[]{:S(2)}) collective-permute-start(bf16[2,4,144,384]{3,2,1,0:T(8,128)(2,1)S(1)} %fusion.40), channel_id=1, source_target_pairs={{0,1},{1,0},{2,3},{3,2},{4,5},{5,4},{6,7},{7,6},{8,9},{9,8},{10,11... | collective-permute-start | bytes 2654216 | tf_op jit(solution)/shard_map/ppermute | solution.py:44
  342.9 26.6 %collective-permute-start.57 = (bf16[4,144,384]{2,1,0:T(8,128)(2,1)S(1)}, bf16[4,144,384]{2,1,0:T(8,128)(2,1)S(1)}, u32[]{:S(2)}, u32[]{:S(2)}) collective-permute-start(bf16[4,144,384]{2,1,0:T(8,128)(2,1)S(1)} %fusion.60), channel_id=1, source_target_pairs={{0,1},{1,0},{2,3},{3,2},{4,5},{5,4},{6,7},{7,6},{8,9},{9,8},{10,11... | collective-permute-start | bytes 1327112 | tf_op jit(solution)/shard_map/ppermute | solution.py:44
  346.9 23.8 %collective-permute-start.55 = (bf16[4,144,384]{2,1,0:T(8,128)(2,1)S(1)}, bf16[4,144,384]{2,1,0:T(8,128)(2,1)S(1)}, u32[]{:S(2)}, u32[]{:S(2)}) collective-permute-start(bf16[4,144,384]{2,1,0:T(8,128)(2,1)S(1)} %fusion.59), channel_id=1, source_target_pairs={{0,2},{1,3},{2,0},{3,1},{4,6},{5,7},{6,4},{7,5},{8,10},{9,11},{10,... | collective-permute-start | bytes 1327112 | tf_op jit(solution)/shard_map/ppermute | solution.py:44
  379.1 27.6 %collective-permute-start.59 = (bf16[144,768]{1,0:T(8,128)(2,1)}, bf16[144,768]{1,0:T(8,128)(2,1)}, u32[]{:S(2)}, u32[]{:S(2)}) collective-permute-start(bf16[144,768]{1,0:T(8,128)(2,1)} %get-tuple-element.101), channel_id=1, source_target_pairs={{0,8},{1,9},{2,10},{3,11},{4,12},{5,13},{6,14},{7,15},{8,0},{9,1},... | collective-permute-start | bytes 663560 | tf_op jit(solution)/shard_map/ppermute | solution.py:44
  381.4 25.2 %collective-permute-start.58 = (bf16[144,768]{1,0:T(8,128)(2,1)}, bf16[144,768]{1,0:T(8,128)(2,1)}, u32[]{:S(2)}, u32[]{:S(2)}) collective-permute-start(bf16[144,768]{1,0:T(8,128)(2,1)} %get-tuple-element.99), channel_id=1, source_target_pairs={{0,4},{1,5},{2,6},{3,7},{4,8},{5,9},{6,10},{7,11},{8,12},{9,13},{1... | collective-permute-start | bytes 663560 | tf_op jit(solution)/shard_map/ppermute | solution.py:44
  385.0 21.7 %collective-permute-start.52 = (bf16[144,768]{1,0:T(8,128)(2,1)}, bf16[144,768]{1,0:T(8,128)(2,1)}, u32[]{:S(2)}, u32[]{:S(2)}) collective-permute-start(bf16[144,768]{1,0:T(8,128)(2,1)} %get-tuple-element.97), channel_id=1, source_target_pairs={{0,12},{1,13},{2,14},{3,15},{4,0},{5,1},{6,2},{7,3},{8,4},{9,5},{1... | collective-permute-start | bytes 663560 | tf_op jit(solution)/shard_map/ppermute | solution.py:44
  387.5 25.1 %collective-permute-start.51 = (bf16[144,768]{1,0:T(8,128)(2,1)}, bf16[144,768]{1,0:T(8,128)(2,1)}, u32[]{:S(2)}, u32[]{:S(2)}) collective-permute-start(bf16[144,768]{1,0:T(8,128)(2,1)} %get-tuple-element.98), channel_id=1, source_target_pairs={{0,8},{1,9},{2,10},{3,11},{4,12},{5,13},{6,14},{7,15},{8,0},{9,1},... | collective-permute-start | bytes 663560 | tf_op jit(solution)/shard_map/ppermute | solution.py:44
  388.6 24.0 %collective-permute-start.50 = (bf16[144,768]{1,0:T(8,128)(2,1)}, bf16[144,768]{1,0:T(8,128)(2,1)}, u32[]{:S(2)}, u32[]{:S(2)}) collective-permute-start(bf16[144,768]{1,0:T(8,128)(2,1)} %get-tuple-element.96), channel_id=1, source_target_pairs={{0,4},{1,5},{2,6},{3,7},{4,8},{5,9},{6,10},{7,11},{8,12},{9,13},{1... | collective-permute-start | bytes 663560 | tf_op jit(solution)/shard_map/ppermute | solution.py:44
  (146 other events, 1237.5 us)

commit v4 on v3

--- a/solution.py
+++ b/solution.py
@@ -73,15 +73,36 @@
     return lax.dynamic_slice(jnp.concatenate([even, odd, edge]), (lead,), (221736,))
 
 
-def sum_all_small(part):
-    for route in (x_swap(), y_swap(), z_turn(2)):
-        part = part + send_dp(part, route)
-    part = part + send_dp(part, [(i, i ^ 4) for i in range(DP)])
+def sum_z_small(part):
+    part = part + send_dp(part, z_turn(2))
+    return part + send_dp(part, [(i, i ^ 4) for i in range(DP)])
+
+
+def sum_rest_small(part):
+    part = part + send_dp(part, x_swap())
+    part = part + send_dp(part, y_swap())
     return part + send_mod(part)
 
 
-def gather_phase(block):
-    stack = jnp.stack([block] + [send_dp(block, z_turn(step)) for step in (1, 2, 3)])
+def xy_swap():
+    return [(i, i ^ 3) for i in range(DP)]
+
+
+def sum_scalar(value, side, place):
+    slots = lax.broadcasted_iota(jnp.int32, (8, 128), 0) * 128
+    slots = slots + lax.broadcasted_iota(jnp.int32, (8, 128), 1)
+    own = jnp.where(slots == side * DP + place, value, 0.0)
+    for routes in ([z_turn(1), z_turn(2), z_turn(3)], [x_swap(), y_swap(), xy_swap()]):
+        got = [send_dp(own, route) for route in routes]
+        own = own + got[0] + got[1] + got[2]
+    return jnp.sum(own + send_mod(own))
+
+
+def gather_z(block):
+    return jnp.stack([block] + [send_dp(block, z_turn(step)) for step in (1, 2, 3)])
+
+
+def gather_phase(stack):
     left, right = stack[:, :, :HALF], stack[:, :, HALF:]
     left_x = send_dp(left, x_swap())
     right_y = send_dp(right, y_swap())
@@ -100,7 +121,7 @@
 
 
 def assemble_body(phase, spot, *refs):
-    pieces, out, sem = refs[:16], refs[16], refs[17]
+    pieces, out, sem = refs[:16], refs[-2], refs[-1]
     side, z, y, x = spot[0], spot[1], spot[2], spot[3]
     copies = []
     for index in range(16):
@@ -122,15 +143,15 @@
         copy.wait()
 
 
-def assemble(phase, spot, pieces):
+def assemble(phase, spot, pieces, after=()):
     return pl.pallas_call(
         functools.partial(assemble_body, phase),
         out_shape=jax.ShapeDtypeStruct((32, BLOCK, D), BF),
-        in_specs=[pl.BlockSpec(memory_space=pltpu.SMEM)] + [pl.BlockSpec(memory_space=pl.ANY)] * 16,
+        in_specs=[pl.BlockSpec(memory_space=pltpu.SMEM)] + [pl.BlockSpec(memory_space=pl.ANY)] * (16 + len(after)),
         out_specs=pl.BlockSpec(memory_space=pltpu.VMEM),
         scratch_shapes=[pltpu.SemaphoreType.DMA((64,))],
         name="assemble",
-    )(spot, *pieces).reshape(PHASE_ROWS, D)
+    )(spot, *pieces, *after).reshape(PHASE_ROWS, D)
 
 
 def scatter_body(phase, pieces, spot, *refs):
@@ -160,7 +181,7 @@
         copy.wait()
 
 
-def scatter(phase, spot, tables):
+def scatter(phase, spot, tables, after=()):
     starts = [0]
     for rows in (D, D, D, D, FF, FF):
         starts.append(starts[-1] + rows)
@@ -180,22 +201,59 @@
         functools.partial(scatter_body, phase, pieces),
         out_shape=(jax.ShapeDtypeStruct((2, 2, 2, 4, BLOCK, HALF), BF),) * 2,
         in_specs=[pl.BlockSpec(memory_space=pltpu.SMEM)]
-        + [pl.BlockSpec(memory_space=pltpu.VMEM)] * len(used),
+        + [pl.BlockSpec(memory_space=pltpu.VMEM)] * len(used)
+        + [pl.BlockSpec(memory_space=pl.ANY)] * len(after),
         out_specs=(pl.BlockSpec(memory_space=pl.ANY),) * 2,
         scratch_shapes=[pltpu.SemaphoreType.DMA((count,))],
         name="scatter",
-    )(spot, *[tables[index] for index in used])
+    )(spot, *[tables[index] for index in used], *after)
 
 
 def plus(left, right):
     return (left.astype(F32) + right.astype(F32)).astype(BF)
 
 
-def reduce_phase(mine, theirs):
-    left_out = send_dp(plus(mine[0, :, 1], theirs[0, :, 1]), x_swap())
-    right_out = send_dp(plus(mine[1, 1], theirs[1, 1]), y_swap())
-    left_in = plus(mine[0, :, 0], theirs[0, :, 0])
-    right_in = plus(mine[1, 0], theirs[1, 0])
+def outs_body(*refs):
+    left_mine, left_theirs, right_mine, right_theirs, left, right = refs[:4] + refs[-2:]
+    index = pl.program_id(0)
+
+    @pl.when(index < 2)
+    def _():
+        left[0] = plus(left_mine[0, 0, 0], left_theirs[0, 0, 0])
+
+    @pl.when(index >= 2)
+    def _():
+        right[0] = plus(right_mine[0, 0, 0], right_theirs[0, 0, 0])
+
+
+def reduce_outs(mine, theirs):
+    block = (1, 1, 1, 4, BLOCK, HALF)
+    left = pl.BlockSpec(block, lambda i: (0, jnp.minimum(i, 1), 1, 0, 0, 0))
+    right = pl.BlockSpec(block, lambda i: (1, 1, jnp.maximum(i - 2, 0), 0, 0, 0))
+    return pl.pallas_call(
+        outs_body,
+        grid=(4,),
+        out_shape=(jax.ShapeDtypeStruct((2, 4, BLOCK, HALF), BF),) * 2,
+        in_specs=[left, left, right, right],
+        out_specs=(
+            pl.BlockSpec((1, 4, BLOCK, HALF), lambda i: (jnp.minimum(i, 1), 0, 0, 0)),
+            pl.BlockSpec((1, 4, BLOCK, HALF), lambda i: (jnp.maximum(i - 2, 0), 0, 0, 0)),
+        ),
+        name="reduce_outs",
+    )(mine, theirs, mine, theirs)
+
+
+def reduce_sends(outs):
+    return send_dp(outs[0], x_swap()), send_dp(outs[1], y_swap())
+
+
+def reduce_ins(mine, theirs):
+    return plus(mine[0, :, 0], theirs[0, :, 0]), plus(mine[1, 0], theirs[1, 0])
+
+
+def reduce_phase(sent, ins):
+    left_out, right_out = sent
+    left_in, right_in = ins
     left_next = send_dp(plus(left_in[1], left_out[1]), y_swap())
     right_next = send_dp(plus(right_in[1], right_out[1]), x_swap())
     left = left_in[0].astype(F32) + left_out[0].astype(F32) + left_next.astype(F32)
@@ -296,10 +354,10 @@
 
 
 def attend_back_body(
-    counts, ids, table, logs, query, key_own, key_other, value_own, value_other, grad,
-    grad_query, grad_key_own, grad_value_own, grad_key_other, grad_value_other, terms,
+    base, counts, ids, table, logs, query, key_own, key_other, value_own, value_other, grad, *refs
 ):
-    pair = pl.program_id(0)
+    grad_query, grad_key_own, grad_value_own, grad_key_other, grad_value_other, terms = refs[-6:]
+    pair = pl.program_id(0) + base
     keys = [joint_keys(key_own, key_other, seq) for seq in range(2)]
     values = [joint_keys(value_own, value_other, seq) for seq in range(2)]
     masks = [key_mask(counts, seq) for seq in range(2)]
@@ -325,7 +383,7 @@
             to_query[seq] = to_query[seq] + dot_f32(grad_scores, half_only(keys[seq], part), NN)
             to_key[seq] = to_key[seq] + dot_f32(grad_scores, asked, TN)
         for c in range(KEYS // 128):
-            terms[c, pl.ds(head, PAD, stride=16), :] = both[:, c * 128 : (c + 1) * 128]
+            terms[c, pl.ds(head - 2 * base, PAD, stride=8), :] = both[:, c * 128 : (c + 1) * 128]
     for seq in range(2):
         rows = pl.ds(seq * PAD, PAD)
         grad_query[rows, :] = (to_query[seq] * 0.125).astype(BF)
@@ -335,20 +393,22 @@
         grad_value_other[rows, :] = to_value[seq][HALF_KEYS : HALF_KEYS + PAD].astype(BF)
 
 
-def attend_back(counts, ids, table, logs, query, keys, values, grad):
+def attend_back(base, counts, ids, table, logs, query, keys, values, grad, before=(), after=()):
     def rows_of(kind):
         return jax.ShapeDtypeStruct((2 * PAD, D), kind)
 
+    columns = pl.BlockSpec((2 * PAD, PAIR), lambda i: (0, i + base))
+    any_ref = pl.BlockSpec(memory_space=pl.ANY)
     return pl.pallas_call(
-        attend_back_body,
-        grid=(H // 2,),
+        functools.partial(attend_back_body, base),
+        grid=(H // 4,),
         out_shape=(
             rows_of(BF),
             rows_of(F32),
             rows_of(F32),
             rows_of(BF),
             rows_of(BF),
-            jax.ShapeDtypeStruct((KEYS // 128, PAD * 16, 128), F32),
+            jax.ShapeDtypeStruct((KEYS // 128, PAD * 8, 128), F32),
         ),
         in_specs=[
             pl.BlockSpec(memory_space=pltpu.SMEM),
@@ -356,16 +416,19 @@
             fixed((16, 128)),
             fixed((2 * PAD, 128)),
         ]
-        + [by_pair()] * 6,
-        out_specs=(by_pair(),) * 5 + (fixed((KEYS // 128, PAD * 16, 128)),),
+        + [columns] * 6
+        + [any_ref] * (len(before) + len(after)),
+        out_specs=(columns,) * 5 + (fixed((KEYS // 128, PAD * 8, 128)),),
+        input_output_aliases={10 + i: i for i in range(len(before))},
         name="attend_back",
-    )(counts, ids, table, logs, query, *keys, *values, grad)
+    )(counts, ids, table, logs, query, *keys, *values, grad, *before, *after)
 
 
 GROUP = 4
 
 
-def table_body(ids, terms, out):
+def table_body(ids, early, late, *refs):
+    out = refs[-1]
     bucket = lax.broadcasted_iota(jnp.int32, (NB + 1, KEYS), 0)
 
     def step(index, totals):
@@ -373,9 +436,13 @@
         for lane_group in range(GROUP):
             row = index * GROUP + lane_group
             hot = jnp.where(ids[pl.ds(row, 1), :] == bucket, 1.0, 0.0).astype(BF)
-            start = pl.multiple_of(row * 16, 16)
+            span = pl.ds(pl.multiple_of(row * 8, 8), 8)
             term = jnp.concatenate(
-                [terms[c, pl.ds(start, 16), :] for c in range(KEYS // 128)], axis=1
+                [
+                    jnp.concatenate([terms[c, span, :] for c in range(KEYS // 128)], axis=1)
+                    for terms in (early, late)
+                ],
+                axis=0,
             )
             high = term.astype(BF)
             low = (term - high.astype(F32)).astype(BF)
@@ -389,43 +456,46 @@
     out[...] = total
 
 
-def table_grad(ids, terms):
+def table_grad(ids, terms, after=()):
     whole = pl.BlockSpec(memory_space=pltpu.VMEM)
     both = pl.pallas_call(
         table_body,
         out_shape=jax.ShapeDtypeStruct((NB + 1, 32), F32),
-        in_specs=[whole, whole],
+        in_specs=[whole] * 3 + [pl.BlockSpec(memory_space=pl.ANY)] * len(after),
         out_specs=whole,
         name="table_grad",
-    )(ids, terms)
-    return both[:NB, :H] + both[:NB, 16 : 16 + H]
+    )(ids, *terms, *after)
+    both = both[:NB, :16] + both[:NB, 16:]
+    return jnp.concatenate([both[:, : H // 2], both[:, 8 : 8 + H // 2]], axis=1)
 
 
 CUT = PHASE_ROWS - 4 * D
 
 
-def spread_body(first, second, out, held):
-    for half, table in enumerate((first, second)):
-        start = 4 * D if half == 0 else 0
-        for c in range(D // 128):
-            lanes = pl.ds(c * 128, 128)
-            held[...] = table[pl.ds(start, CUT), lanes].astype(F32)
-            for part in range(4):
-                out[pl.ds(half * CUT // 4, CUT // 4), pl.ds(part * D + c * 128, 128)] = held[
-                    pl.ds(part, CUT // 4, stride=4), :
-                ].astype(BF)
-
-
-def spread(first, second):
+def spread_body(half, table, *refs):
+    out, held = refs[-2], refs[-1]
+    start = 4 * D if half == 0 else 0
+    for c in range(D // 128):
+        held[...] = table[pl.ds(start, CUT), pl.ds(c * 128, 128)].astype(F32)
+        for part in range(4):
+            out[:, pl.ds(part * D + c * 128, 128)] = held[
+                pl.ds(part, CUT // 4, stride=4), :
+            ].astype(BF)
+
+
+def spread(half, table, before=None):
     whole = pl.BlockSpec(memory_space=pltpu.VMEM)
+    extra = () if before is None else (before,)
     return pl.pallas_call(
-        spread_body,
+        functools.partial(spread_body, half),
+        grid=(1,),
         out_shape=jax.ShapeDtypeStruct((D, FF), BF),
-        in_specs=[whole, whole],
-        out_specs=whole,
+        in_specs=[whole] + [pl.BlockSpec(memory_space=pl.ANY)] * len(extra),
+        out_specs=pl.BlockSpec((CUT // 4, FF), lambda i: (half, 0)),
         scratch_shapes=[pltpu.VMEM((CUT, 128), F32)],
+        input_output_aliases={1: 0} if extra else {},
         name="spread",
-    )(first, second)
+    )(table, *extra)
 
 
 def inner_grad_body(share, left, right, out, turned, held):
@@ -508,17 +578,6 @@
         pieces.append(flat[offset : offset + extent].reshape(dims_pair))
         offset += extent
     return pieces
-
-
-def unpack_tables(first, second, vec):
-    square = [first[i * D : (i + 1) * D] for i in range(4)]
-    return square + [
-        spread(first, second),
-        second[CUT:],
-        vec[:10],
-        vec[10:22].reshape(3, FF),
-        vec[22].reshape(NB + 1, H),
-    ]
 
 
 def widen(values):
@@ -540,15 +599,18 @@
         is_last = jnp.logical_and(side == 1, place == DP - 1)
         vec = jnp.where(is_last, own_copy[-EDGE:], jnp.zeros((), BF))
         vec = jnp.pad(vec, (0, D)).reshape(24, D)
-        vec, first = lax.optimization_barrier((vec, first))
-        weights = unpack_tables(
-            assemble(0, spot, gather_phase(first)),
-            assemble(1, spot, gather_phase(second)),
-            sum_all_small(vec),
-        )
+        vec, first = lax.optimization_barrier((sum_z_small(vec), first))
+        second_stack = gather_z(second)
+        first_table = assemble(0, spot, gather_phase(gather_z(first)), (second_stack,))
+        second_pieces = gather_phase(second_stack)
+        vec = sum_rest_small(vec)
+        square = [first_table[i * D : (i + 1) * D] for i in range(4)]
+        vec_model, vec_inner = vec[:10], vec[10:22].reshape(3, FF)
+        head_table = vec[22].reshape(NB + 1, H)
     else:
         weights = unpack(lax.all_gather(own_copy, ("mod", "dp"), axis=0, tiled=True))
-    w_query, w_key, w_value, w_out, w_inner, w_outer, vec_model, vec_inner, head_table = weights
+        square, (w_inner, w_outer, vec_model, vec_inner, head_table) = weights[:4], weights[4:]
+    w_query, w_key, w_value, w_out = square
     model_vec = vec_model.astype(jnp.float32)
     inner_vec = vec_inner.astype(jnp.float32)
     head_vals = head_table.astype(jnp.float32)
@@ -575,6 +637,11 @@
     keys_both, values_both = (keys_own, keys_other), (values_own, values_other)
     attended, logs = attend(counts, ids, table, query, *keys_both, *values_both)
 
+    if fast:
+        w_inner = spread(0, first_table)
+        second_table = assemble(1, spot, second_pieces, (attended, w_inner))
+        w_inner = spread(1, second_table, w_inner)
+        w_outer = second_table[CUT:]
     scaled = attended * scale_row
     mixed = layer_norm(scaled, model_vec[4], model_vec[5])
     mixed_low = mixed.astype(BF)
@@ -624,20 +691,33 @@
     )
     grad_head_scale = jnp.sum(jnp.sum(grad_scaled * attended, axis=0).reshape(H, HD), axis=1)
     grad_attended = (grad_scaled * scale_row).astype(BF)
+    parts = (counts, ids, table, logs, query, keys_both, values_both, grad_attended)
     if fast:
-        late = scatter(1, spot, [None] * 4 + [grad_w_inner, grad_w_outer])
-        late, grad_attended = lax.optimization_barrier((late, grad_attended))
-        late = (late[0], send_mod(late[1]))
-    grad_query, key_kept, value_kept, key_sent, value_sent, terms = attend_back(
-        counts, ids, table, logs, query, keys_both, values_both, grad_attended
-    )
+        kept, lent = scatter(1, spot, [None] * 4 + [grad_w_inner, grad_w_outer])
+        early = attend_back(0, *parts, after=(kept,))
+        got = send_mod(lent)
+        late_outs, late_ins = reduce_outs(kept, got), reduce_ins(kept, got)
+        late = attend_back(H // 4, *parts, before=early[:5], after=late_outs)
+    else:
+        early = attend_back(0, *parts)
+        late = attend_back(H // 4, *parts, before=early[:5])
+    grad_query, key_kept, value_kept, key_sent, value_sent, late_terms = late
+    terms = (early[5], late_terms)
     back_keys, back_values = from_partner((key_sent, value_sent), "mod", 0)
     grad_key = (key_kept + back_keys.astype(F32)).astype(BF)
     grad_value = (value_kept + back_values.astype(F32)).astype(BF)
-    grad_table = table_grad(ids, terms)
     grad_w_query = weight_grad(normed_low, grad_query)
     grad_w_key = weight_grad(normed_low, grad_key)
     grad_w_value = weight_grad(normed_low, grad_value)
+    matrices = [grad_w_query, grad_w_key, grad_w_value, grad_w_out, grad_w_inner, grad_w_outer]
+    if fast:
+        late_sent = reduce_sends(late_outs)
+        kept, lent = scatter(0, spot, matrices, late_sent)
+        got = send_mod(lent)
+        first_outs = reduce_outs(kept, got)
+        grad_table = table_grad(ids, terms, (result_rows, *first_outs))
+    else:
+        grad_table = table_grad(ids, terms)
     grad_b_query = jnp.sum(grad_query.astype(F32), axis=0)
     grad_b_value = jnp.sum(grad_value.astype(F32), axis=0)
     grad_normed = (
@@ -669,15 +749,13 @@
         )
         * share
     )
-    matrices = [grad_w_query, grad_w_key, grad_w_value, grad_w_out, grad_w_inner, grad_w_outer]
     if fast:
-        second = reduce_phase(*late)
-        kept, lent = scatter(0, spot, matrices)
-        first = reduce_phase(kept, send_mod(lent))
-        vec_grad = sum_all_small(jnp.pad(vec_grad, ((0, 1), (0, 0))))
+        second = reduce_phase(late_sent, late_ins)
+        first = reduce_phase(reduce_sends(first_outs), reduce_ins(kept, got))
+        vec_grad = sum_rest_small(sum_z_small(jnp.pad(vec_grad, ((0, 1), (0, 0)))))
         square = jnp.sum(first * first) + jnp.sum(second * second)
         square = square + jnp.where(is_last, jnp.sum(vec_grad * vec_grad), 0.0)
-        square_sum = sum_all_small(jnp.full((8, 128), square))[0, 0]
+        square_sum = sum_scalar(square, side, place)
         grad_shard = unpack_shard(first, second, vec_grad, side, place)
     else:
         local_grad = jnp.concatenate([part.reshape(-1) for part in matrices + [vec_grad]])

time: 461 us -> 497 us (1.078)
  Pallas kernels: 96.3 us -> 108 us
  other arithmetic: 57.5 us -> 69.1 us
  local copies, waits for them, and re-layouts: 25.5 us -> 31 us
    pallas_call x2 -> x6, Pallas kernels: 31.9 us -> 44.1 us  [the longest x2 24 us: attend_back(): pl.pallas_call(functools.partial(attend_back_body, base), grid=(H // 4,),...]
    reduce_sum x1, other arithmetic: 5.59 us -> 17.6 us  [on_device(): grad_b_inner = jnp.sum(grad_inner_low.astype(F32), axis=0)]
    convert_element_type x9 -> x8, other arithmetic: 14.4 us -> 7.6 us  [plus(): return (left.astype(F32) + right.astype(F32)).astype(BF)]
    unnamed x215 -> x235, local copies, waits for them, and re-layouts: 11.8 us -> 10.6 us
    ppermute x44 -> x46, starting transfers between devices: 60.2 us -> 61.3 us  [send_dp(): return lax.ppermute(block, 'dp', route)]
    ppermute x44 -> x46, waiting for transfers between devices: 127 us -> 128 us  [send_dp(): return lax.ppermute(block, 'dp', route)]
  transfers between devices with their start and end apart: 73 -> 75, of which waited for: 24 -> 29; matrix products, arithmetic and copies ran while one was open for 17% -> 20% of each run, Pallas kernels for 10% -> 9%
where the time goes in v4:
time: 497 us; the launch traced here: 487 us
  waiting for transfers between devices  130 us (26%)
  Pallas kernels  108 us (22%)
  starting transfers between devices  72.7 us (15%)
  matrix products  70.1 us (14%)
  other arithmetic  69.1 us (14%)
  local copies, waits for them, and re-layouts  31 us (6%)
  between operations  6.64 us (1%)
    ppermute x46, waiting for transfers between devices, send_dp(): return lax.ppermute(block, 'dp', route)  128 us
    ppermute x46, starting transfers between devices, send_dp(): return lax.ppermute(block, 'dp', route)  61.3 us
    dot_general x6, matrix products, matmul(): return jnp.dot(left, right, preferred_element_type=jnp.float32)  33.9 us
    pallas_call x2, Pallas kernels, attend_back(): pl.pallas_call(functools.partial(attend_back_body, base), grid=(H // 4,),...  24 us
    dot_general x6, matrix products, matmul_nt(): lax.dot_general(left, right, (((1,), (1,)), ((), ())), preferred_element_...  21.1 us
    reduce_sum x1, other arithmetic, on_device(): grad_b_inner = jnp.sum(grad_inner_low.astype(F32), axis=0)  17.6 us
    dot_general x5, matrix products, matmul_tn(): lax.dot_general(left, right, (((0,), (0,)), ((), ())), preferred_element_...  15.1 us
    pallas_call x2, Pallas kernels, scatter(): pl.pallas_call(functools.partial(scatter_body, phase, pieces), out_shape=...  14.6 us
  transfers between devices with their start and end apart: 75, of which 29 were waited for; matrix products, arithmetic and copies ran while one was open for 20% of the time, Pallas kernels for 9%

profile of v4, /device:TPU:0, one launch (start us, length us, event | category | flops | bytes accessed | tf_op | source)
XLA Modules:
  0.0 487.0 jit_solution(16531713369094096574)
XLA Ops:
  2.7 4.1 collective-permute-start
  40.6 19.6 %collective-permute-done.8 = bf16[144,768]{1,0:T(8,128)(2,1)S(1)} collective-permute-done((bf16[144,768]{1,0:T(8,128)(2,1)}, bf16[144,768]{1,0:T(8,128)(2,1)S(1)}, u32[]{:S(2)}, u32[]{:S(2)}) %collective-permute-start.8) | collective-permute-done | bytes 221216 | tf_op jit(solution)/shard_map/ppermute | solution.py:44
  69.4 8.9 %collective-permute-done.24 = bf16[144,768]{1,0:T(8,128)(2,1)S(1)} collective-permute-done((bf16[144,768]{1,0:T(8,128)(2,1)}, bf16[144,768]{1,0:T(8,128)(2,1)S(1)}, u32[]{:S(2)}, u32[]{:S(2)}) %collective-permute-start.24) | collective-permute-done | bytes 221216 | tf_op jit(solution)/shard_map/ppermute | solution.py:44
  86.7 6.2 %collective-permute-done.12.refs_3_ = bf16[4,144,384]{2,1,0:T(8,128)(2,1)S(1)} collective-permute-done((bf16[4,144,384]{2,1,0:T(8,128)(2,1)S(1)}, bf16[4,144,384]{2,1,0:T(8,128)(2,1)S(1)}, u32[]{:S(2)}, u32[]{:S(2)}) %collective-permute-start.12) | collective-permute-done | bytes 442400 | tf_op jit(solution)/shard_map/ppermute | solution.py:44
  100.1 7.2 %assemble.2 = bf16[32,144,768]{2,1,0:T(8,128)(2,1)} custom-call(s32[4]{0:T(128)} %pad_add_fusion.2.spot, bf16[4,144,384]{2,1,0:T(8,128)(2,1)} %copy-done.34, bf16[4,144,384]{2,1,0:T(8,128)(2,1)} %copy-done.49, bf16[4,144,384]{2,1,0:T(8,128)(2,1)} %copy-done.50, bf16[4,144,384]{2,1,0:T(8,128)(2,1)} %copy-done.55, bf16[4,144,384]{2,1,0:T(8,128)(2,1)} %copy-done.33, ...), custom_call_target="tpu_custom_call" | custom-call | tf_op jit(solution)/shard_map/assemble/pallas_call | solution.py:147
  118.4 5.4 %spread.2.refs_17_.refs_0_ = bf16[768,3072]{1,0:T(8,128)(2,1)} custom-call(bf16[4608,768]{1,0:T(8,128)(2,1)} %bitcast.156), custom_call_target="tpu_custom_call" | custom-call | tf_op jit(solution)/shard_map/spread/pallas_call | solution.py:489
  127.1 13.4 %attend.1 = (f32[416,768]{1,0:T(8,128)}, f32[416,128]{1,0:T(8,128)}) custom-call(s32[4]{0:T(128)} %pad_add_fusion.1.counts, s32[208,512]{1,0:T(8,128)} %pad_add_fusion.ids, f32[16,128]{1,0:T(8,128)} %pad.30.table, bf16[416,768]{1,0:T(8,128)(2,1)} %fusion.23.query, bf16[416,768]{1,0:T(8,128)(2,1)} %copy-done.14, ...), custom_call_target="tpu_custom_call" | custom-call | tf_op jit(solution)/shard_map/attend/pallas_call | solution.py:342
  147.8 7.6 %collective-permute-done.31.refs_3_ = bf16[4,144,384]{2,1,0:T(8,128)(2,1)S(1)} collective-permute-done((bf16[4,144,384]{2,1,0:T(8,128)(2,1)}, bf16[4,144,384]{2,1,0:T(8,128)(2,1)S(1)}, u32[]{:S(2)}, u32[]{:S(2)}) %collective-permute-start.31) | collective-permute-done | bytes 442400 | tf_op jit(solution)/shard_map/ppermute | solution.py:44
  160.0 7.3 %assemble.3 = bf16[32,144,768]{2,1,0:T(8,128)(2,1)} custom-call(s32[4]{0:T(128)} %pad_add_fusion.2.spot, bf16[4,144,384]{2,1,0:T(8,128)(2,1)} %get-tuple-element.151.refs_0_, bf16[4,144,384]{2,1,0:T(8,128)(2,1)} %collective-permute-done.29.refs_1_, bf16[4,144,384]{2,1,0:T(8,128)(2,1)} %collective-permute-done.30.refs_2_, bf16[4,144,384]{2,1,0:T(8,128)(2,1)} %copy-done.58, ...), custom_call_target="tpu_custom_call" | custom-call | tf_op jit(solution)/shard_map/assemble/pallas_call | solution.py:147
  167.3 5.4 %spread.3 = bf16[768,3072]{1,0:T(8,128)(2,1)} custom-call(bf16[4608,768]{1,0:T(8,128)(2,1)} %bitcast.165, bf16[768,3072]{1,0:T(8,128)(2,1)} %spread.2.refs_17_.refs_0_), custom_call_target="tpu_custom_call", output_to_operand_aliasing={{}: (1, {})} | custom-call | tf_op jit(solution)/shard_map/spread/pallas_call | solution.py:489
  173.0 17.2 %fusion.81 = (f32[416]{0:T(512)S(1)}, f32[416,3072]{1,0:T(8,128)S(1)}, f32[416,3072]{1,0:T(8,128)S(1)}, f32[416,3072]{1,0:T(8,128)S(1)}) fusion(f32[3072]{0:T(1024)S(1)} %add.417, bf16[416,768]{1,0:T(8,128)(2,1)S(1)} %add_convert_fusion.8.left, bf16[768,3072]{1,0:T(8,128)(2,1)} %spread.3), kind=kOutput, calls=%fused_computation.228 | convolution fusion | flops 2047278720 | bytes 20706944 | tf_op jit(solution)/shard_map/dot_general | solution.py:553
  190.3 4.3 multiply_reduce_fusion.1
  197.7 17.6 %convert_reduce_fusion = (f32[3072]{0:T(1024)}, bf16[416,3072]{1,0:T(8,128)(2,1)}) fusion(f32[416,3072]{1,0:T(8,128)S(1)} %get-tuple-element.141, f32[416]{0:T(512)S(1)} %negate_multiply_fusion.4, f32[416]{0:T(512)S(1)} %get-tuple-element.170, f32[416,3072]{1,0:T(8,128)S(1)} %get-tuple-element.140, f32[416]{0:T(512)S(1)} %broadcast_multiply_fusion.3, ...), kind=kLoop, calls=%fused_computation.5 | loop fusion | flops 30667776 | bytes 23046656 | tf_op jit(solution)/shard_map/reduce_sum | solution.py:679
  215.3 7.0 %inner_grad.1.refs_0_.refs_4_ = bf16[3072,768]{1,0:T(8,128)(2,1)} custom-call(bf16[416,768]{1,0:T(8,128)(2,1)} %copy-done.31, bf16[416,3072]{1,0:T(8,128)(2,1)} %get-tuple-element.130.right), custom_call_target="tpu_custom_call" | custom-call | tf_op jit(solution)/shard_map/inner_grad/pallas_call | solution.py:520
  222.3 7.5 %multiply_convert_fusion.refs_1_ = bf16[3072,768]{1,0:T(8,128)(2,1)} fusion(bf16[416,768]{1,0:T(8,128)(2,1)S(1)} %copy-done.41, f32[416,3072]{1,0:T(8,128)} %copy-done.5, f32[3072]{0:T(1024)S(1)} %add.421, f32[3072]{0:T(1024)S(1)} %mul.436, f32[416]{0:T(512)S(1)} %get-tuple-element.171, f32[416]{0:T(512)S(1)} %broadcast_multiply_fusion.3), kind=kOutput, calls=%fused_computation | convolution fusion | flops 1974042624 | bytes 10497280 | tf_op jit(solution)/shard_map/dot_general | solution.py:557
  229.7 7.3 %scatter.2 = (bf16[2,2,2,4,144,384]{5,4,3,2,1,0:T(8,128)(2,1)}, bf16[2,2,2,4,144,384]{5,4,3,2,1,0:T(8,128)(2,1)}) custom-call(s32[4]{0:T(128)} %pad_add_fusion.2.spot, bf16[3072,768]{1,0:T(8,128)(2,1)} %inner_grad.1.refs_0_.refs_4_, bf16[3072,768]{1,0:T(8,128)(2,1)} %multiply_convert_fusion.refs_1_), custom_call_target="tpu_custom_call" | custom-call | tf_op jit(solution)/shard_map/scatter/pallas_call | solution.py:200
  237.4 6.2 %multiply_reduce_fusion.4 = (f32[768]{0:T(1024)}, f32[416]{0:T(512)S(1)}, f32[768]{0:T(1024)}, f32[416,768]{1,0:T(8,128)S(1)}) fusion(f32[416,768]{1,0:T(8,128)S(1)} %get-tuple-element.175, f32[416]{0:T(512)S(1)} %fusion.70, f32[416]{0:T(512)S(1)} %broadcast_multiply_fusion.4, f32[768]{0:T(1024)S(1)} %get-tuple-element.110, ...), kind=kOutput, calls=%fused_computation.65 | convolution fusion | flops 1965488256 | bytes 9844608 | tf_op jit(solution)/shard_map/dot_general | solution.py:563
  251.2 11.9 %attend_back.2 = (bf16[416,768]{1,0:T(8,128)(2,1)}, f32[416,768]{1,0:T(8,128)}, f32[416,768]{1,0:T(8,128)}, bf16[416,768]{1,0:T(8,128)(2,1)}, bf16[416,768]{1,0:T(8,128)(2,1)}, /*index=5*/f32[4,1664,128]{2,1,0:T(8,128)}) custom-call(s32[4]{0:T(128)} %pad_add_fusion.1.counts, s32[208,512]{1,0:T(8,128)} %pad_add_fusion.ids, f32[16,128]{1,0:T(8,128)} %pad.30.table, ...), custom_call_target="tpu_custom_call" | custom-call | tf_op jit(solution)/shard_map/attend_back/pallas_call | solution.py:402
  263.1 4.6 reduce_outs.2
  267.8 12.1 %attend_back.3 = (bf16[416,768]{1,0:T(8,128)(2,1)}, f32[416,768]{1,0:T(8,128)}, f32[416,768]{1,0:T(8,128)}, bf16[416,768]{1,0:T(8,128)(2,1)}, bf16[416,768]{1,0:T(8,128)(2,1)}, /*index=5*/f32[4,1664,128]{2,1,0:T(8,128)}) custom-call(s32[4]{0:T(128)} %pad_add_fusion.1.counts, ...), custom_call_target="tpu_custom_call", output_to_operand_aliasing={{0}: (10, {}), {1}: (11, {}), {2}: (12, {}), {3}: (13, {}),... | custom-call | tf_op jit(solution)/shard_map/attend_back/pallas_call | solution.py:402
  291.9 13.3 %collective-permute-done.47.refs_6_ = bf16[2,4,144,384]{3,2,1,0:T(8,128)(2,1)S(1)} collective-permute-done((bf16[2,4,144,384]{3,2,1,0:T(8,128)(2,1)S(1)}, bf16[2,4,144,384]{3,2,1,0:T(8,128)(2,1)S(1)}, u32[]{:S(2)}, u32[]{:S(2)}) %collective-permute-start.47) | collective-permute-done | bytes 884768 | tf_op jit(solution)/shard_map/ppermute | solution.py:44
  307.1 7.3 %scatter.3 = (bf16[2,2,2,4,144,384]{5,4,3,2,1,0:T(8,128)(2,1)}, bf16[2,2,2,4,144,384]{5,4,3,2,1,0:T(8,128)(2,1)}) custom-call(s32[4]{0:T(128)} %pad_add_fusion.2.spot, bf16[768,768]{1,0:T(8,128)(2,1)} %multiply_convert_fusion.4.refs_0_, bf16[768,768]{1,0:T(8,128)(2,1)} %multiply_convert_fusion.3.refs_1_, bf16[768,768]{1,0:T(8,128)(2,1)} %multiply_convert_fusion.2.refs_2_, ...), custom_call_target="tpu_custom_call" | custom-call | tf_op jit(solution)/shard_map/scatter/pallas_call | solution.py:200
  314.4 6.7 %fusion.20 = bf16[416,768]{1,0:T(8,128)(2,1)S(1)} fusion(f32[416,768]{1,0:T(8,128)} %copy-done.10, bf16[4608,768]{1,0:T(8,128)(2,1)} %bitcast.166, f32[768]{0:T(1024)} %get-tuple-element.111, f32[416,3072]{1,0:T(8,128)} %copy-done.5, f32[3072]{0:T(1024)} %copy-done.94, f32[3072]{0:T(1024)S(1)} %mul.436, f32[416]{0:T(512)} %copy-done.89, f32[416]{0:T(512)} %copy-done.88), kind=kOutput, calls=%fused_computation.56 | convolution fusion | flops 1970282496 | bytes 11780096 | tf_op jit(solution)/shard_map/dot_general | solution.py:553
  344.9 9.9 %collective-permute-done.57 = bf16[4,144,384]{2,1,0:T(8,128)(2,1)S(1)} collective-permute-done((bf16[4,144,384]{2,1,0:T(8,128)(2,1)S(1)}, bf16[4,144,384]{2,1,0:T(8,128)(2,1)S(1)}, u32[]{:S(2)}, u32[]{:S(2)}) %collective-permute-start.57) | collective-permute-done | bytes 442400 | tf_op jit(solution)/shard_map/ppermute | solution.py:44
  355.7 4.6 reduce_outs.3
  361.5 14.4 %table_grad.1 = f32[64,32]{1,0:T(8,128)} custom-call(s32[208,512]{1,0:T(8,128)} %pad_add_fusion.ids, f32[4,1664,128]{2,1,0:T(8,128)} %get-tuple-element.54.early, f32[4,1664,128]{2,1,0:T(8,128)} %get-tuple-element.55.late, bf16[1,2,196,768]{3,2,1,0:T(8,128)(2,1)} %copy-done.17, bf16[2,4,144,384]{3,2,1,0:T(8,128)(2,1)} %get-tuple-element.52.refs_1_, ...), custom_call_target="tpu_custom_call" | custom-call | tf_op jit(solution)/shard_map/table_grad/pallas_call | solution.py:461
  377.9 6.7 %collective-permute-start.61 = (f32[24,768]{1,0:T(8,128)S(1)}, f32[24,768]{1,0:T(8,128)S(1)}, u32[]{:S(2)}, u32[]{:S(2)}) collective-permute-start(f32[24,768]{1,0:T(8,128)S(1)} %pad.32), channel_id=1, source_target_pairs={{0,8},{1,9},{2,10},{3,11},{4,12},{5,13},{6,14},{7,15},{8,0},{9,1},... | collective-permute-start | bytes 221192 | tf_op jit(solution)/shard_map/ppermute | solution.py:44
  394.4 12.3 %collective-permute-done.63 = f32[24,768]{1,0:T(8,128)S(1)} collective-permute-done((f32[24,768]{1,0:T(8,128)S(1)}, f32[24,768]{1,0:T(8,128)S(1)}, u32[]{:S(2)}, u32[]{:S(2)}) %collective-permute-start.63) | collective-permute-done | bytes 73760 | tf_op jit(solution)/shard_map/ppermute | solution.py:44
  414.8 4.1 collective-permute-done.52
  422.4 5.6 %collective-permute-start.54 = (bf16[144,768]{1,0:T(8,128)(2,1)}, bf16[144,768]{1,0:T(8,128)(2,1)}, u32[]{:S(2)}, u32[]{:S(2)}) collective-permute-start(bf16[144,768]{1,0:T(8,128)(2,1)} %get-tuple-element.146), channel_id=1, source_target_pairs={{0,8},{1,9},{2,10},{3,11},{4,12},{5,13},{6,14},{7,15},{8,0},{9,1},... | collective-permute-start | bytes 663560 | tf_op jit(solution)/shard_map/ppermute | solution.py:44
  431.0 11.7 %collective-permute-done.59 = bf16[144,768]{1,0:T(8,128)(2,1)S(1)} collective-permute-done((bf16[144,768]{1,0:T(8,128)(2,1)}, bf16[144,768]{1,0:T(8,128)(2,1)S(1)}, u32[]{:S(2)}, u32[]{:S(2)}) %collective-permute-start.59) | collective-permute-done | bytes 221216 | tf_op jit(solution)/shard_map/ppermute | solution.py:44
  442.7 6.5 %collective-permute-done.54 = bf16[144,768]{1,0:T(8,128)(2,1)} collective-permute-done((bf16[144,768]{1,0:T(8,128)(2,1)}, bf16[144,768]{1,0:T(8,128)(2,1)}, u32[]{:S(2)}, u32[]{:S(2)}) %collective-permute-start.54) | collective-permute-done | bytes 221216 | tf_op jit(solution)/shard_map/ppermute | solution.py:44
  (527 shorter events, 196.4 us)
Async XLA Ops:
  33.1 27.1 %collective-permute-start.8 = (bf16[144,768]{1,0:T(8,128)(2,1)}, bf16[144,768]{1,0:T(8,128)(2,1)S(1)}, u32[]{:S(2)}, u32[]{:S(2)}) collective-permute-start(bf16[144,768]{1,0:T(8,128)(2,1)} %select_n.120), channel_id=1, source_target_pairs={{0,8},{1,9},{2,10},{3,11},{4,12},{5,13},{6,14},{7,15},{8,0},{9,1},... | collective-permute-start | bytes 663560 | tf_op jit(solution)/shard_map/ppermute | solution.py:44
  34.8 25.4 %collective-permute-start.7 = (bf16[144,768]{1,0:T(8,128)(2,1)}, bf16[144,768]{1,0:T(8,128)(2,1)S(1)}, u32[]{:S(2)}, u32[]{:S(2)}) collective-permute-start(bf16[144,768]{1,0:T(8,128)(2,1)} %select_n.120), channel_id=1, source_target_pairs={{0,4},{1,5},{2,6},{3,7},{4,8},{5,9},{6,10},{7,11},{8,12},{9,13},{1... | collective-permute-start | bytes 663560 | tf_op jit(solution)/shard_map/ppermute | solution.py:44
  35.9 29.1 %collective-permute-start.26 = (bf16[144,768]{1,0:T(8,128)(2,1)}, bf16[144,768]{1,0:T(8,128)(2,1)S(1)}, u32[]{:S(2)}, u32[]{:S(2)}) collective-permute-start(bf16[144,768]{1,0:T(8,128)(2,1)} %select_n.127), channel_id=1, source_target_pairs={{0,12},{1,13},{2,14},{3,15},{4,0},{5,1},{6,2},{7,3},{8,4},{9,5},{1... | collective-permute-start | bytes 663560 | tf_op jit(solution)/shard_map/ppermute | solution.py:44
  39.8 29.5 %collective-permute-start.25 = (bf16[144,768]{1,0:T(8,128)(2,1)}, bf16[144,768]{1,0:T(8,128)(2,1)S(1)}, u32[]{:S(2)}, u32[]{:S(2)}) collective-permute-start(bf16[144,768]{1,0:T(8,128)(2,1)} %select_n.127), channel_id=1, source_target_pairs={{0,8},{1,9},{2,10},{3,11},{4,12},{5,13},{6,14},{7,15},{8,0},{9,1},... | collective-permute-start | bytes 663560 | tf_op jit(solution)/shard_map/ppermute | solution.py:44
  61.4 16.8 %collective-permute-start.10 = (bf16[4,144,384]{2,1,0:T(8,128)(2,1)S(1)}, bf16[4,144,384]{2,1,0:T(8,128)(2,1)S(1)}, u32[]{:S(2)}, u32[]{:S(2)}) collective-permute-start(bf16[4,144,384]{2,1,0:T(8,128)(2,1)S(1)} %get-tuple-element.153.refs_0_), channel_id=1, source_target_pairs={{0,1},{1,0},{2,3},{3,2},{4,5},{5,4},{6,7},{7,6},{8,9},{9,8},{10,11... | collective-permute-start | bytes 1327112 | tf_op jit(solution)/shard_map/ppermute | solution.py:44
  63.0 15.8 %collective-permute-start.11 = (bf16[4,144,384]{2,1,0:T(8,128)(2,1)S(1)}, bf16[4,144,384]{2,1,0:T(8,128)(2,1)S(1)}, u32[]{:S(2)}, u32[]{:S(2)}) collective-permute-start(bf16[4,144,384]{2,1,0:T(8,128)(2,1)S(1)} %get-tuple-element.153.refs_0_), channel_id=1, source_target_pairs={{0,2},{1,3},{2,0},{3,1},{4,6},{5,7},{6,4},{7,5},{8,10},{9,11},{10,... | collective-permute-start | bytes 1327112 | tf_op jit(solution)/shard_map/ppermute | solution.py:44
  63.1 19.1 %collective-permute-start.13 = (bf16[4,144,384]{2,1,0:T(8,128)(2,1)S(1)}, bf16[4,144,384]{2,1,0:T(8,128)(2,1)S(1)}, u32[]{:S(2)}, u32[]{:S(2)}) collective-permute-start(bf16[4,144,384]{2,1,0:T(8,128)(2,1)S(1)} %get-tuple-element.152.refs_4_), channel_id=1, source_target_pairs={{0,1},{1,0},{2,3},{3,2},{4,5},{5,4},{6,7},{7,6},{8,9},{9,8},{10,11... | collective-permute-start | bytes 1327112 | tf_op jit(solution)/shard_map/ppermute | solution.py:44
  65.1 20.4 %collective-permute-start.14 = (bf16[4,144,384]{2,1,0:T(8,128)(2,1)S(1)}, bf16[4,144,384]{2,1,0:T(8,128)(2,1)S(1)}, u32[]{:S(2)}, u32[]{:S(2)}) collective-permute-start(bf16[4,144,384]{2,1,0:T(8,128)(2,1)S(1)} %get-tuple-element.152.refs_4_), channel_id=1, source_target_pairs={{0,2},{1,3},{2,0},{3,1},{4,6},{5,7},{6,4},{7,5},{8,10},{9,11},{10,... | collective-permute-start | bytes 1327112 | tf_op jit(solution)/shard_map/ppermute | solution.py:44
  78.8 14.2 %collective-permute-start.12 = (bf16[4,144,384]{2,1,0:T(8,128)(2,1)S(1)}, bf16[4,144,384]{2,1,0:T(8,128)(2,1)S(1)}, u32[]{:S(2)}, u32[]{:S(2)}) collective-permute-start(bf16[4,144,384]{2,1,0:T(8,128)(2,1)S(1)} %collective-permute-done.10.refs_1_), channel_id=1, source_target_pairs={{0,2},{1,3},{2,0},{3,1},{4,6},{5,7},{6,4},{7,5},{8,10},{9,11},{10,... | collective-permute-start | bytes 1327112 | tf_op jit(solution)/shard_map/ppermute | solution.py:44
  82.2 12.6 %collective-permute-start.17 = (bf16[4,144,384]{2,1,0:T(8,128)(2,1)S(1)}, bf16[4,144,384]{2,1,0:T(8,128)(2,1)S(1)}, u32[]{:S(2)}, u32[]{:S(2)}) collective-permute-start(bf16[4,144,384]{2,1,0:T(8,128)(2,1)S(1)} %collective-permute-done.10.refs_1_), channel_id=1, source_target_pairs={{0,16},{16,0},{1,17},{17,1},{2,18},{18,2},{3,19},{19,3},{4,20},{20... | collective-permute-start | bytes 1327112 | tf_op jit(solution)/shard_map/ppermute | solution.py:48
  109.3 17.2 %collective-permute-start.27 = (bf16[416,768]{1,0:T(8,128)(2,1)S(1)}, bf16[416,768]{1,0:T(8,128)(2,1)}, u32[]{:S(2)}, u32[]{:S(2)}) collective-permute-start(bf16[416,768]{1,0:T(8,128)(2,1)S(1)} %convolution_convert_fusion.key_own), channel_id=1, source_target_pairs={{0,16},{16,0},{1,17},{17,1},{2,18},{18,2},{3,19},{19,3},{4,20},{20... | collective-permute-start | bytes 1916936 | tf_op jit(solution)/shard_map/ppermute | solution.py:538
  112.4 14.7 %collective-permute-start.28 = (bf16[416,768]{1,0:T(8,128)(2,1)}, bf16[416,768]{1,0:T(8,128)(2,1)}, u32[]{:S(2)}, u32[]{:S(2)}) collective-permute-start(bf16[416,768]{1,0:T(8,128)(2,1)} %fusion.24.value_own), channel_id=1, source_target_pairs={{0,16},{16,0},{1,17},{17,1},{2,18},{18,2},{3,19},{19,3},{4,20},{20... | collective-permute-start | bytes 1916936 | tf_op jit(solution)/shard_map/ppermute | solution.py:538
  114.8 27.7 %collective-permute-start.29 = (bf16[4,144,384]{2,1,0:T(8,128)(2,1)}, bf16[4,144,384]{2,1,0:T(8,128)(2,1)}, u32[]{:S(2)}, u32[]{:S(2)}) collective-permute-start(bf16[4,144,384]{2,1,0:T(8,128)(2,1)} %get-tuple-element.151.refs_0_), channel_id=1, source_target_pairs={{0,1},{1,0},{2,3},{3,2},{4,5},{5,4},{6,7},{7,6},{8,9},{9,8},{10,11... | collective-permute-start | bytes 1327112 | tf_op jit(solution)/shard_map/ppermute | solution.py:44
  116.3 26.8 %collective-permute-start.30 = (bf16[4,144,384]{2,1,0:T(8,128)(2,1)}, bf16[4,144,384]{2,1,0:T(8,128)(2,1)}, u32[]{:S(2)}, u32[]{:S(2)}) collective-permute-start(bf16[4,144,384]{2,1,0:T(8,128)(2,1)} %get-tuple-element.151.refs_0_), channel_id=1, source_target_pairs={{0,2},{1,3},{2,0},{3,1},{4,6},{5,7},{6,4},{7,5},{8,10},{9,11},{10,... | collective-permute-start | bytes 1327112 | tf_op jit(solution)/shard_map/ppermute | solution.py:44
  116.6 28.0 %collective-permute-start.32 = (bf16[4,144,384]{2,1,0:T(8,128)(2,1)}, bf16[4,144,384]{2,1,0:T(8,128)(2,1)}, u32[]{:S(2)}, u32[]{:S(2)}) collective-permute-start(bf16[4,144,384]{2,1,0:T(8,128)(2,1)} %get-tuple-element.150.refs_4_), channel_id=1, source_target_pairs={{0,1},{1,0},{2,3},{3,2},{4,5},{5,4},{6,7},{7,6},{8,9},{9,8},{10,11... | collective-permute-start | bytes 1327112 | tf_op jit(solution)/shard_map/ppermute | solution.py:44
  126.6 18.0 %collective-permute-start.33 = (bf16[4,144,384]{2,1,0:T(8,128)(2,1)}, bf16[4,144,384]{2,1,0:T(8,128)(2,1)}, u32[]{:S(2)}, u32[]{:S(2)}) collective-permute-start(bf16[4,144,384]{2,1,0:T(8,128)(2,1)} %get-tuple-element.150.refs_4_), channel_id=1, source_target_pairs={{0,2},{1,3},{2,0},{3,1},{4,6},{5,7},{6,4},{7,5},{8,10},{9,11},{10,... | collective-permute-start | bytes 1327112 | tf_op jit(solution)/shard_map/ppermute | solution.py:44
  127.1 20.1 %collective-permute-start.35 = (bf16[4,144,384]{2,1,0:T(8,128)(2,1)}, bf16[4,144,384]{2,1,0:T(8,128)(2,1)}, u32[]{:S(2)}, u32[]{:S(2)}) collective-permute-start(bf16[4,144,384]{2,1,0:T(8,128)(2,1)} %get-tuple-element.151.refs_0_), channel_id=1, source_target_pairs={{0,16},{16,0},{1,17},{17,1},{2,18},{18,2},{3,19},{19,3},{4,20},{20... | collective-permute-start | bytes 1327112 | tf_op jit(solution)/shard_map/ppermute | solution.py:48
  144.6 12.8 %collective-permute-start.36 = (bf16[4,144,384]{2,1,0:T(8,128)(2,1)}, bf16[4,144,384]{2,1,0:T(8,128)(2,1)S(1)}, u32[]{:S(2)}, u32[]{:S(2)}) collective-permute-start(bf16[4,144,384]{2,1,0:T(8,128)(2,1)} %collective-permute-done.29.refs_1_), channel_id=1, source_target_pairs={{0,16},{16,0},{1,17},{17,1},{2,18},{18,2},{3,19},{19,3},{4,20},{20... | collective-permute-start | bytes 1327112 | tf_op jit(solution)/shard_map/ppermute | solution.py:48
  144.6 12.8 %collective-permute-start.34 = (bf16[4,144,384]{2,1,0:T(8,128)(2,1)}, bf16[4,144,384]{2,1,0:T(8,128)(2,1)S(1)}, u32[]{:S(2)}, u32[]{:S(2)}) collective-permute-start(bf16[4,144,384]{2,1,0:T(8,128)(2,1)} %collective-permute-done.33.refs_6_), channel_id=1, source_target_pairs={{0,1},{1,0},{2,3},{3,2},{4,5},{5,4},{6,7},{7,6},{8,9},{9,8},{10,11... | collective-permute-start | bytes 1327112 | tf_op jit(solution)/shard_map/ppermute | solution.py:44
  237.0 26.1 %collective-permute-start.43 = (bf16[2,2,2,4,144,384]{5,4,3,2,1,0:T(8,128)(2,1)}, bf16[2,2,2,4,144,384]{5,4,3,2,1,0:T(8,128)(2,1)}, u32[]{:S(2)}, u32[]{:S(2)}) collective-permute-start(bf16[2,2,2,4,144,384]{5,4,3,2,1,0:T(8,128)(2,1)} %get-tuple-element.42), channel_id=1, source_target_pairs={{0,16},{16,0},{1,17},{17,1},{2,18},{18,2},{3,19},{19,3},{4,20},{20... | collective-permute-start | bytes 10616840 | tf_op jit(solution)/shard_map/ppermute | solution.py:48
  283.5 21.7 %collective-permute-start.47 = (bf16[2,4,144,384]{3,2,1,0:T(8,128)(2,1)S(1)}, bf16[2,4,144,384]{3,2,1,0:T(8,128)(2,1)S(1)}, u32[]{:S(2)}, u32[]{:S(2)}) collective-permute-start(bf16[2,4,144,384]{3,2,1,0:T(8,128)(2,1)S(1)} %copy-done.38), channel_id=1, source_target_pairs={{0,2},{1,3},{2,0},{3,1},{4,6},{5,7},{6,4},{7,5},{8,10},{9,11},{10,... | collective-permute-start | bytes 2654216 | tf_op jit(solution)/shard_map/ppermute | solution.py:44
  284.1 21.4 %collective-permute-start.46 = (bf16[2,4,144,384]{3,2,1,0:T(8,128)(2,1)S(1)}, bf16[2,4,144,384]{3,2,1,0:T(8,128)(2,1)S(1)}, u32[]{:S(2)}, u32[]{:S(2)}) collective-permute-start(bf16[2,4,144,384]{3,2,1,0:T(8,128)(2,1)S(1)} %copy-done.37), channel_id=1, source_target_pairs={{0,1},{1,0},{2,3},{3,2},{4,5},{5,4},{6,7},{7,6},{8,9},{9,8},{10,11... | collective-permute-start | bytes 2654216 | tf_op jit(solution)/shard_map/ppermute | solution.py:44
  314.4 41.3 %collective-permute-start.48 = (bf16[2,2,2,4,144,384]{5,4,3,2,1,0:T(8,128)(2,1)}, bf16[2,2,2,4,144,384]{5,4,3,2,1,0:T(8,128)(2,1)}, u32[]{:S(2)}, u32[]{:S(2)}) collective-permute-start(bf16[2,2,2,4,144,384]{5,4,3,2,1,0:T(8,128)(2,1)} %get-tuple-element.51), channel_id=1, source_target_pairs={{0,16},{16,0},{1,17},{17,1},{2,18},{18,2},{3,19},{19,3},{4,20},{20... | collective-permute-start | bytes 10616840 | tf_op jit(solution)/shard_map/ppermute | solution.py:48
  342.2 12.6 %collective-permute-start.57 = (bf16[4,144,384]{2,1,0:T(8,128)(2,1)S(1)}, bf16[4,144,384]{2,1,0:T(8,128)(2,1)S(1)}, u32[]{:S(2)}, u32[]{:S(2)}) collective-permute-start(bf16[4,144,384]{2,1,0:T(8,128)(2,1)S(1)} %fusion.56), channel_id=1, source_target_pairs={{0,1},{1,0},{2,3},{3,2},{4,5},{5,4},{6,7},{7,6},{8,9},{9,8},{10,11... | collective-permute-start | bytes 1327112 | tf_op jit(solution)/shard_map/ppermute | solution.py:44
  360.3 47.6 %collective-permute-start.51 = (bf16[2,4,144,384]{3,2,1,0:T(8,128)(2,1)}, bf16[2,4,144,384]{3,2,1,0:T(8,128)(2,1)}, u32[]{:S(2)}, u32[]{:S(2)}) collective-permute-start(bf16[2,4,144,384]{3,2,1,0:T(8,128)(2,1)} %get-tuple-element.53.refs_2_), channel_id=1, source_target_pairs={{0,2},{1,3},{2,0},{3,1},{4,6},{5,7},{6,4},{7,5},{8,10},{9,11},{10,... | collective-permute-start | bytes 2654216 | tf_op jit(solution)/shard_map/ppermute | solution.py:44
  384.7 25.0 %collective-permute-start.49 = (bf16[2,4,144,384]{3,2,1,0:T(8,128)(2,1)S(1)}, bf16[2,4,144,384]{3,2,1,0:T(8,128)(2,1)S(1)}, u32[]{:S(2)}, u32[]{:S(2)}) collective-permute-start(bf16[2,4,144,384]{3,2,1,0:T(8,128)(2,1)S(1)} %copy-done.39), channel_id=1, source_target_pairs={{0,1},{1,0},{2,3},{3,2},{4,5},{5,4},{6,7},{7,6},{8,9},{9,8},{10,11... | collective-permute-start | bytes 2654216 | tf_op jit(solution)/shard_map/ppermute | solution.py:44
  392.2 14.5 %collective-permute-start.63 = (f32[24,768]{1,0:T(8,128)S(1)}, f32[24,768]{1,0:T(8,128)S(1)}, u32[]{:S(2)}, u32[]{:S(2)}) collective-permute-start(f32[24,768]{1,0:T(8,128)S(1)} %add.465), channel_id=1, source_target_pairs={{0,1},{1,0},{2,3},{3,2},{4,5},{5,4},{6,7},{7,6},{8,9},{9,8},{10,11... | collective-permute-start | bytes 221192 | tf_op jit(solution)/shard_map/ppermute | solution.py:44
  412.1 30.6 %collective-permute-start.59 = (bf16[144,768]{1,0:T(8,128)(2,1)}, bf16[144,768]{1,0:T(8,128)(2,1)S(1)}, u32[]{:S(2)}, u32[]{:S(2)}) collective-permute-start(bf16[144,768]{1,0:T(8,128)(2,1)} %get-tuple-element.149), channel_id=1, source_target_pairs={{0,8},{1,9},{2,10},{3,11},{4,12},{5,13},{6,14},{7,15},{8,0},{9,1},... | collective-permute-start | bytes 663560 | tf_op jit(solution)/shard_map/ppermute | solution.py:44
  412.7 30.0 %collective-permute-start.58 = (bf16[144,768]{1,0:T(8,128)(2,1)}, bf16[144,768]{1,0:T(8,128)(2,1)}, u32[]{:S(2)}, u32[]{:S(2)}) collective-permute-start(bf16[144,768]{1,0:T(8,128)(2,1)} %get-tuple-element.147), channel_id=1, source_target_pairs={{0,4},{1,5},{2,6},{3,7},{4,8},{5,9},{6,10},{7,11},{8,12},{9,13},{1... | collective-permute-start | bytes 663560 | tf_op jit(solution)/shard_map/ppermute | solution.py:44
  421.9 20.8 %collective-permute-start.55 = (bf16[144,768]{1,0:T(8,128)(2,1)}, bf16[144,768]{1,0:T(8,128)(2,1)}, u32[]{:S(2)}, u32[]{:S(2)}) collective-permute-start(bf16[144,768]{1,0:T(8,128)(2,1)} %get-tuple-element.145), channel_id=1, source_target_pairs={{0,12},{1,13},{2,14},{3,15},{4,0},{5,1},{6,2},{7,3},{8,4},{9,5},{1... | collective-permute-start | bytes 663560 | tf_op jit(solution)/shard_map/ppermute | solution.py:44
  422.4 26.8 %collective-permute-start.54 = (bf16[144,768]{1,0:T(8,128)(2,1)}, bf16[144,768]{1,0:T(8,128)(2,1)}, u32[]{:S(2)}, u32[]{:S(2)}) collective-permute-start(bf16[144,768]{1,0:T(8,128)(2,1)} %get-tuple-element.146), channel_id=1, source_target_pairs={{0,8},{1,9},{2,10},{3,11},{4,12},{5,13},{6,14},{7,15},{8,0},{9,1},... | collective-permute-start | bytes 663560 | tf_op jit(solution)/shard_map/ppermute | solution.py:44
  428.0 21.2 %collective-permute-start.53 = (bf16[144,768]{1,0:T(8,128)(2,1)}, bf16[144,768]{1,0:T(8,128)(2,1)}, u32[]{:S(2)}, u32[]{:S(2)}) collective-permute-start(bf16[144,768]{1,0:T(8,128)(2,1)} %get-tuple-element.144), channel_id=1, source_target_pairs={{0,4},{1,5},{2,6},{3,7},{4,8},{5,9},{6,10},{7,11},{8,12},{9,13},{1... | collective-permute-start | bytes 663560 | tf_op jit(solution)/shard_map/ppermute | solution.py:44
  (158 other events, 1821.4 us)
